TPU v7x, 128 devices: a whole 4x4x4 slice. The times are simulated.
128 devices in a mesh: seq: 32 (over z, y_lo, x), grp: 4 (over y_hi, core).
Axes of the slice: x: 4, y: 4 (y_hi: 2, y_lo: 2; y = y_hi * 2 + y_lo), z: 4, core: 2. Of those that a mesh axis runs over, the one named last changes fastest.
Arguments:
- queries: bfloat16 [32768, 4096], P(('grp', 'seq')), parts along dimension 0, may hold values from -6 to 6
- stored_keys: bfloat16 [32768, 2048], P(('grp', 'seq')), parts along dimension 0, may hold values from -6 to 6
- stored_values: bfloat16 [32768, 2048], P(('grp', 'seq')), parts along dimension 0, may hold values from -6 to 6
- stored_output: bfloat16 [32768, 4096], P(('grp', 'seq')), parts along dimension 0, may hold values from -6 to 6
- output_cotangent: bfloat16 [32768, 4096], P(('grp', 'seq')), parts along dimension 0, may hold values from -48 to 48
- score_logsumexp: float32 [32, 32768], P(None, ('grp', 'seq')), parts along dimension 1, may hold values from 6.5 to 7.5
- valid_count: int32 [4], P('grp'), parts along dimension 0, may hold values from 4096 to 8192
Outputs:
- query_gradient: float32 [32768, 4096], P(('grp', 'seq')), parts along dimension 0
- key_grad: float32 [32768, 2048], P(('grp', 'seq')), parts along dimension 0
- value_grad: float32 [32768, 2048], P(('grp', 'seq')), parts along dimension 0
There are 4 independent parts, one for each index of `grp`. A program takes and returns all parts, laid end to end along the dimension named above; each array names one. Nothing has to cross between parts.
All inputs are finite; a program needn't handle non-finite values.
Results may differ from a plain program's by a relative error of at most 0.0047.
Values may be sent and summed in bfloat16 or wider, within the bound.
A program may use at most 128 MiB of HBM per device.

v0:
```python
import functools

import jax
import jax.numpy as jnp
from jax import lax
from jax.experimental import pallas as pl
from jax.experimental.pallas import tpu as pltpu
from jax.sharding import PartitionSpec as P


QUERY_HEADS = 32
KEY_VALUE_HEADS = 16
HEAD_SIZE = 128
WINDOW = 1024
HEADS_PER_STEP = 4


score_scale = 168.0 ** (-0.5)


def passed_along(x, axis, by):
    count = lax.axis_size(axis)
    pairs = [(i, i + by) for i in range(count) if 0 <= i + by < count]
    return lax.ppermute(x, axis, pairs)


def pair_kernel(group, heads, accumulate, sc_ref, q_ref, do_ref, k_ref, v_ref, lse_ref, dl_ref, *rest):
    if accumulate:
        dq_in_ref, dq_ref, dk_ref, dv_ref = rest
    else:
        dq_ref, dk_ref, dv_ref = rest
    rows = q_ref.shape[0]
    cols = k_ref.shape[0]
    qs = sc_ref[0]
    ks = sc_ref[1]
    vc = sc_ref[2]
    i = lax.broadcasted_iota(jnp.int32, (rows, cols), 0) + qs
    j = lax.broadcasted_iota(jnp.int32, (rows, cols), 1) + ks
    live = (j <= i) & (i - j < WINDOW) & (j >= 0) & (i < vc) & (j < vc)
    nt = (((1,), (1,)), ((), ()))
    tn = (((0,), (0,)), ((), ()))
    for c in range(heads):
        ksl = slice(c * HEAD_SIZE, (c + 1) * HEAD_SIZE)
        k = k_ref[:, ksl]
        v = v_ref[:, ksl]
        dk = jnp.zeros((cols, HEAD_SIZE), jnp.float32)
        dv = jnp.zeros((cols, HEAD_SIZE), jnp.float32)
        for g in range(group):
            hq = c * group + g
            sl = slice(hq * HEAD_SIZE, (hq + 1) * HEAD_SIZE)
            q = q_ref[:, sl]
            do = do_ref[:, sl]
            lse = lse_ref[c, :, g : g + 1]
            dl = dl_ref[c, :, g : g + 1]
            s = lax.dot_general(q, k, nt, preferred_element_type=jnp.float32) * score_scale
            p = jnp.where(live, jnp.exp(s - lse), 0.0)
            dp = lax.dot_general(do, v, nt, preferred_element_type=jnp.float32)
            ds = (p * (dp - dl)).astype(jnp.bfloat16)
            pb = p.astype(jnp.bfloat16)
            dv = dv + lax.dot_general(pb, do, tn, preferred_element_type=jnp.float32)
            dk = dk + lax.dot_general(ds, q, tn, preferred_element_type=jnp.float32)
            dq = jnp.dot(ds, k, preferred_element_type=jnp.float32) * score_scale
            if accumulate:
                dq = dq + dq_in_ref[:, sl]
            dq_ref[:, sl] = dq
        dk_ref[:, ksl] = (dk * score_scale).astype(dk_ref.dtype)
        dv_ref[:, ksl] = dv.astype(dv_ref.dtype)


def pair_grads(scalars, q, do, k, v, lse3, dl3, dq_in, kv_dtype):
    rows = q.shape[0]
    cols = k.shape[0]
    group = QUERY_HEADS // KEY_VALUE_HEADS
    accumulate = dq_in is not None
    heads = HEADS_PER_STEP
    qspec = pl.BlockSpec((rows, heads * group * HEAD_SIZE), lambda h, sc: (0, h))
    kspec = pl.BlockSpec((cols, heads * HEAD_SIZE), lambda h, sc: (0, h))
    sspec = pl.BlockSpec((heads, rows, group), lambda h, sc: (h, 0, 0))
    in_specs = [qspec, qspec, kspec, kspec, sspec, sspec]
    args = [q, do, k, v, lse3, dl3]
    if accumulate:
        in_specs.append(qspec)
        args.append(dq_in)
    out_shape = (
        jax.ShapeDtypeStruct((rows, QUERY_HEADS * HEAD_SIZE), jnp.float32),
        jax.ShapeDtypeStruct((cols, KEY_VALUE_HEADS * HEAD_SIZE), kv_dtype),
        jax.ShapeDtypeStruct((cols, KEY_VALUE_HEADS * HEAD_SIZE), kv_dtype),
    )
    flops = 5 * 2 * rows * cols * HEAD_SIZE * QUERY_HEADS
    nbytes = 2 * (2 * q.size + 2 * k.size) + 4 * q.size * (2 if accumulate else 1) + 2 * 2 * k.size * jnp.dtype(kv_dtype).itemsize
    return pl.pallas_call(
        functools.partial(pair_kernel, group, heads, accumulate),
        out_shape=out_shape,
        grid_spec=pltpu.PrefetchScalarGridSpec(
            num_scalar_prefetch=1,
            grid=(KEY_VALUE_HEADS // heads,),
            in_specs=in_specs,
            out_specs=[qspec, kspec, kspec],
        ),
        input_output_aliases=({7: 0} if accumulate else {}),
        cost_estimate=pl.CostEstimate(
            flops=flops, transcendentals=rows * cols * QUERY_HEADS, bytes_accessed=int(nbytes)
        ),
    )(scalars, *args)


def local(
    queries,
    stored_keys,
    stored_values,
    stored_output,
    output_cotangent,
    score_logsumexp,
    valid_count,
):
    tokens_here = queries.shape[0]
    blocks = WINDOW // tokens_here
    group = QUERY_HEADS // KEY_VALUE_HEADS
    shard = lax.axis_index("seq")
    halos = []
    for distance in range(1, blocks + 1):
        halos.append(passed_along((stored_keys, stored_values), "seq", distance))
    limit = valid_count[0]

    delta = jnp.sum(
        (output_cotangent.astype(jnp.float32) * stored_output.astype(jnp.float32)).reshape(
            tokens_here, QUERY_HEADS, HEAD_SIZE
        ),
        -1,
    )
    dl3 = delta.reshape(tokens_here, KEY_VALUE_HEADS, group).transpose(1, 0, 2)
    lse3 = score_logsumexp.T.reshape(tokens_here, KEY_VALUE_HEADS, group).transpose(1, 0, 2)
    qstart = shard * tokens_here

    def scalars_for(distance):
        return jnp.stack([qstart, qstart - distance * tokens_here, limit]).astype(jnp.int32)

    dq, key_grad, value_grad = pair_grads(
        scalars_for(0), queries, output_cotangent, stored_keys, stored_values, lse3, dl3, None, jnp.float32
    )
    for distance in range(1, blocks + 1):
        k_far, v_far = halos[distance - 1]
        dq, dk_part, dv_part = pair_grads(
            scalars_for(distance),
            queries,
            output_cotangent,
            k_far,
            v_far,
            lse3,
            dl3,
            dq,
            jnp.bfloat16,
        )
        arrived = passed_along((dk_part, dv_part), "seq", -distance)
        key_grad = key_grad + arrived[0].astype(jnp.float32)
        value_grad = value_grad + arrived[1].astype(jnp.float32)
    return (dq, key_grad, value_grad)


def solution(mesh):
    placed = (
        P(("grp", "seq"), None),
        P(("grp", "seq"), None),
        P(("grp", "seq"), None),
        P(("grp", "seq"), None),
        P(("grp", "seq"), None),
        P(None, ("grp", "seq")),
        P("grp"),
    )

    return jax.shard_map(
        local,
        mesh=mesh,
        in_specs=placed,
        out_specs=(P(("grp", "seq"), None), P(("grp", "seq"), None), P(("grp", "seq"), None)),
        check_vma=False,
    )
```

profile of v0, /device:TPU:30, one launch (start us, length us, event | category | flops | bytes accessed | tf_op | source)
XLA Modules:
  0.0 373.4 jit_solution(13976660593458610545)
XLA Ops:
  0.6 3.9 %collective-permute-start.6 = (bf16[256,2048]{1,0:T(8,128)(2,1)}, bf16[256,2048]{1,0:T(8,128)(2,1)S(1)}, u32[]{:S(2)}, u32[]{:S(2)}) collective-permute-start(bf16[256,2048]{1,0:T(8,128)(2,1)} %k_ref.1), channel_id=1, source_target_pairs={{0,4},{4,8},{8,12},{12,16},{16,20},{20,24},{24,28},{28,32},{32,36}... | collective-permute-start | bytes 3145736 | tf_op jit(solution)/shard_map/ppermute | solution.py:24
  4.6 3.4 collective-permute-start.7
  8.0 4.0 %collective-permute-start.4 = (bf16[256,2048]{1,0:T(8,128)(2,1)}, bf16[256,2048]{1,0:T(8,128)(2,1)S(1)}, u32[]{:S(2)}, u32[]{:S(2)}) collective-permute-start(bf16[256,2048]{1,0:T(8,128)(2,1)} %k_ref.1), channel_id=1, source_target_pairs={{0,8},{4,12},{8,16},{12,20},{16,24},{20,28},{24,32},{28,36},{32,40... | collective-permute-start | bytes 3145736 | tf_op jit(solution)/shard_map/ppermute | solution.py:24
  12.0 4.0 %collective-permute-start.5 = (bf16[256,2048]{1,0:T(8,128)(2,1)}, bf16[256,2048]{1,0:T(8,128)(2,1)}, u32[]{:S(2)}, u32[]{:S(2)}) collective-permute-start(bf16[256,2048]{1,0:T(8,128)(2,1)} %v_ref.1), channel_id=1, source_target_pairs={{0,8},{4,12},{8,16},{12,20},{16,24},{20,28},{24,32},{28,36},{32,40... | collective-permute-start | bytes 3145736 | tf_op jit(solution)/shard_map/ppermute | solution.py:24
  16.1 4.0 %collective-permute-start.2 = (bf16[256,2048]{1,0:T(8,128)(2,1)}, bf16[256,2048]{1,0:T(8,128)(2,1)S(1)}, u32[]{:S(2)}, u32[]{:S(2)}) collective-permute-start(bf16[256,2048]{1,0:T(8,128)(2,1)} %k_ref.1), channel_id=1, source_target_pairs={{0,12},{4,16},{8,20},{12,24},{16,28},{20,32},{24,36},{28,40},{32,4... | collective-permute-start | bytes 3145736 | tf_op jit(solution)/shard_map/ppermute | solution.py:24
  20.7 2.9 multiply_bitcast_fusion
  23.6 0.6 add_add_fusion.4.sc_ref
  24.3 0.6 add_add_fusion.3.sc_ref
  24.9 3.9 %collective-permute-done.6.k_ref = bf16[256,2048]{1,0:T(8,128)(2,1)S(1)} collective-permute-done((bf16[256,2048]{1,0:T(8,128)(2,1)}, bf16[256,2048]{1,0:T(8,128)(2,1)S(1)}, u32[]{:S(2)}, u32[]{:S(2)}) %collective-permute-start.6) | collective-permute-done | bytes 1048608 | tf_op jit(solution)/shard_map/ppermute | solution.py:24
  28.8 4.3 %collective-permute-start.3 = (bf16[256,2048]{1,0:T(8,128)(2,1)}, bf16[256,2048]{1,0:T(8,128)(2,1)}, u32[]{:S(2)}, u32[]{:S(2)}) collective-permute-start(bf16[256,2048]{1,0:T(8,128)(2,1)} %v_ref.1), channel_id=1, source_target_pairs={{0,12},{4,16},{8,20},{12,24},{16,28},{20,32},{24,36},{28,40},{32,4... | collective-permute-start | bytes 3145736 | tf_op jit(solution)/shard_map/ppermute | solution.py:24
  33.0 0.6 add_add_fusion.2.sc_ref
  33.6 0.6 add_add_fusion.1.sc_ref
  34.2 83.3 %collective-permute-done.7.v_ref = bf16[256,2048]{1,0:T(8,128)(2,1)} collective-permute-done((bf16[256,2048]{1,0:T(8,128)(2,1)}, bf16[256,2048]{1,0:T(8,128)(2,1)}, u32[]{:S(2)}, u32[]{:S(2)}) %collective-permute-start.7) | collective-permute-done | bytes 1048608 | tf_op jit(solution)/shard_map/ppermute | solution.py:24
  117.6 1.9 collective-permute-start
  119.5 0.0 collective-permute-done.4.k_ref
  119.5 5.3 %collective-permute-start.1 = (bf16[256,2048]{1,0:T(8,128)(2,1)}, bf16[256,2048]{1,0:T(8,128)(2,1)}, u32[]{:S(2)}, u32[]{:S(2)}) collective-permute-start(bf16[256,2048]{1,0:T(8,128)(2,1)} %v_ref.1), channel_id=1, source_target_pairs={{0,16},{4,20},{8,24},{12,28},{16,32},{20,36},{24,40},{28,44},{32,4... | collective-permute-start | bytes 3145736 | tf_op jit(solution)/shard_map/ppermute | solution.py:24
  124.8 0.6 add_add_fusion.sc_ref
  125.4 2.7 copy.19
  128.1 3.3 reduce_sum.9
  131.5 0.0 copy-start.5
  131.5 0.1 copy.17
  131.6 2.0 copy.18
  133.6 2.0 copy.16
  135.6 14.2 %shard_map.94 = (f32[256,4096]{1,0:T(8,128)}, f32[256,2048]{1,0:T(8,128)}, f32[256,2048]{1,0:T(8,128)}) custom-call(s32[3]{0:T(128)} %add_add_fusion.4.sc_ref, bf16[256,4096]{1,0:T(8,128)(2,1)} %q_ref.9, bf16[256,4096]{1,0:T(8,128)(2,1)} %do_ref.9, bf16[256,2048]{1,0:T(8,128)(2,1)} %k_ref.1, bf16[256,2048]{1,0:T(8,128)(2,1)} %v_ref.1, ...), custom_call_target="tpu_custom_call" | custom-call | flops 2684354560 | bytes 18874368 | tf_op jit(solution)/shard_map/pallas_call | solution.py:91
  149.8 14.2 %shard_map.95 = (f32[256,4096]{1,0:T(8,128)}, bf16[256,2048]{1,0:T(8,128)(2,1)}, bf16[256,2048]{1,0:T(8,128)(2,1)}) custom-call(s32[3]{0:T(128)} %add_add_fusion.3.sc_ref, bf16[256,4096]{1,0:T(8,128)(2,1)} %q_ref.9, bf16[256,4096]{1,0:T(8,128)(2,1)} %do_ref.9, bf16[256,2048]{1,0:T(8,128)(2,1)} %copy-done.4, ...), custom_call_target="tpu_custom_call", output_to_operand_aliasing={{0}: (7, {})} | custom-call | flops 2684354560 | bytes 18874368 | tf_op jit(solution)/shard_map/pallas_call | solution.py:91
  164.0 0.0 collective-permute-done.5.v_ref
  164.0 14.2 %shard_map.96 = (f32[256,4096]{1,0:T(8,128)}, bf16[256,2048]{1,0:T(8,128)(2,1)}, bf16[256,2048]{1,0:T(8,128)(2,1)}) custom-call(s32[3]{0:T(128)} %add_add_fusion.2.sc_ref, bf16[256,4096]{1,0:T(8,128)(2,1)} %q_ref.9, bf16[256,4096]{1,0:T(8,128)(2,1)} %do_ref.9, bf16[256,2048]{1,0:T(8,128)(2,1)} %copy-done.3, ...), custom_call_target="tpu_custom_call", output_to_operand_aliasing={{0}: (7, {})} | custom-call | flops 2684354560 | bytes 18874368 | tf_op jit(solution)/shard_map/pallas_call | solution.py:91
  178.2 0.0 collective-permute-done.2.k_ref
  178.2 1.0 copy-done.2
  179.2 14.2 %shard_map.97 = (f32[256,4096]{1,0:T(8,128)}, bf16[256,2048]{1,0:T(8,128)(2,1)}, bf16[256,2048]{1,0:T(8,128)(2,1)}) custom-call(s32[3]{0:T(128)} %add_add_fusion.1.sc_ref, bf16[256,4096]{1,0:T(8,128)(2,1)} %q_ref.9, bf16[256,4096]{1,0:T(8,128)(2,1)} %do_ref.9, bf16[256,2048]{1,0:T(8,128)(2,1)} %copy-done.2, ...), custom_call_target="tpu_custom_call", output_to_operand_aliasing={{0}: (7, {})} | custom-call | flops 2684354560 | bytes 18874368 | tf_op jit(solution)/shard_map/pallas_call | solution.py:91
  193.3 0.0 collective-permute-done.k_ref
  193.3 0.0 collective-permute-done.1.v_ref
  193.4 14.5 %shard_map.98 = (f32[256,4096]{1,0:T(8,128)}, bf16[256,2048]{1,0:T(8,128)(2,1)}, bf16[256,2048]{1,0:T(8,128)(2,1)}) custom-call(s32[3]{0:T(128)} %add_add_fusion.sc_ref, bf16[256,4096]{1,0:T(8,128)(2,1)} %q_ref.9, bf16[256,4096]{1,0:T(8,128)(2,1)} %do_ref.9, bf16[256,2048]{1,0:T(8,128)(2,1)} %collective-permute-done.k_ref, ...), custom_call_target="tpu_custom_call", output_to_operand_aliasing={{0}: (7, {})} | custom-call | flops 2684354560 | bytes 18874368 | tf_op jit(solution)/shard_map/pallas_call | solution.py:91
  207.9 1.9 collective-permute-start.15
  209.8 9.1 %collective-permute-start.14 = (bf16[256,2048]{1,0:T(8,128)(2,1)}, bf16[256,2048]{1,0:T(8,128)(2,1)S(1)}, u32[]{:S(2)}, u32[]{:S(2)}) collective-permute-start(bf16[256,2048]{1,0:T(8,128)(2,1)} %get-tuple-element.31), channel_id=1, source_target_pairs={{12,0},{16,4},{20,8},{24,12},{28,16},{32,20},{36,24},{40,28},{44,3... | collective-permute-start | bytes 3145736 | tf_op jit(solution)/shard_map/ppermute | solution.py:24
  218.9 1.9 collective-permute-start.13
  220.8 2.8 collective-permute-start.12
  223.6 1.9 collective-permute-start.11
  225.5 100.7 %collective-permute-done.15 = bf16[256,2048]{1,0:T(8,128)(2,1)S(1)} collective-permute-done((bf16[256,2048]{1,0:T(8,128)(2,1)}, bf16[256,2048]{1,0:T(8,128)(2,1)S(1)}, u32[]{:S(2)}, u32[]{:S(2)}) %collective-permute-start.15) | collective-permute-done | bytes 1048608 | tf_op jit(solution)/shard_map/ppermute | solution.py:24
  326.2 1.9 collective-permute-start.10
  328.2 0.0 collective-permute-done.14
  328.2 1.9 collective-permute-start.9
  330.1 0.0 collective-permute-done.13
  330.1 1.9 collective-permute-start.8
  332.1 2.1 convert_add_fusion
  334.2 37.1 %collective-permute-done.11 = bf16[256,2048]{1,0:T(8,128)(2,1)S(1)} collective-permute-done((bf16[256,2048]{1,0:T(8,128)(2,1)}, bf16[256,2048]{1,0:T(8,128)(2,1)S(1)}, u32[]{:S(2)}, u32[]{:S(2)}) %collective-permute-start.11) | collective-permute-done | bytes 1048608 | tf_op jit(solution)/shard_map/ppermute | solution.py:24
  371.3 0.0 collective-permute-done.8
  371.3 2.1 convert_add_fusion.1
  (18 shorter events, 0.1 us)
Async XLA Ops:
  0.6 28.1 %collective-permute-start.6 = (bf16[256,2048]{1,0:T(8,128)(2,1)}, bf16[256,2048]{1,0:T(8,128)(2,1)S(1)}, u32[]{:S(2)}, u32[]{:S(2)}) collective-permute-start(bf16[256,2048]{1,0:T(8,128)(2,1)} %k_ref.1), channel_id=1, source_target_pairs={{0,4},{4,8},{8,12},{12,16},{16,20},{20,24},{24,28},{28,32},{32,36}... | collective-permute-start | bytes 3145736 | tf_op jit(solution)/shard_map/ppermute | solution.py:24
  4.6 113.0 %collective-permute-start.7 = (bf16[256,2048]{1,0:T(8,128)(2,1)}, bf16[256,2048]{1,0:T(8,128)(2,1)}, u32[]{:S(2)}, u32[]{:S(2)}) collective-permute-start(bf16[256,2048]{1,0:T(8,128)(2,1)} %v_ref.1), channel_id=1, source_target_pairs={{0,4},{4,8},{8,12},{12,16},{16,20},{20,24},{24,28},{28,32},{32,36}... | collective-permute-start | bytes 3145736 | tf_op jit(solution)/shard_map/ppermute | solution.py:24
  8.0 111.5 %collective-permute-start.4 = (bf16[256,2048]{1,0:T(8,128)(2,1)}, bf16[256,2048]{1,0:T(8,128)(2,1)S(1)}, u32[]{:S(2)}, u32[]{:S(2)}) collective-permute-start(bf16[256,2048]{1,0:T(8,128)(2,1)} %k_ref.1), channel_id=1, source_target_pairs={{0,8},{4,12},{8,16},{12,20},{16,24},{20,28},{24,32},{28,36},{32,40... | collective-permute-start | bytes 3145736 | tf_op jit(solution)/shard_map/ppermute | solution.py:24
  12.0 152.0 %collective-permute-start.5 = (bf16[256,2048]{1,0:T(8,128)(2,1)}, bf16[256,2048]{1,0:T(8,128)(2,1)}, u32[]{:S(2)}, u32[]{:S(2)}) collective-permute-start(bf16[256,2048]{1,0:T(8,128)(2,1)} %v_ref.1), channel_id=1, source_target_pairs={{0,8},{4,12},{8,16},{12,20},{16,24},{20,28},{24,32},{28,36},{32,40... | collective-permute-start | bytes 3145736 | tf_op jit(solution)/shard_map/ppermute | solution.py:24
  16.1 162.1 %collective-permute-start.2 = (bf16[256,2048]{1,0:T(8,128)(2,1)}, bf16[256,2048]{1,0:T(8,128)(2,1)S(1)}, u32[]{:S(2)}, u32[]{:S(2)}) collective-permute-start(bf16[256,2048]{1,0:T(8,128)(2,1)} %k_ref.1), channel_id=1, source_target_pairs={{0,12},{4,16},{8,20},{12,24},{16,28},{20,32},{24,36},{28,40},{32,4... | collective-permute-start | bytes 3145736 | tf_op jit(solution)/shard_map/ppermute | solution.py:24
  28.8 99.4 %copy-start.4 = (bf16[256,2048]{1,0:T(8,128)(2,1)}, bf16[256,2048]{1,0:T(8,128)(2,1)S(1)}, u32[]{:S(2)}) copy-start(bf16[256,2048]{1,0:T(8,128)(2,1)S(1)} %collective-permute-done.6.k_ref) | copy-start | bytes 3145732
  28.8 149.4 %collective-permute-start.3 = (bf16[256,2048]{1,0:T(8,128)(2,1)}, bf16[256,2048]{1,0:T(8,128)(2,1)}, u32[]{:S(2)}, u32[]{:S(2)}) collective-permute-start(bf16[256,2048]{1,0:T(8,128)(2,1)} %v_ref.1), channel_id=1, source_target_pairs={{0,12},{4,16},{8,20},{12,24},{16,28},{20,32},{24,36},{28,40},{32,4... | collective-permute-start | bytes 3145736 | tf_op jit(solution)/shard_map/ppermute | solution.py:24
  117.6 75.8 %collective-permute-start = (bf16[256,2048]{1,0:T(8,128)(2,1)}, bf16[256,2048]{1,0:T(8,128)(2,1)}, u32[]{:S(2)}, u32[]{:S(2)}) collective-permute-start(bf16[256,2048]{1,0:T(8,128)(2,1)} %k_ref.1), channel_id=1, source_target_pairs={{0,16},{4,20},{8,24},{12,28},{16,32},{20,36},{24,40},{28,44},{32,4... | collective-permute-start | bytes 3145736 | tf_op jit(solution)/shard_map/ppermute | solution.py:24
  119.5 8.6 %copy-start.3 = (bf16[256,2048]{1,0:T(8,128)(2,1)}, bf16[256,2048]{1,0:T(8,128)(2,1)S(1)}, u32[]{:S(2)}) copy-start(bf16[256,2048]{1,0:T(8,128)(2,1)S(1)} %collective-permute-done.4.k_ref) | copy-start | bytes 3145732
  119.5 73.8 %collective-permute-start.1 = (bf16[256,2048]{1,0:T(8,128)(2,1)}, bf16[256,2048]{1,0:T(8,128)(2,1)}, u32[]{:S(2)}, u32[]{:S(2)}) collective-permute-start(bf16[256,2048]{1,0:T(8,128)(2,1)} %v_ref.1), channel_id=1, source_target_pairs={{0,16},{4,20},{8,24},{12,28},{16,32},{20,36},{24,40},{28,44},{32,4... | collective-permute-start | bytes 3145736 | tf_op jit(solution)/shard_map/ppermute | solution.py:24
  131.5 2.1 copy-start.5
  178.2 1.0 copy-start.2
  193.3 136.8 %copy-start.6 = (bf16[256,2048]{1,0:T(8,128)(2,1)S(1)}, bf16[256,2048]{1,0:T(8,128)(2,1)}, u32[]{:S(2)}) copy-start(bf16[256,2048]{1,0:T(8,128)(2,1)} %get-tuple-element.24) | copy-start | bytes 3145732
  193.3 138.7 %copy-start.1 = (f32[256,2048]{1,0:T(8,128)S(1)}, f32[256,2048]{1,0:T(8,128)}, u32[]{:S(2)}) copy-start(f32[256,2048]{1,0:T(8,128)} %get-tuple-element.28) | copy-start | bytes 6291460
  207.9 118.4 %collective-permute-start.15 = (bf16[256,2048]{1,0:T(8,128)(2,1)}, bf16[256,2048]{1,0:T(8,128)(2,1)S(1)}, u32[]{:S(2)}, u32[]{:S(2)}) collective-permute-start(bf16[256,2048]{1,0:T(8,128)(2,1)} %get-tuple-element.32), channel_id=1, source_target_pairs={{16,0},{20,4},{24,8},{28,12},{32,16},{36,20},{40,24},{44,28},{48,3... | collective-permute-start | bytes 3145736 | tf_op jit(solution)/shard_map/ppermute | solution.py:24
  209.8 118.4 %collective-permute-start.14 = (bf16[256,2048]{1,0:T(8,128)(2,1)}, bf16[256,2048]{1,0:T(8,128)(2,1)S(1)}, u32[]{:S(2)}, u32[]{:S(2)}) collective-permute-start(bf16[256,2048]{1,0:T(8,128)(2,1)} %get-tuple-element.31), channel_id=1, source_target_pairs={{12,0},{16,4},{20,8},{24,12},{28,16},{32,20},{36,24},{40,28},{44,3... | collective-permute-start | bytes 3145736 | tf_op jit(solution)/shard_map/ppermute | solution.py:24
  218.9 111.2 %collective-permute-start.13 = (bf16[256,2048]{1,0:T(8,128)(2,1)}, bf16[256,2048]{1,0:T(8,128)(2,1)S(1)}, u32[]{:S(2)}, u32[]{:S(2)}) collective-permute-start(bf16[256,2048]{1,0:T(8,128)(2,1)} %get-tuple-element.30), channel_id=1, source_target_pairs={{8,0},{12,4},{16,8},{20,12},{24,16},{28,20},{32,24},{36,28},{40,32... | collective-permute-start | bytes 3145736 | tf_op jit(solution)/shard_map/ppermute | solution.py:24
  220.8 111.2 %collective-permute-start.12 = (bf16[256,2048]{1,0:T(8,128)(2,1)}, bf16[256,2048]{1,0:T(8,128)(2,1)S(1)}, u32[]{:S(2)}, u32[]{:S(2)}) collective-permute-start(bf16[256,2048]{1,0:T(8,128)(2,1)} %get-tuple-element.29), channel_id=1, source_target_pairs={{4,0},{8,4},{12,8},{16,12},{20,16},{24,20},{28,24},{32,28},{36,32}... | collective-permute-start | bytes 3145736 | tf_op jit(solution)/shard_map/ppermute | solution.py:24
  223.6 147.7 %collective-permute-start.11 = (bf16[256,2048]{1,0:T(8,128)(2,1)}, bf16[256,2048]{1,0:T(8,128)(2,1)S(1)}, u32[]{:S(2)}, u32[]{:S(2)}) collective-permute-start(bf16[256,2048]{1,0:T(8,128)(2,1)} %get-tuple-element.27), channel_id=1, source_target_pairs={{16,0},{20,4},{24,8},{28,12},{32,16},{36,20},{40,24},{44,28},{48,3... | collective-permute-start | bytes 3145736 | tf_op jit(solution)/shard_map/ppermute | solution.py:24
  326.2 45.0 %collective-permute-start.10 = (bf16[256,2048]{1,0:T(8,128)(2,1)}, bf16[256,2048]{1,0:T(8,128)(2,1)S(1)}, u32[]{:S(2)}, u32[]{:S(2)}) collective-permute-start(bf16[256,2048]{1,0:T(8,128)(2,1)} %get-tuple-element.26), channel_id=1, source_target_pairs={{12,0},{16,4},{20,8},{24,12},{28,16},{32,20},{36,24},{40,28},{44,3... | collective-permute-start | bytes 3145736 | tf_op jit(solution)/shard_map/ppermute | solution.py:24
  328.2 43.1 %collective-permute-start.9 = (bf16[256,2048]{1,0:T(8,128)(2,1)}, bf16[256,2048]{1,0:T(8,128)(2,1)S(1)}, u32[]{:S(2)}, u32[]{:S(2)}) collective-permute-start(bf16[256,2048]{1,0:T(8,128)(2,1)} %get-tuple-element.25), channel_id=1, source_target_pairs={{8,0},{12,4},{16,8},{20,12},{24,16},{28,20},{32,24},{36,28},{40,32... | collective-permute-start | bytes 3145736 | tf_op jit(solution)/shard_map/ppermute | solution.py:24
  330.1 41.2 %collective-permute-start.8 = (bf16[256,2048]{1,0:T(8,128)(2,1)S(1)}, bf16[256,2048]{1,0:T(8,128)(2,1)S(1)}, u32[]{:S(2)}, u32[]{:S(2)}) collective-permute-start(bf16[256,2048]{1,0:T(8,128)(2,1)S(1)} %copy-done.6), channel_id=1, source_target_pairs={{4,0},{8,4},{12,8},{16,12},{20,16},{24,20},{28,24},{32,28},{36,32}... | collective-permute-start | bytes 3145736 | tf_op jit(solution)/shard_map/ppermute | solution.py:24
  332.1 39.2 %copy-start = (f32[256,2048]{1,0:T(8,128)S(1)}, f32[256,2048]{1,0:T(8,128)}, u32[]{:S(2)}) copy-start(f32[256,2048]{1,0:T(8,128)} %get-tuple-element.23) | copy-start | bytes 6291460
where the time goes:
time: 374 us; the launch traced here: 373 us
  waiting for transfers between devices  225 us (60%)
  Pallas kernels  71.3 us (19%)
  starting transfers between devices  54.2 us (14%)
  other arithmetic  13.5 us (4%)
  local copies, waits for them, and re-layouts  7.82 us (2%)
    ppermute x16, waiting for transfers between devices, passed_along(): return lax.ppermute(x, axis, pairs)  225 us
    pallas_call x5, Pallas kernels, pair_grads(): pl.pallas_call(functools.partial(pair_kernel, group, heads, accumulate),...  71.3 us
    ppermute x16, starting transfers between devices, passed_along(): return lax.ppermute(x, axis, pairs)  54.2 us
  transfers between devices with their start and end apart: 16, of which 4 were waited for; matrix products, arithmetic and copies ran while one was open for 5% of the time, Pallas kernels for 15%

commit v1 on v0

--- a/solution.py
+++ b/solution.py
@@ -13,6 +13,8 @@
 HEAD_SIZE = 128
 WINDOW = 1024
 HEADS_PER_STEP = 4
+ROW_DEVICES = 4
+PAIR_ORDER = (1, 4, 2, 3)
 
 
 score_scale = 168.0 ** (-0.5)
@@ -104,6 +106,10 @@
     )(scalars, *args)
 
 
+def sent_by(x, axis, pairs):
+    return lax.ppermute(x, axis, pairs)
+
+
 def local(
     queries,
     stored_keys,
@@ -116,10 +122,16 @@
     tokens_here = queries.shape[0]
     blocks = WINDOW // tokens_here
     group = QUERY_HEADS // KEY_VALUE_HEADS
+    count = lax.axis_size("seq")
     shard = lax.axis_index("seq")
-    halos = []
-    for distance in range(1, blocks + 1):
-        halos.append(passed_along((stored_keys, stored_values), "seq", distance))
+    row = ROW_DEVICES
+    kv = (stored_keys, stored_values)
+    far = passed_along(kv, "seq", blocks)
+    near = sent_by(kv, "seq", [(i, i + 1) for i in range(count - 1) if i % row != row - 1])
+    handed = sent_by(far, "seq", [(i, i - row + 1) for i in range(row, count) if i % row == row - 1])
+    halos = {blocks: far, 1: (near[0] + handed[0], near[1] + handed[1])}
+    for distance in range(2, blocks):
+        halos[distance] = passed_along(kv, "seq", distance)
     limit = valid_count[0]
 
     delta = jnp.sum(
@@ -138,8 +150,9 @@
     dq, key_grad, value_grad = pair_grads(
         scalars_for(0), queries, output_cotangent, stored_keys, stored_values, lse3, dl3, None, jnp.float32
     )
-    for distance in range(1, blocks + 1):
-        k_far, v_far = halos[distance - 1]
+    handed_back = None
+    for distance in PAIR_ORDER:
+        k_far, v_far = halos[distance]
         dq, dk_part, dv_part = pair_grads(
             scalars_for(distance),
             queries,
@@ -151,7 +164,18 @@
             dq,
             jnp.bfloat16,
         )
-        arrived = passed_along((dk_part, dv_part), "seq", -distance)
+        if distance == 1:
+            arrived = sent_by(
+                (dk_part, dv_part), "seq", [(i, i - 1) for i in range(1, count) if i % row != 0]
+            )
+            handed_back = sent_by(
+                (dk_part, dv_part), "seq", [(i, i + row - 1) for i in range(row, count) if i % row == 0]
+            )
+        else:
+            if distance == blocks:
+                dk_part = (dk_part.astype(jnp.float32) + handed_back[0].astype(jnp.float32)).astype(jnp.bfloat16)
+                dv_part = (dv_part.astype(jnp.float32) + handed_back[1].astype(jnp.float32)).astype(jnp.bfloat16)
+            arrived = passed_along((dk_part, dv_part), "seq", -distance)
         key_grad = key_grad + arrived[0].astype(jnp.float32)
         value_grad = value_grad + arrived[1].astype(jnp.float32)
     return (dq, key_grad, value_grad)

time: 374 us -> 333 us (0.89)
  the two profiles are of different devices: /device:TPU:30 before, /device:TPU:31 now
where the time goes in v1:
time: 333 us; the launch traced here: 329 us
  waiting for transfers between devices  169 us (51%)
  Pallas kernels  70.9 us (21%)
  starting transfers between devices  56.8 us (17%)
  other arithmetic  22.7 us (7%)
  local copies, waits for them, and re-layouts  7.83 us (2%)
    ppermute x12, waiting for transfers between devices, passed_along(): return lax.ppermute(x, axis, pairs)  150 us
    pallas_call x5, Pallas kernels, pair_grads(): pl.pallas_call(functools.partial(pair_kernel, group, heads, accumulate),...  70.9 us
    ppermute x12, starting transfers between devices, passed_along(): return lax.ppermute(x, axis, pairs)  41.1 us
    ppermute x8, waiting for transfers between devices, sent_by(): return lax.ppermute(x, axis, pairs)  18.4 us
    ppermute x8, starting transfers between devices, sent_by(): return lax.ppermute(x, axis, pairs)  15.8 us
  transfers between devices with their start and end apart: 20, of which 6 were waited for; matrix products, arithmetic and copies ran while one was open for 8% of the time, Pallas kernels for 22%

profile of v1, /device:TPU:31, one launch (start us, length us, event | category | flops | bytes accessed | tf_op | source)
XLA Modules:
  0.0 328.7 jit_solution(5467601833513264181)
XLA Ops:
  0.6 3.7 %collective-permute-start.4 = (bf16[256,2048]{1,0:T(8,128)(2,1)}, bf16[256,2048]{1,0:T(8,128)(2,1)S(1)}, u32[]{:S(2)}, u32[]{:S(2)}) collective-permute-start(bf16[256,2048]{1,0:T(8,128)(2,1)} %k_ref.1), channel_id=1, source_target_pairs={{0,16},{4,20},{8,24},{12,28},{16,32},{20,36},{24,40},{28,44},{32,4... | collective-permute-start | bytes 3145736 | tf_op jit(solution)/shard_map/ppermute | solution.py:26
  4.4 2.9 collective-permute-start.5
  7.3 1.3 collective-permute-start.6
  8.6 18.3 %collective-permute-done.4.k_ref = bf16[256,2048]{1,0:T(8,128)(2,1)S(1)} collective-permute-done((bf16[256,2048]{1,0:T(8,128)(2,1)}, bf16[256,2048]{1,0:T(8,128)(2,1)S(1)}, u32[]{:S(2)}, u32[]{:S(2)}) %collective-permute-start.4) | collective-permute-done | bytes 1048608 | tf_op jit(solution)/shard_map/ppermute | solution.py:26
  26.9 3.0 collective-permute-start.7
  29.9 1.3 collective-permute-start.8
  31.1 18.2 %collective-permute-done.5.v_ref = bf16[256,2048]{1,0:T(8,128)(2,1)S(1)} collective-permute-done((bf16[256,2048]{1,0:T(8,128)(2,1)}, bf16[256,2048]{1,0:T(8,128)(2,1)S(1)}, u32[]{:S(2)}, u32[]{:S(2)}) %collective-permute-start.5) | collective-permute-done | bytes 1048608 | tf_op jit(solution)/shard_map/ppermute | solution.py:26
  49.4 3.1 collective-permute-start.9
  52.5 3.9 %collective-permute-start.2 = (bf16[256,2048]{1,0:T(8,128)(2,1)}, bf16[256,2048]{1,0:T(8,128)(2,1)S(1)}, u32[]{:S(2)}, u32[]{:S(2)}) collective-permute-start(bf16[256,2048]{1,0:T(8,128)(2,1)} %k_ref.1), channel_id=1, source_target_pairs={{0,8},{4,12},{8,16},{12,20},{16,24},{20,28},{24,32},{28,36},{32,40... | collective-permute-start | bytes 3145736 | tf_op jit(solution)/shard_map/ppermute | solution.py:26
  57.0 2.9 multiply_bitcast_fusion
  60.0 2.8 copy.19
  62.8 3.3 %reduce_sum.9 = f32[256,32]{1,0:T(8,128)S(1)} reduce(f32[256,32,128]{2,1,0:T(8,128)} %bitcast.25, f32[]{:T(128)} %constant.17.clone.1), dimensions={2}, to_apply=%region_0.0 | reduce | flops 1040384 | bytes 4227076 | tf_op jit(solution)/shard_map/reduce_sum | solution.py:137
  66.2 2.0 copy.18
  68.2 2.0 copy.16
  70.2 0.6 add_add_fusion.4.sc_ref
  70.8 0.7 add_add_fusion.3.sc_ref
  71.5 5.3 %collective-permute-start.3 = (bf16[256,2048]{1,0:T(8,128)(2,1)}, bf16[256,2048]{1,0:T(8,128)(2,1)}, u32[]{:S(2)}, u32[]{:S(2)}) collective-permute-start(bf16[256,2048]{1,0:T(8,128)(2,1)} %v_ref.1), channel_id=1, source_target_pairs={{0,8},{4,12},{8,16},{12,20},{16,24},{20,28},{24,32},{28,36},{32,40... | collective-permute-start | bytes 3145736 | tf_op jit(solution)/shard_map/ppermute | solution.py:26
  76.8 14.0 %shard_map.94 = (f32[256,4096]{1,0:T(8,128)}, f32[256,2048]{1,0:T(8,128)}, f32[256,2048]{1,0:T(8,128)}) custom-call(s32[3]{0:T(128)} %add_add_fusion.4.sc_ref, bf16[256,4096]{1,0:T(8,128)(2,1)} %q_ref.9, bf16[256,4096]{1,0:T(8,128)(2,1)} %do_ref.9, bf16[256,2048]{1,0:T(8,128)(2,1)} %k_ref.1, bf16[256,2048]{1,0:T(8,128)(2,1)} %v_ref.1, ...), custom_call_target="tpu_custom_call" | custom-call | flops 2684354560 | bytes 18874368 | tf_op jit(solution)/shard_map/pallas_call | solution.py:93
  90.8 1.9 collective-permute-start
  92.8 2.9 add.40.k_ref
  95.7 3.4 %collective-permute-start.1 = (bf16[256,2048]{1,0:T(8,128)(2,1)}, bf16[256,2048]{1,0:T(8,128)(2,1)}, u32[]{:S(2)}, u32[]{:S(2)}) collective-permute-start(bf16[256,2048]{1,0:T(8,128)(2,1)} %v_ref.1), channel_id=1, source_target_pairs={{0,12},{4,16},{8,20},{12,24},{16,28},{20,32},{24,36},{28,40},{32,4... | collective-permute-start | bytes 3145736 | tf_op jit(solution)/shard_map/ppermute | solution.py:26
  99.1 18.4 %collective-permute-done.9 = bf16[256,2048]{1,0:T(8,128)(2,1)} collective-permute-done((bf16[256,2048]{1,0:T(8,128)(2,1)S(1)}, bf16[256,2048]{1,0:T(8,128)(2,1)}, u32[]{:S(2)}, u32[]{:S(2)}) %collective-permute-start.9) | collective-permute-done | bytes 1048608 | tf_op jit(solution)/shard_map/ppermute | solution.py:110
  117.5 2.9 add.41.v_ref
  120.4 14.2 %shard_map.95 = (f32[256,4096]{1,0:T(8,128)}, bf16[256,2048]{1,0:T(8,128)(2,1)}, bf16[256,2048]{1,0:T(8,128)(2,1)}) custom-call(s32[3]{0:T(128)} %add_add_fusion.3.sc_ref, bf16[256,4096]{1,0:T(8,128)(2,1)} %q_ref.9, bf16[256,4096]{1,0:T(8,128)(2,1)} %do_ref.9, bf16[256,2048]{1,0:T(8,128)(2,1)} %add.40.k_ref, ...), custom_call_target="tpu_custom_call", output_to_operand_aliasing={{0}: (7, {})} | custom-call | flops 2684354560 | bytes 18874368 | tf_op jit(solution)/shard_map/pallas_call | solution.py:93
  134.5 1.5 collective-permute-start.16
  136.0 0.6 add_add_fusion.2.sc_ref
  136.6 0.6 add_add_fusion.1.sc_ref
  137.2 0.7 add_add_fusion.sc_ref
  137.8 14.2 %shard_map.96 = (f32[256,4096]{1,0:T(8,128)}, bf16[256,2048]{1,0:T(8,128)(2,1)}, bf16[256,2048]{1,0:T(8,128)(2,1)}) custom-call(s32[3]{0:T(128)} %add_add_fusion.2.sc_ref, bf16[256,4096]{1,0:T(8,128)(2,1)} %q_ref.9, bf16[256,4096]{1,0:T(8,128)(2,1)} %do_ref.9, bf16[256,2048]{1,0:T(8,128)(2,1)} %copy-done.2, ...), custom_call_target="tpu_custom_call", output_to_operand_aliasing={{0}: (7, {})} | custom-call | flops 2684354560 | bytes 18874368 | tf_op jit(solution)/shard_map/pallas_call | solution.py:93
  152.0 2.3 collective-permute-start.15
  154.3 1.3 collective-permute-start.11
  155.6 14.2 %shard_map.97 = (f32[256,4096]{1,0:T(8,128)}, bf16[256,2048]{1,0:T(8,128)(2,1)}, bf16[256,2048]{1,0:T(8,128)(2,1)}) custom-call(s32[3]{0:T(128)} %add_add_fusion.1.sc_ref, bf16[256,4096]{1,0:T(8,128)(2,1)} %q_ref.9, bf16[256,4096]{1,0:T(8,128)(2,1)} %do_ref.9, bf16[256,2048]{1,0:T(8,128)(2,1)} %copy-done.4, ...), custom_call_target="tpu_custom_call", output_to_operand_aliasing={{0}: (7, {})} | custom-call | flops 2684354560 | bytes 18874368 | tf_op jit(solution)/shard_map/pallas_call | solution.py:93
  169.8 1.0 copy-done.5
  170.8 14.3 %shard_map.98 = (f32[256,4096]{1,0:T(8,128)}, bf16[256,2048]{1,0:T(8,128)(2,1)}, bf16[256,2048]{1,0:T(8,128)(2,1)}) custom-call(s32[3]{0:T(128)} %add_add_fusion.sc_ref, bf16[256,4096]{1,0:T(8,128)(2,1)} %q_ref.9, bf16[256,4096]{1,0:T(8,128)(2,1)} %do_ref.9, bf16[256,2048]{1,0:T(8,128)(2,1)} %copy-done.5, ...), custom_call_target="tpu_custom_call", output_to_operand_aliasing={{0}: (7, {})} | custom-call | flops 2684354560 | bytes 18874368 | tf_op jit(solution)/shard_map/pallas_call | solution.py:93
  185.1 6.3 %collective-permute-start.19 = (bf16[256,2048]{1,0:T(8,128)(2,1)}, bf16[256,2048]{1,0:T(8,128)(2,1)S(1)}, u32[]{:S(2)}, u32[]{:S(2)}) collective-permute-start(bf16[256,2048]{1,0:T(8,128)(2,1)} %get-tuple-element.32), channel_id=1, source_target_pairs={{12,0},{16,4},{20,8},{24,12},{28,16},{32,20},{36,24},{40,28},{44,3... | collective-permute-start | bytes 3145736 | tf_op jit(solution)/shard_map/ppermute | solution.py:26
  191.4 2.4 collective-permute-start.18
  193.8 0.4 add_convert_fusion
  194.3 2.2 collective-permute-start.17
  196.5 2.1 collective-permute-start.10
  198.6 1.6 add_convert_fusion.1
  200.2 34.7 %collective-permute-done.19 = bf16[256,2048]{1,0:T(8,128)(2,1)S(1)} collective-permute-done((bf16[256,2048]{1,0:T(8,128)(2,1)}, bf16[256,2048]{1,0:T(8,128)(2,1)S(1)}, u32[]{:S(2)}, u32[]{:S(2)}) %collective-permute-start.19) | collective-permute-done | bytes 1048608 | tf_op jit(solution)/shard_map/ppermute | solution.py:26
  234.8 5.2 %collective-permute-start.14 = (bf16[256,2048]{1,0:T(8,128)(2,1)S(1)}, bf16[256,2048]{1,0:T(8,128)(2,1)S(1)}, u32[]{:S(2)}, u32[]{:S(2)}) collective-permute-start(bf16[256,2048]{1,0:T(8,128)(2,1)S(1)} %copy-done.11), channel_id=1, source_target_pairs={{12,0},{16,4},{20,8},{24,12},{28,16},{32,20},{36,24},{40,28},{44,3... | collective-permute-start | bytes 3145736 | tf_op jit(solution)/shard_map/ppermute | solution.py:26
  240.1 1.9 collective-permute-start.13
  242.0 1.9 collective-permute-start.12
  243.9 60.2 %collective-permute-done.17 = bf16[256,2048]{1,0:T(8,128)(2,1)S(1)} collective-permute-done((bf16[256,2048]{1,0:T(8,128)(2,1)S(1)}, bf16[256,2048]{1,0:T(8,128)(2,1)S(1)}, u32[]{:S(2)}, u32[]{:S(2)}) %collective-permute-start.17) | collective-permute-done | bytes 1048608 | tf_op jit(solution)/shard_map/ppermute | solution.py:26
  304.1 3.4 %convert_add_fusion = f32[256,2048]{1,0:T(8,128)} fusion(bf16[256,2048]{1,0:T(8,128)(2,1)S(1)} %collective-permute-done.19, bf16[256,2048]{1,0:T(8,128)(2,1)S(1)} %collective-permute-done.18, bf16[256,2048]{1,0:T(8,128)(2,1)S(1)} %collective-permute-done.17, f32[256,2048]{1,0:T(8,128)S(1)} %copy-done.1, bf16[256,2048]{1,0:T(8,128)(2,1)} %collective-permute-done.15), kind=kLoop, calls=%fused_computation.1 | loop fusion | flops 4194304 | bytes 8388608 | tf_op jit(solution)/shard_map/add | solution.py:180
  307.6 19.0 %collective-permute-done.12 = bf16[256,2048]{1,0:T(8,128)(2,1)S(1)} collective-permute-done((bf16[256,2048]{1,0:T(8,128)(2,1)S(1)}, bf16[256,2048]{1,0:T(8,128)(2,1)S(1)}, u32[]{:S(2)}, u32[]{:S(2)}) %collective-permute-start.12) | collective-permute-done | bytes 1048608 | tf_op jit(solution)/shard_map/ppermute | solution.py:26
  326.6 2.1 convert_add_fusion.1
  (40 shorter events, 0.2 us)
Async XLA Ops:
  0.6 26.3 %collective-permute-start.4 = (bf16[256,2048]{1,0:T(8,128)(2,1)}, bf16[256,2048]{1,0:T(8,128)(2,1)S(1)}, u32[]{:S(2)}, u32[]{:S(2)}) collective-permute-start(bf16[256,2048]{1,0:T(8,128)(2,1)} %k_ref.1), channel_id=1, source_target_pairs={{0,16},{4,20},{8,24},{12,28},{16,32},{20,36},{24,40},{28,44},{32,4... | collective-permute-start | bytes 3145736 | tf_op jit(solution)/shard_map/ppermute | solution.py:26
  4.4 45.0 %collective-permute-start.5 = (bf16[256,2048]{1,0:T(8,128)(2,1)}, bf16[256,2048]{1,0:T(8,128)(2,1)S(1)}, u32[]{:S(2)}, u32[]{:S(2)}) collective-permute-start(bf16[256,2048]{1,0:T(8,128)(2,1)} %v_ref.1), channel_id=1, source_target_pairs={{0,16},{4,20},{8,24},{12,28},{16,32},{20,36},{24,40},{28,44},{32,4... | collective-permute-start | bytes 3145736 | tf_op jit(solution)/shard_map/ppermute | solution.py:26
  7.3 64.2 %collective-permute-start.6 = (bf16[256,2048]{1,0:T(8,128)(2,1)}, bf16[256,2048]{1,0:T(8,128)(2,1)}, u32[]{:S(2)}, u32[]{:S(2)}) collective-permute-start(bf16[256,2048]{1,0:T(8,128)(2,1)} %k_ref.1), channel_id=1, source_target_pairs={{0,4},{4,8},{8,12},{16,20},{20,24},{24,28},{32,36},{36,40},{40,44}... | collective-permute-start | bytes 3145736 | tf_op jit(solution)/shard_map/ppermute | solution.py:110
  26.9 33.1 %copy-start.2 = (bf16[256,2048]{1,0:T(8,128)(2,1)}, bf16[256,2048]{1,0:T(8,128)(2,1)S(1)}, u32[]{:S(2)}) copy-start(bf16[256,2048]{1,0:T(8,128)(2,1)S(1)} %collective-permute-done.4.k_ref) | copy-start | bytes 3145732
  26.9 63.9 %collective-permute-start.7 = (bf16[256,2048]{1,0:T(8,128)(2,1)S(1)}, bf16[256,2048]{1,0:T(8,128)(2,1)}, u32[]{:S(2)}, u32[]{:S(2)}) collective-permute-start(bf16[256,2048]{1,0:T(8,128)(2,1)S(1)} %collective-permute-done.4.k_ref), channel_id=1, source_target_pairs={{28,16},{44,32},{60,48},{76,64},{92,80},{108,96},{124,112},{29,17}... | collective-permute-start | bytes 3145736 | tf_op jit(solution)/shard_map/ppermute | solution.py:110
  29.9 65.8 %collective-permute-start.8 = (bf16[256,2048]{1,0:T(8,128)(2,1)}, bf16[256,2048]{1,0:T(8,128)(2,1)}, u32[]{:S(2)}, u32[]{:S(2)}) collective-permute-start(bf16[256,2048]{1,0:T(8,128)(2,1)} %v_ref.1), channel_id=1, source_target_pairs={{0,4},{4,8},{8,12},{16,20},{20,24},{24,28},{32,36},{36,40},{40,44}... | collective-permute-start | bytes 3145736 | tf_op jit(solution)/shard_map/ppermute | solution.py:110
  49.4 10.6 %copy-start.3 = (bf16[256,2048]{1,0:T(8,128)(2,1)}, bf16[256,2048]{1,0:T(8,128)(2,1)S(1)}, u32[]{:S(2)}) copy-start(bf16[256,2048]{1,0:T(8,128)(2,1)S(1)} %collective-permute-done.5.v_ref) | copy-start | bytes 3145732
  49.4 68.1 %collective-permute-start.9 = (bf16[256,2048]{1,0:T(8,128)(2,1)S(1)}, bf16[256,2048]{1,0:T(8,128)(2,1)}, u32[]{:S(2)}, u32[]{:S(2)}) collective-permute-start(bf16[256,2048]{1,0:T(8,128)(2,1)S(1)} %collective-permute-done.5.v_ref), channel_id=1, source_target_pairs={{28,16},{44,32},{60,48},{76,64},{92,80},{108,96},{124,112},{29,17}... | collective-permute-start | bytes 3145736 | tf_op jit(solution)/shard_map/ppermute | solution.py:110
  52.5 99.5 %collective-permute-start.2 = (bf16[256,2048]{1,0:T(8,128)(2,1)}, bf16[256,2048]{1,0:T(8,128)(2,1)S(1)}, u32[]{:S(2)}, u32[]{:S(2)}) collective-permute-start(bf16[256,2048]{1,0:T(8,128)(2,1)} %k_ref.1), channel_id=1, source_target_pairs={{0,8},{4,12},{8,16},{12,20},{16,24},{20,28},{24,32},{28,36},{32,40... | collective-permute-start | bytes 3145736 | tf_op jit(solution)/shard_map/ppermute | solution.py:26
  66.1 2.1 copy-start.8
  71.5 82.8 %collective-permute-start.3 = (bf16[256,2048]{1,0:T(8,128)(2,1)}, bf16[256,2048]{1,0:T(8,128)(2,1)}, u32[]{:S(2)}, u32[]{:S(2)}) collective-permute-start(bf16[256,2048]{1,0:T(8,128)(2,1)} %v_ref.1), channel_id=1, source_target_pairs={{0,8},{4,12},{8,16},{12,20},{16,24},{20,28},{24,32},{28,36},{32,40... | collective-permute-start | bytes 3145736 | tf_op jit(solution)/shard_map/ppermute | solution.py:26
  90.8 79.0 %collective-permute-start = (bf16[256,2048]{1,0:T(8,128)(2,1)}, bf16[256,2048]{1,0:T(8,128)(2,1)S(1)}, u32[]{:S(2)}, u32[]{:S(2)}) collective-permute-start(bf16[256,2048]{1,0:T(8,128)(2,1)} %k_ref.1), channel_id=1, source_target_pairs={{0,12},{4,16},{8,20},{12,24},{16,28},{20,32},{24,36},{28,40},{32,4... | collective-permute-start | bytes 3145736 | tf_op jit(solution)/shard_map/ppermute | solution.py:26
  95.7 74.1 %collective-permute-start.1 = (bf16[256,2048]{1,0:T(8,128)(2,1)}, bf16[256,2048]{1,0:T(8,128)(2,1)}, u32[]{:S(2)}, u32[]{:S(2)}) collective-permute-start(bf16[256,2048]{1,0:T(8,128)(2,1)} %v_ref.1), channel_id=1, source_target_pairs={{0,12},{4,16},{8,20},{12,24},{16,28},{20,32},{24,36},{28,40},{32,4... | collective-permute-start | bytes 3145736 | tf_op jit(solution)/shard_map/ppermute | solution.py:26
  134.5 59.3 %collective-permute-start.16 = (bf16[256,2048]{1,0:T(8,128)(2,1)}, bf16[256,2048]{1,0:T(8,128)(2,1)S(1)}, u32[]{:S(2)}, u32[]{:S(2)}) collective-permute-start(bf16[256,2048]{1,0:T(8,128)(2,1)} %get-tuple-element.29), channel_id=1, source_target_pairs={{16,28},{32,44},{48,60},{64,76},{80,92},{96,108},{112,124},{17,29}... | collective-permute-start | bytes 3145736 | tf_op jit(solution)/shard_map/ppermute | solution.py:110
  152.0 3.6 %copy-start.4 = (bf16[256,2048]{1,0:T(8,128)(2,1)}, bf16[256,2048]{1,0:T(8,128)(2,1)S(1)}, u32[]{:S(2)}) copy-start(bf16[256,2048]{1,0:T(8,128)(2,1)S(1)} %collective-permute-done.2.k_ref) | copy-start | bytes 3145732
  152.0 90.0 %collective-permute-start.15 = (bf16[256,2048]{1,0:T(8,128)(2,1)}, bf16[256,2048]{1,0:T(8,128)(2,1)}, u32[]{:S(2)}, u32[]{:S(2)}) collective-permute-start(bf16[256,2048]{1,0:T(8,128)(2,1)} %get-tuple-element.29), channel_id=1, source_target_pairs={{4,0},{8,4},{12,8},{20,16},{24,20},{28,24},{36,32},{40,36},{44,40}... | collective-permute-start | bytes 3145736 | tf_op jit(solution)/shard_map/ppermute | solution.py:110
  154.3 42.1 %collective-permute-start.11 = (bf16[256,2048]{1,0:T(8,128)(2,1)}, bf16[256,2048]{1,0:T(8,128)(2,1)}, u32[]{:S(2)}, u32[]{:S(2)}) collective-permute-start(bf16[256,2048]{1,0:T(8,128)(2,1)} %get-tuple-element.24), channel_id=1, source_target_pairs={{16,28},{32,44},{48,60},{64,76},{80,92},{96,108},{112,124},{17,29}... | collective-permute-start | bytes 3145736 | tf_op jit(solution)/shard_map/ppermute | solution.py:110
  169.8 1.0 copy-start.5
  170.8 23.0 %copy-start.7 = (bf16[256,2048]{1,0:T(8,128)(2,1)S(1)}, bf16[256,2048]{1,0:T(8,128)(2,1)}, u32[]{:S(2)}) copy-start(bf16[256,2048]{1,0:T(8,128)(2,1)} %get-tuple-element.30) | copy-start | bytes 3145732
  185.1 11.4 %copy-start.9 = (bf16[256,2048]{1,0:T(8,128)(2,1)S(1)}, bf16[256,2048]{1,0:T(8,128)(2,1)}, u32[]{:S(2)}) copy-start(bf16[256,2048]{1,0:T(8,128)(2,1)} %get-tuple-element.24) | copy-start | bytes 3145732
  185.1 13.5 %copy-start.6 = (bf16[256,2048]{1,0:T(8,128)(2,1)S(1)}, bf16[256,2048]{1,0:T(8,128)(2,1)}, u32[]{:S(2)}) copy-start(bf16[256,2048]{1,0:T(8,128)(2,1)} %get-tuple-element.25) | copy-start | bytes 3145732
  185.1 49.7 %collective-permute-start.19 = (bf16[256,2048]{1,0:T(8,128)(2,1)}, bf16[256,2048]{1,0:T(8,128)(2,1)S(1)}, u32[]{:S(2)}, u32[]{:S(2)}) collective-permute-start(bf16[256,2048]{1,0:T(8,128)(2,1)} %get-tuple-element.32), channel_id=1, source_target_pairs={{12,0},{16,4},{20,8},{24,12},{28,16},{32,20},{36,24},{40,28},{44,3... | collective-permute-start | bytes 3145736 | tf_op jit(solution)/shard_map/ppermute | solution.py:26
  191.4 48.6 %collective-permute-start.18 = (bf16[256,2048]{1,0:T(8,128)(2,1)}, bf16[256,2048]{1,0:T(8,128)(2,1)S(1)}, u32[]{:S(2)}, u32[]{:S(2)}) collective-permute-start(bf16[256,2048]{1,0:T(8,128)(2,1)} %get-tuple-element.31), channel_id=1, source_target_pairs={{8,0},{12,4},{16,8},{20,12},{24,16},{28,20},{32,24},{36,28},{40,32... | collective-permute-start | bytes 3145736 | tf_op jit(solution)/shard_map/ppermute | solution.py:26
  193.8 41.0 %copy-start.11 = (bf16[256,2048]{1,0:T(8,128)(2,1)S(1)}, bf16[256,2048]{1,0:T(8,128)(2,1)}, u32[]{:S(2)}) copy-start(bf16[256,2048]{1,0:T(8,128)(2,1)} %get-tuple-element.27) | copy-start | bytes 3145732
  194.2 45.8 %copy-start.10 = (bf16[256,2048]{1,0:T(8,128)(2,1)S(1)}, bf16[256,2048]{1,0:T(8,128)(2,1)}, u32[]{:S(2)}) copy-start(bf16[256,2048]{1,0:T(8,128)(2,1)} %get-tuple-element.26) | copy-start | bytes 3145732
  194.2 109.9 %copy-start.1 = (f32[256,2048]{1,0:T(8,128)S(1)}, f32[256,2048]{1,0:T(8,128)}, u32[]{:S(2)}) copy-start(f32[256,2048]{1,0:T(8,128)} %get-tuple-element.28) | copy-start | bytes 6291460
  194.3 109.8 %collective-permute-start.17 = (bf16[256,2048]{1,0:T(8,128)(2,1)S(1)}, bf16[256,2048]{1,0:T(8,128)(2,1)S(1)}, u32[]{:S(2)}, u32[]{:S(2)}) collective-permute-start(bf16[256,2048]{1,0:T(8,128)(2,1)S(1)} %add_convert_fusion), channel_id=1, source_target_pairs={{16,0},{20,4},{24,8},{28,12},{32,16},{36,20},{40,24},{44,28},{48,3... | collective-permute-start | bytes 3145736 | tf_op jit(solution)/shard_map/ppermute | solution.py:26
  196.5 111.1 %collective-permute-start.10 = (bf16[256,2048]{1,0:T(8,128)(2,1)S(1)}, bf16[256,2048]{1,0:T(8,128)(2,1)S(1)}, u32[]{:S(2)}, u32[]{:S(2)}) collective-permute-start(bf16[256,2048]{1,0:T(8,128)(2,1)S(1)} %copy-done.9), channel_id=1, source_target_pairs={{4,0},{8,4},{12,8},{20,16},{24,20},{28,24},{36,32},{40,36},{44,40}... | collective-permute-start | bytes 3145736 | tf_op jit(solution)/shard_map/ppermute | solution.py:110
  234.8 72.7 %collective-permute-start.14 = (bf16[256,2048]{1,0:T(8,128)(2,1)S(1)}, bf16[256,2048]{1,0:T(8,128)(2,1)S(1)}, u32[]{:S(2)}, u32[]{:S(2)}) collective-permute-start(bf16[256,2048]{1,0:T(8,128)(2,1)S(1)} %copy-done.11), channel_id=1, source_target_pairs={{12,0},{16,4},{20,8},{24,12},{28,16},{32,20},{36,24},{40,28},{44,3... | collective-permute-start | bytes 3145736 | tf_op jit(solution)/shard_map/ppermute | solution.py:26
  240.1 67.5 %collective-permute-start.13 = (bf16[256,2048]{1,0:T(8,128)(2,1)S(1)}, bf16[256,2048]{1,0:T(8,128)(2,1)S(1)}, u32[]{:S(2)}, u32[]{:S(2)}) collective-permute-start(bf16[256,2048]{1,0:T(8,128)(2,1)S(1)} %copy-done.10), channel_id=1, source_target_pairs={{8,0},{12,4},{16,8},{20,12},{24,16},{28,20},{32,24},{36,28},{40,32... | collective-permute-start | bytes 3145736 | tf_op jit(solution)/shard_map/ppermute | solution.py:26
  242.0 84.6 %collective-permute-start.12 = (bf16[256,2048]{1,0:T(8,128)(2,1)S(1)}, bf16[256,2048]{1,0:T(8,128)(2,1)S(1)}, u32[]{:S(2)}, u32[]{:S(2)}) collective-permute-start(bf16[256,2048]{1,0:T(8,128)(2,1)S(1)} %add_convert_fusion.1), channel_id=1, source_target_pairs={{16,0},{20,4},{24,8},{28,12},{32,16},{36,20},{40,24},{44,28},{48,3... | collective-permute-start | bytes 3145736 | tf_op jit(solution)/shard_map/ppermute | solution.py:26
  304.1 22.5 %copy-start = (f32[256,2048]{1,0:T(8,128)S(1)}, f32[256,2048]{1,0:T(8,128)}, u32[]{:S(2)}) copy-start(f32[256,2048]{1,0:T(8,128)} %get-tuple-element.23) | copy-start | bytes 6291460

commit v2 on v1

--- a/solution.py
+++ b/solution.py
@@ -36,8 +36,8 @@
     qs = sc_ref[0]
     ks = sc_ref[1]
     vc = sc_ref[2]
-    i = lax.broadcasted_iota(jnp.int32, (rows, cols), 0) + qs
-    j = lax.broadcasted_iota(jnp.int32, (rows, cols), 1) + ks
+    j = lax.broadcasted_iota(jnp.int32, (cols, rows), 0) + ks
+    i = lax.broadcasted_iota(jnp.int32, (cols, rows), 1) + qs
     live = (j <= i) & (i - j < WINDOW) & (j >= 0) & (i < vc) & (j < vc)
     nt = (((1,), (1,)), ((), ()))
     tn = (((0,), (0,)), ((), ()))
@@ -52,16 +52,16 @@
             sl = slice(hq * HEAD_SIZE, (hq + 1) * HEAD_SIZE)
             q = q_ref[:, sl]
             do = do_ref[:, sl]
-            lse = lse_ref[c, :, g : g + 1]
-            dl = dl_ref[c, :, g : g + 1]
-            s = lax.dot_general(q, k, nt, preferred_element_type=jnp.float32) * score_scale
+            lse = lse_ref[c, g : g + 1, :]
+            dl = dl_ref[c, g : g + 1, :]
+            s = lax.dot_general(k, q, nt, preferred_element_type=jnp.float32) * score_scale
             p = jnp.where(live, jnp.exp(s - lse), 0.0)
-            dp = lax.dot_general(do, v, nt, preferred_element_type=jnp.float32)
+            dp = lax.dot_general(v, do, nt, preferred_element_type=jnp.float32)
             ds = (p * (dp - dl)).astype(jnp.bfloat16)
             pb = p.astype(jnp.bfloat16)
-            dv = dv + lax.dot_general(pb, do, tn, preferred_element_type=jnp.float32)
-            dk = dk + lax.dot_general(ds, q, tn, preferred_element_type=jnp.float32)
-            dq = jnp.dot(ds, k, preferred_element_type=jnp.float32) * score_scale
+            dv = dv + jnp.dot(pb, do, preferred_element_type=jnp.float32)
+            dk = dk + jnp.dot(ds, q, preferred_element_type=jnp.float32)
+            dq = lax.dot_general(ds, k, tn, preferred_element_type=jnp.float32) * score_scale
             if accumulate:
                 dq = dq + dq_in_ref[:, sl]
             dq_ref[:, sl] = dq
@@ -77,7 +77,7 @@
     heads = HEADS_PER_STEP
     qspec = pl.BlockSpec((rows, heads * group * HEAD_SIZE), lambda h, sc: (0, h))
     kspec = pl.BlockSpec((cols, heads * HEAD_SIZE), lambda h, sc: (0, h))
-    sspec = pl.BlockSpec((heads, rows, group), lambda h, sc: (h, 0, 0))
+    sspec = pl.BlockSpec((heads, group, rows), lambda h, sc: (h, 0, 0))
     in_specs = [qspec, qspec, kspec, kspec, sspec, sspec]
     args = [q, do, k, v, lse3, dl3]
     if accumulate:
@@ -140,8 +140,8 @@
         ),
         -1,
     )
-    dl3 = delta.reshape(tokens_here, KEY_VALUE_HEADS, group).transpose(1, 0, 2)
-    lse3 = score_logsumexp.T.reshape(tokens_here, KEY_VALUE_HEADS, group).transpose(1, 0, 2)
+    dl3 = delta.T.reshape(KEY_VALUE_HEADS, group, tokens_here)
+    lse3 = score_logsumexp.reshape(KEY_VALUE_HEADS, group, tokens_here)
     qstart = shard * tokens_here
 
     def scalars_for(distance):

time: 333 us -> 330 us (level)
  waiting for transfers between devices: 169 us -> 176 us
    ppermute x8, waiting for transfers between devices: 18.4 us -> 41 us  [sent_by(): return lax.ppermute(x, axis, pairs)]
    ppermute x12, waiting for transfers between devices: 150 us -> 135 us  [passed_along(): return lax.ppermute(x, axis, pairs)]
  transfers between devices with their start and end apart: 20 -> 20, of which waited for: 6 -> 7; matrix products, arithmetic and copies ran while one was open for 8% -> 7% of each run, Pallas kernels for 22% -> 22%
where the time goes in v2:
time: 330 us; the launch traced here: 327 us
  waiting for transfers between devices  176 us (53%)
  Pallas kernels  70.4 us (21%)
  starting transfers between devices  54.3 us (16%)
  other arithmetic  19.8 us (6%)
  local copies, waits for them, and re-layouts  5.08 us (2%)
    ppermute x12, waiting for transfers between devices, passed_along(): return lax.ppermute(x, axis, pairs)  135 us
    pallas_call x5, Pallas kernels, pair_grads(): pl.pallas_call(functools.partial(pair_kernel, group, heads, accumulate),...  70.4 us
    ppermute x8, waiting for transfers between devices, sent_by(): return lax.ppermute(x, axis, pairs)  41 us
    ppermute x12, starting transfers between devices, passed_along(): return lax.ppermute(x, axis, pairs)  40.1 us
    ppermute x8, starting transfers between devices, sent_by(): return lax.ppermute(x, axis, pairs)  14.2 us
  transfers between devices with their start and end apart: 20, of which 7 were waited for; matrix products, arithmetic and copies ran while one was open for 7% of the time, Pallas kernels for 22%

profile of v2, /device:TPU:31, one launch (start us, length us, event | category | flops | bytes accessed | tf_op | source)
XLA Modules:
  0.0 326.9 jit_solution(9790378251126485288)
XLA Ops:
  0.6 3.7 %collective-permute-start.4 = (bf16[256,2048]{1,0:T(8,128)(2,1)}, bf16[256,2048]{1,0:T(8,128)(2,1)}, u32[]{:S(2)}, u32[]{:S(2)}) collective-permute-start(bf16[256,2048]{1,0:T(8,128)(2,1)} %k_ref.1), channel_id=1, source_target_pairs={{0,16},{4,20},{8,24},{12,28},{16,32},{20,36},{24,40},{28,44},{32,4... | collective-permute-start | bytes 3145736 | tf_op jit(solution)/shard_map/ppermute | solution.py:26
  4.4 2.9 collective-permute-start.5
  7.3 1.3 collective-permute-start.6
  8.6 18.3 %collective-permute-done.4.k_ref = bf16[256,2048]{1,0:T(8,128)(2,1)} collective-permute-done((bf16[256,2048]{1,0:T(8,128)(2,1)}, bf16[256,2048]{1,0:T(8,128)(2,1)}, u32[]{:S(2)}, u32[]{:S(2)}) %collective-permute-start.4) | collective-permute-done | bytes 1048608 | tf_op jit(solution)/shard_map/ppermute | solution.py:26
  26.9 3.1 collective-permute-start.7
  30.0 1.3 collective-permute-start.8
  31.3 18.1 %collective-permute-done.5.v_ref = bf16[256,2048]{1,0:T(8,128)(2,1)} collective-permute-done((bf16[256,2048]{1,0:T(8,128)(2,1)}, bf16[256,2048]{1,0:T(8,128)(2,1)}, u32[]{:S(2)}, u32[]{:S(2)}) %collective-permute-start.5) | collective-permute-done | bytes 1048608 | tf_op jit(solution)/shard_map/ppermute | solution.py:26
  49.4 2.2 collective-permute-start.9
  51.5 4.0 %collective-permute-start.2 = (bf16[256,2048]{1,0:T(8,128)(2,1)}, bf16[256,2048]{1,0:T(8,128)(2,1)}, u32[]{:S(2)}, u32[]{:S(2)}) collective-permute-start(bf16[256,2048]{1,0:T(8,128)(2,1)} %k_ref.1), channel_id=1, source_target_pairs={{0,8},{4,12},{8,16},{12,20},{16,24},{20,28},{24,32},{28,36},{32,40... | collective-permute-start | bytes 3145736 | tf_op jit(solution)/shard_map/ppermute | solution.py:26
  56.2 2.9 multiply_bitcast_fusion
  59.2 2.8 copy.15
  61.9 3.3 %reduce_sum.9 = f32[256,32]{1,0:T(8,128)S(1)} reduce(f32[256,32,128]{2,1,0:T(8,128)} %bitcast.9, f32[]{:T(128)} %constant.17.clone.1), dimensions={2}, to_apply=%region_0.0 | reduce | flops 1040384 | bytes 4227076 | tf_op jit(solution)/shard_map/reduce_sum | solution.py:137
  65.3 0.6 reshape.17.dl_ref
  66.0 0.6 reshape.15.lse_ref
  66.6 0.6 add_add_fusion.4.sc_ref
  67.2 0.6 add_add_fusion.3.sc_ref
  67.8 5.2 %collective-permute-start.3 = (bf16[256,2048]{1,0:T(8,128)(2,1)}, bf16[256,2048]{1,0:T(8,128)(2,1)}, u32[]{:S(2)}, u32[]{:S(2)}) collective-permute-start(bf16[256,2048]{1,0:T(8,128)(2,1)} %v_ref.1), channel_id=1, source_target_pairs={{0,8},{4,12},{8,16},{12,20},{16,24},{20,28},{24,32},{28,36},{32,40... | collective-permute-start | bytes 3145736 | tf_op jit(solution)/shard_map/ppermute | solution.py:26
  73.0 14.0 %shard_map.94 = (f32[256,4096]{1,0:T(8,128)}, f32[256,2048]{1,0:T(8,128)}, f32[256,2048]{1,0:T(8,128)}) custom-call(s32[3]{0:T(128)} %add_add_fusion.4.sc_ref, bf16[256,4096]{1,0:T(8,128)(2,1)} %q_ref.9, bf16[256,4096]{1,0:T(8,128)(2,1)} %do_ref.9, bf16[256,2048]{1,0:T(8,128)(2,1)} %k_ref.1, bf16[256,2048]{1,0:T(8,128)(2,1)} %v_ref.1, ...), custom_call_target="tpu_custom_call" | custom-call | flops 2684354560 | bytes 18874368 | tf_op jit(solution)/shard_map/pallas_call | solution.py:93
  87.0 1.9 collective-permute-start
  89.0 2.7 add.40.k_ref
  91.7 3.5 %collective-permute-start.1 = (bf16[256,2048]{1,0:T(8,128)(2,1)}, bf16[256,2048]{1,0:T(8,128)(2,1)S(1)}, u32[]{:S(2)}, u32[]{:S(2)}) collective-permute-start(bf16[256,2048]{1,0:T(8,128)(2,1)} %v_ref.1), channel_id=1, source_target_pairs={{0,12},{4,16},{8,20},{12,24},{16,28},{20,32},{24,36},{28,40},{32,4... | collective-permute-start | bytes 3145736 | tf_op jit(solution)/shard_map/ppermute | solution.py:26
  95.2 22.5 %collective-permute-done.9 = bf16[256,2048]{1,0:T(8,128)(2,1)S(1)} collective-permute-done((bf16[256,2048]{1,0:T(8,128)(2,1)}, bf16[256,2048]{1,0:T(8,128)(2,1)S(1)}, u32[]{:S(2)}, u32[]{:S(2)}) %collective-permute-start.9) | collective-permute-done | bytes 1048608 | tf_op jit(solution)/shard_map/ppermute | solution.py:110
  117.7 1.4 add.41.v_ref
  119.1 14.1 %shard_map.95 = (f32[256,4096]{1,0:T(8,128)}, bf16[256,2048]{1,0:T(8,128)(2,1)}, bf16[256,2048]{1,0:T(8,128)(2,1)}) custom-call(s32[3]{0:T(128)} %add_add_fusion.3.sc_ref, bf16[256,4096]{1,0:T(8,128)(2,1)} %q_ref.9, bf16[256,4096]{1,0:T(8,128)(2,1)} %do_ref.9, bf16[256,2048]{1,0:T(8,128)(2,1)} %add.40.k_ref, ...), custom_call_target="tpu_custom_call", output_to_operand_aliasing={{0}: (7, {})} | custom-call | flops 2684354560 | bytes 18874368 | tf_op jit(solution)/shard_map/pallas_call | solution.py:93
  133.2 1.3 collective-permute-start.16
  134.5 0.7 add_add_fusion.2.sc_ref
  135.1 0.6 add_add_fusion.1.sc_ref
  135.7 0.6 add_add_fusion.sc_ref
  136.3 14.1 %shard_map.96 = (f32[256,4096]{1,0:T(8,128)}, bf16[256,2048]{1,0:T(8,128)(2,1)}, bf16[256,2048]{1,0:T(8,128)(2,1)}) custom-call(s32[3]{0:T(128)} %add_add_fusion.2.sc_ref, bf16[256,4096]{1,0:T(8,128)(2,1)} %q_ref.9, bf16[256,4096]{1,0:T(8,128)(2,1)} %do_ref.9, bf16[256,2048]{1,0:T(8,128)(2,1)} %collective-permute-done.4.k_ref, ...), custom_call_target="tpu_custom_call", output_to_operand_aliasing={{0}: (7, {})} | custom-call | flops 2684354560 | bytes 18874368 | tf_op jit(solution)/shard_map/pallas_call | solution.py:93
  150.3 2.3 collective-permute-start.15
  152.6 1.5 collective-permute-start.11
  154.1 14.1 %shard_map.97 = (f32[256,4096]{1,0:T(8,128)}, bf16[256,2048]{1,0:T(8,128)(2,1)}, bf16[256,2048]{1,0:T(8,128)(2,1)}) custom-call(s32[3]{0:T(128)} %add_add_fusion.1.sc_ref, bf16[256,4096]{1,0:T(8,128)(2,1)} %q_ref.9, bf16[256,4096]{1,0:T(8,128)(2,1)} %do_ref.9, bf16[256,2048]{1,0:T(8,128)(2,1)} %collective-permute-done.2.k_ref, ...), custom_call_target="tpu_custom_call", output_to_operand_aliasing={{0}: (7, {})} | custom-call | flops 2684354560 | bytes 18874368 | tf_op jit(solution)/shard_map/pallas_call | solution.py:93
  168.2 1.0 copy-done.4
  169.1 14.2 %shard_map.98 = (f32[256,4096]{1,0:T(8,128)}, bf16[256,2048]{1,0:T(8,128)(2,1)}, bf16[256,2048]{1,0:T(8,128)(2,1)}) custom-call(s32[3]{0:T(128)} %add_add_fusion.sc_ref, bf16[256,4096]{1,0:T(8,128)(2,1)} %q_ref.9, bf16[256,4096]{1,0:T(8,128)(2,1)} %do_ref.9, bf16[256,2048]{1,0:T(8,128)(2,1)} %collective-permute-done.k_ref, ...), custom_call_target="tpu_custom_call", output_to_operand_aliasing={{0}: (7, {})} | custom-call | flops 2684354560 | bytes 18874368 | tf_op jit(solution)/shard_map/pallas_call | solution.py:93
  183.3 5.4 %collective-permute-start.19 = (bf16[256,2048]{1,0:T(8,128)(2,1)}, bf16[256,2048]{1,0:T(8,128)(2,1)S(1)}, u32[]{:S(2)}, u32[]{:S(2)}) collective-permute-start(bf16[256,2048]{1,0:T(8,128)(2,1)} %get-tuple-element.32), channel_id=1, source_target_pairs={{12,0},{16,4},{20,8},{24,12},{28,16},{32,20},{36,24},{40,28},{44,3... | collective-permute-start | bytes 3145736 | tf_op jit(solution)/shard_map/ppermute | solution.py:26
  188.7 2.2 collective-permute-start.18
  191.4 2.2 collective-permute-start.17
  193.6 18.5 %collective-permute-done.11 = bf16[256,2048]{1,0:T(8,128)(2,1)S(1)} collective-permute-done((bf16[256,2048]{1,0:T(8,128)(2,1)}, bf16[256,2048]{1,0:T(8,128)(2,1)S(1)}, u32[]{:S(2)}, u32[]{:S(2)}) %collective-permute-start.11) | collective-permute-done | bytes 1048608 | tf_op jit(solution)/shard_map/ppermute | solution.py:110
  212.1 1.3 collective-permute-start.10
  213.4 0.4 add_convert_fusion.1
  213.8 18.3 %collective-permute-done.19 = bf16[256,2048]{1,0:T(8,128)(2,1)S(1)} collective-permute-done((bf16[256,2048]{1,0:T(8,128)(2,1)}, bf16[256,2048]{1,0:T(8,128)(2,1)S(1)}, u32[]{:S(2)}, u32[]{:S(2)}) %collective-permute-start.19) | collective-permute-done | bytes 1048608 | tf_op jit(solution)/shard_map/ppermute | solution.py:26
  232.1 5.2 %collective-permute-start.14 = (bf16[256,2048]{1,0:T(8,128)(2,1)S(1)}, bf16[256,2048]{1,0:T(8,128)(2,1)S(1)}, u32[]{:S(2)}, u32[]{:S(2)}) collective-permute-start(bf16[256,2048]{1,0:T(8,128)(2,1)S(1)} %copy-done.8), channel_id=1, source_target_pairs={{12,0},{16,4},{20,8},{24,12},{28,16},{32,20},{36,24},{40,28},{44,3... | collective-permute-start | bytes 3145736 | tf_op jit(solution)/shard_map/ppermute | solution.py:26
  237.4 1.9 collective-permute-start.13
  239.3 1.9 collective-permute-start.12
  241.2 61.1 %collective-permute-done.17 = bf16[256,2048]{1,0:T(8,128)(2,1)S(1)} collective-permute-done((bf16[256,2048]{1,0:T(8,128)(2,1)S(1)}, bf16[256,2048]{1,0:T(8,128)(2,1)S(1)}, u32[]{:S(2)}, u32[]{:S(2)}) %collective-permute-start.17) | collective-permute-done | bytes 1048608 | tf_op jit(solution)/shard_map/ppermute | solution.py:26
  302.3 3.4 %convert_add_fusion = f32[256,2048]{1,0:T(8,128)} fusion(bf16[256,2048]{1,0:T(8,128)(2,1)S(1)} %collective-permute-done.19, bf16[256,2048]{1,0:T(8,128)(2,1)S(1)} %collective-permute-done.18, bf16[256,2048]{1,0:T(8,128)(2,1)S(1)} %collective-permute-done.17, f32[256,2048]{1,0:T(8,128)S(1)} %copy-done.1, bf16[256,2048]{1,0:T(8,128)(2,1)} %collective-permute-done.15), kind=kLoop, calls=%fused_computation.1 | loop fusion | flops 4194304 | bytes 8388608 | tf_op jit(solution)/shard_map/add | solution.py:180
  305.8 19.0 %collective-permute-done.12 = bf16[256,2048]{1,0:T(8,128)(2,1)S(1)} collective-permute-done((bf16[256,2048]{1,0:T(8,128)(2,1)S(1)}, bf16[256,2048]{1,0:T(8,128)(2,1)S(1)}, u32[]{:S(2)}, u32[]{:S(2)}) %collective-permute-start.12) | collective-permute-done | bytes 1048608 | tf_op jit(solution)/shard_map/ppermute | solution.py:26
  324.8 2.1 convert_add_fusion.1
  (32 shorter events, 0.5 us)
Async XLA Ops:
  0.6 26.3 %collective-permute-start.4 = (bf16[256,2048]{1,0:T(8,128)(2,1)}, bf16[256,2048]{1,0:T(8,128)(2,1)}, u32[]{:S(2)}, u32[]{:S(2)}) collective-permute-start(bf16[256,2048]{1,0:T(8,128)(2,1)} %k_ref.1), channel_id=1, source_target_pairs={{0,16},{4,20},{8,24},{12,28},{16,32},{20,36},{24,40},{28,44},{32,4... | collective-permute-start | bytes 3145736 | tf_op jit(solution)/shard_map/ppermute | solution.py:26
  4.4 45.0 %collective-permute-start.5 = (bf16[256,2048]{1,0:T(8,128)(2,1)}, bf16[256,2048]{1,0:T(8,128)(2,1)}, u32[]{:S(2)}, u32[]{:S(2)}) collective-permute-start(bf16[256,2048]{1,0:T(8,128)(2,1)} %v_ref.1), channel_id=1, source_target_pairs={{0,16},{4,20},{8,24},{12,28},{16,32},{20,36},{24,40},{28,44},{32,4... | collective-permute-start | bytes 3145736 | tf_op jit(solution)/shard_map/ppermute | solution.py:26
  7.3 60.6 %collective-permute-start.6 = (bf16[256,2048]{1,0:T(8,128)(2,1)}, bf16[256,2048]{1,0:T(8,128)(2,1)S(1)}, u32[]{:S(2)}, u32[]{:S(2)}) collective-permute-start(bf16[256,2048]{1,0:T(8,128)(2,1)} %k_ref.1), channel_id=1, source_target_pairs={{0,4},{4,8},{8,12},{16,20},{20,24},{24,28},{32,36},{36,40},{40,44}... | collective-permute-start | bytes 3145736 | tf_op jit(solution)/shard_map/ppermute | solution.py:110
  26.9 60.1 %collective-permute-start.7 = (bf16[256,2048]{1,0:T(8,128)(2,1)}, bf16[256,2048]{1,0:T(8,128)(2,1)}, u32[]{:S(2)}, u32[]{:S(2)}) collective-permute-start(bf16[256,2048]{1,0:T(8,128)(2,1)} %collective-permute-done.4.k_ref), channel_id=1, source_target_pairs={{28,16},{44,32},{60,48},{76,64},{92,80},{108,96},{124,112},{29,17}... | collective-permute-start | bytes 3145736 | tf_op jit(solution)/shard_map/ppermute | solution.py:110
  30.0 61.7 %collective-permute-start.8 = (bf16[256,2048]{1,0:T(8,128)(2,1)}, bf16[256,2048]{1,0:T(8,128)(2,1)S(1)}, u32[]{:S(2)}, u32[]{:S(2)}) collective-permute-start(bf16[256,2048]{1,0:T(8,128)(2,1)} %v_ref.1), channel_id=1, source_target_pairs={{0,4},{4,8},{8,12},{16,20},{20,24},{24,28},{32,36},{36,40},{40,44}... | collective-permute-start | bytes 3145736 | tf_op jit(solution)/shard_map/ppermute | solution.py:110
  49.4 68.3 %collective-permute-start.9 = (bf16[256,2048]{1,0:T(8,128)(2,1)}, bf16[256,2048]{1,0:T(8,128)(2,1)S(1)}, u32[]{:S(2)}, u32[]{:S(2)}) collective-permute-start(bf16[256,2048]{1,0:T(8,128)(2,1)} %collective-permute-done.5.v_ref), channel_id=1, source_target_pairs={{28,16},{44,32},{60,48},{76,64},{92,80},{108,96},{124,112},{29,17}... | collective-permute-start | bytes 3145736 | tf_op jit(solution)/shard_map/ppermute | solution.py:110
  51.5 98.8 %collective-permute-start.2 = (bf16[256,2048]{1,0:T(8,128)(2,1)}, bf16[256,2048]{1,0:T(8,128)(2,1)}, u32[]{:S(2)}, u32[]{:S(2)}) collective-permute-start(bf16[256,2048]{1,0:T(8,128)(2,1)} %k_ref.1), channel_id=1, source_target_pairs={{0,8},{4,12},{8,16},{12,20},{16,24},{20,28},{24,32},{28,36},{32,40... | collective-permute-start | bytes 3145736 | tf_op jit(solution)/shard_map/ppermute | solution.py:26
  61.9 4.1 %copy-start.5 = (f32[32,256]{1,0:T(8,128)S(1)}, f32[32,256]{1,0:T(8,128)}, u32[]{:S(2)}) copy-start(f32[32,256]{1,0:T(8,128)} %param.12) | copy-start | bytes 98308
  67.8 84.7 %collective-permute-start.3 = (bf16[256,2048]{1,0:T(8,128)(2,1)}, bf16[256,2048]{1,0:T(8,128)(2,1)}, u32[]{:S(2)}, u32[]{:S(2)}) collective-permute-start(bf16[256,2048]{1,0:T(8,128)(2,1)} %v_ref.1), channel_id=1, source_target_pairs={{0,8},{4,12},{8,16},{12,20},{16,24},{20,28},{24,32},{28,36},{32,40... | collective-permute-start | bytes 3145736 | tf_op jit(solution)/shard_map/ppermute | solution.py:26
  87.0 81.1 %collective-permute-start = (bf16[256,2048]{1,0:T(8,128)(2,1)}, bf16[256,2048]{1,0:T(8,128)(2,1)}, u32[]{:S(2)}, u32[]{:S(2)}) collective-permute-start(bf16[256,2048]{1,0:T(8,128)(2,1)} %k_ref.1), channel_id=1, source_target_pairs={{0,12},{4,16},{8,20},{12,24},{16,28},{20,32},{24,36},{28,40},{32,4... | collective-permute-start | bytes 3145736 | tf_op jit(solution)/shard_map/ppermute | solution.py:26
  91.7 76.5 %collective-permute-start.1 = (bf16[256,2048]{1,0:T(8,128)(2,1)}, bf16[256,2048]{1,0:T(8,128)(2,1)S(1)}, u32[]{:S(2)}, u32[]{:S(2)}) collective-permute-start(bf16[256,2048]{1,0:T(8,128)(2,1)} %v_ref.1), channel_id=1, source_target_pairs={{0,12},{4,16},{8,20},{12,24},{16,28},{20,32},{24,36},{28,40},{32,4... | collective-permute-start | bytes 3145736 | tf_op jit(solution)/shard_map/ppermute | solution.py:26
  133.2 57.8 %collective-permute-start.16 = (bf16[256,2048]{1,0:T(8,128)(2,1)}, bf16[256,2048]{1,0:T(8,128)(2,1)S(1)}, u32[]{:S(2)}, u32[]{:S(2)}) collective-permute-start(bf16[256,2048]{1,0:T(8,128)(2,1)} %get-tuple-element.29), channel_id=1, source_target_pairs={{16,28},{32,44},{48,60},{64,76},{80,92},{96,108},{112,124},{17,29}... | collective-permute-start | bytes 3145736 | tf_op jit(solution)/shard_map/ppermute | solution.py:110
  150.3 89.0 %collective-permute-start.15 = (bf16[256,2048]{1,0:T(8,128)(2,1)}, bf16[256,2048]{1,0:T(8,128)(2,1)}, u32[]{:S(2)}, u32[]{:S(2)}) collective-permute-start(bf16[256,2048]{1,0:T(8,128)(2,1)} %get-tuple-element.29), channel_id=1, source_target_pairs={{4,0},{8,4},{12,8},{20,16},{24,20},{28,24},{36,32},{40,36},{44,40}... | collective-permute-start | bytes 3145736 | tf_op jit(solution)/shard_map/ppermute | solution.py:110
  152.6 59.5 %collective-permute-start.11 = (bf16[256,2048]{1,0:T(8,128)(2,1)}, bf16[256,2048]{1,0:T(8,128)(2,1)S(1)}, u32[]{:S(2)}, u32[]{:S(2)}) collective-permute-start(bf16[256,2048]{1,0:T(8,128)(2,1)} %get-tuple-element.24), channel_id=1, source_target_pairs={{16,28},{32,44},{48,60},{64,76},{80,92},{96,108},{112,124},{17,29}... | collective-permute-start | bytes 3145736 | tf_op jit(solution)/shard_map/ppermute | solution.py:110
  168.1 1.0 copy-start.4
  169.1 21.9 %copy-start.3 = (bf16[256,2048]{1,0:T(8,128)(2,1)S(1)}, bf16[256,2048]{1,0:T(8,128)(2,1)}, u32[]{:S(2)}) copy-start(bf16[256,2048]{1,0:T(8,128)(2,1)} %get-tuple-element.30) | copy-start | bytes 3145732
  183.3 28.7 %copy-start.6 = (bf16[256,2048]{1,0:T(8,128)(2,1)S(1)}, bf16[256,2048]{1,0:T(8,128)(2,1)}, u32[]{:S(2)}) copy-start(bf16[256,2048]{1,0:T(8,128)(2,1)} %get-tuple-element.24) | copy-start | bytes 3145732
  183.3 30.1 %copy-start.2 = (bf16[256,2048]{1,0:T(8,128)(2,1)S(1)}, bf16[256,2048]{1,0:T(8,128)(2,1)}, u32[]{:S(2)}) copy-start(bf16[256,2048]{1,0:T(8,128)(2,1)} %get-tuple-element.25) | copy-start | bytes 3145732
  183.3 48.8 %collective-permute-start.19 = (bf16[256,2048]{1,0:T(8,128)(2,1)}, bf16[256,2048]{1,0:T(8,128)(2,1)S(1)}, u32[]{:S(2)}, u32[]{:S(2)}) collective-permute-start(bf16[256,2048]{1,0:T(8,128)(2,1)} %get-tuple-element.32), channel_id=1, source_target_pairs={{12,0},{16,4},{20,8},{24,12},{28,16},{32,20},{36,24},{40,28},{44,3... | collective-permute-start | bytes 3145736 | tf_op jit(solution)/shard_map/ppermute | solution.py:26
  188.7 48.6 %collective-permute-start.18 = (bf16[256,2048]{1,0:T(8,128)(2,1)}, bf16[256,2048]{1,0:T(8,128)(2,1)S(1)}, u32[]{:S(2)}, u32[]{:S(2)}) collective-permute-start(bf16[256,2048]{1,0:T(8,128)(2,1)} %get-tuple-element.31), channel_id=1, source_target_pairs={{8,0},{12,4},{16,8},{20,12},{24,16},{28,20},{32,24},{36,28},{40,32... | collective-permute-start | bytes 3145736 | tf_op jit(solution)/shard_map/ppermute | solution.py:26
  191.0 41.2 %copy-start.8 = (bf16[256,2048]{1,0:T(8,128)(2,1)S(1)}, bf16[256,2048]{1,0:T(8,128)(2,1)}, u32[]{:S(2)}) copy-start(bf16[256,2048]{1,0:T(8,128)(2,1)} %get-tuple-element.27) | copy-start | bytes 3145732
  191.4 46.0 %copy-start.7 = (bf16[256,2048]{1,0:T(8,128)(2,1)S(1)}, bf16[256,2048]{1,0:T(8,128)(2,1)}, u32[]{:S(2)}) copy-start(bf16[256,2048]{1,0:T(8,128)(2,1)} %get-tuple-element.26) | copy-start | bytes 3145732
  191.4 110.9 %copy-start.1 = (f32[256,2048]{1,0:T(8,128)S(1)}, f32[256,2048]{1,0:T(8,128)}, u32[]{:S(2)}) copy-start(f32[256,2048]{1,0:T(8,128)} %get-tuple-element.28) | copy-start | bytes 6291460
  191.4 110.9 %collective-permute-start.17 = (bf16[256,2048]{1,0:T(8,128)(2,1)S(1)}, bf16[256,2048]{1,0:T(8,128)(2,1)S(1)}, u32[]{:S(2)}, u32[]{:S(2)}) collective-permute-start(bf16[256,2048]{1,0:T(8,128)(2,1)S(1)} %add_convert_fusion), channel_id=1, source_target_pairs={{16,0},{20,4},{24,8},{28,12},{32,16},{36,20},{40,24},{44,28},{48,3... | collective-permute-start | bytes 3145736 | tf_op jit(solution)/shard_map/ppermute | solution.py:26
  212.1 93.7 %collective-permute-start.10 = (bf16[256,2048]{1,0:T(8,128)(2,1)S(1)}, bf16[256,2048]{1,0:T(8,128)(2,1)S(1)}, u32[]{:S(2)}, u32[]{:S(2)}) collective-permute-start(bf16[256,2048]{1,0:T(8,128)(2,1)S(1)} %copy-done.6), channel_id=1, source_target_pairs={{4,0},{8,4},{12,8},{20,16},{24,20},{28,24},{36,32},{40,36},{44,40}... | collective-permute-start | bytes 3145736 | tf_op jit(solution)/shard_map/ppermute | solution.py:110
  232.1 73.6 %collective-permute-start.14 = (bf16[256,2048]{1,0:T(8,128)(2,1)S(1)}, bf16[256,2048]{1,0:T(8,128)(2,1)S(1)}, u32[]{:S(2)}, u32[]{:S(2)}) collective-permute-start(bf16[256,2048]{1,0:T(8,128)(2,1)S(1)} %copy-done.8), channel_id=1, source_target_pairs={{12,0},{16,4},{20,8},{24,12},{28,16},{32,20},{36,24},{40,28},{44,3... | collective-permute-start | bytes 3145736 | tf_op jit(solution)/shard_map/ppermute | solution.py:26
  237.4 68.4 %collective-permute-start.13 = (bf16[256,2048]{1,0:T(8,128)(2,1)S(1)}, bf16[256,2048]{1,0:T(8,128)(2,1)S(1)}, u32[]{:S(2)}, u32[]{:S(2)}) collective-permute-start(bf16[256,2048]{1,0:T(8,128)(2,1)S(1)} %copy-done.7), channel_id=1, source_target_pairs={{8,0},{12,4},{16,8},{20,12},{24,16},{28,20},{32,24},{36,28},{40,32... | collective-permute-start | bytes 3145736 | tf_op jit(solution)/shard_map/ppermute | solution.py:26
  239.3 85.5 %collective-permute-start.12 = (bf16[256,2048]{1,0:T(8,128)(2,1)S(1)}, bf16[256,2048]{1,0:T(8,128)(2,1)S(1)}, u32[]{:S(2)}, u32[]{:S(2)}) collective-permute-start(bf16[256,2048]{1,0:T(8,128)(2,1)S(1)} %add_convert_fusion.1), channel_id=1, source_target_pairs={{16,0},{20,4},{24,8},{28,12},{32,16},{36,20},{40,24},{44,28},{48,3... | collective-permute-start | bytes 3145736 | tf_op jit(solution)/shard_map/ppermute | solution.py:26
  302.3 22.5 %copy-start = (f32[256,2048]{1,0:T(8,128)S(1)}, f32[256,2048]{1,0:T(8,128)}, u32[]{:S(2)}) copy-start(f32[256,2048]{1,0:T(8,128)} %get-tuple-element.23) | copy-start | bytes 6291460

commit v3 on v2

--- a/solution.py
+++ b/solution.py
@@ -14,7 +14,7 @@
 WINDOW = 1024
 HEADS_PER_STEP = 4
 ROW_DEVICES = 4
-PAIR_ORDER = (1, 4, 2, 3)
+PAIR_ORDER = (4, 1, 2, 3)
 
 
 score_scale = 168.0 ** (-0.5)
@@ -126,12 +126,15 @@
     shard = lax.axis_index("seq")
     row = ROW_DEVICES
     kv = (stored_keys, stored_values)
+    assert blocks == row
     far = passed_along(kv, "seq", blocks)
-    near = sent_by(kv, "seq", [(i, i + 1) for i in range(count - 1) if i % row != row - 1])
-    handed = sent_by(far, "seq", [(i, i - row + 1) for i in range(row, count) if i % row == row - 1])
-    halos = {blocks: far, 1: (near[0] + handed[0], near[1] + handed[1])}
-    for distance in range(2, blocks):
-        halos[distance] = passed_along(kv, "seq", distance)
+    halos = {blocks: far}
+    for distance in range(1, blocks):
+        direct = sent_by(
+            kv, "seq", [(i, i + distance) for i in range(count) if i % row + distance < row]
+        )
+        relayed = sent_by(far, "seq", [(i, i - row + distance) for i in range(row, count) if i % row >= row - distance])
+        halos[distance] = (direct[0] + relayed[0], direct[1] + relayed[1])
     limit = valid_count[0]
 
     delta = jnp.sum(
@@ -150,7 +153,8 @@
     dq, key_grad, value_grad = pair_grads(
         scalars_for(0), queries, output_cotangent, stored_keys, stored_values, lse3, dl3, None, jnp.float32
     )
-    handed_back = None
+    merged = []
+    far_part = None
     for distance in PAIR_ORDER:
         k_far, v_far = halos[distance]
         dq, dk_part, dv_part = pair_grads(
@@ -164,20 +168,23 @@
             dq,
             jnp.bfloat16,
         )
-        if distance == 1:
-            arrived = sent_by(
-                (dk_part, dv_part), "seq", [(i, i - 1) for i in range(1, count) if i % row != 0]
-            )
-            handed_back = sent_by(
-                (dk_part, dv_part), "seq", [(i, i + row - 1) for i in range(row, count) if i % row == 0]
-            )
-        else:
-            if distance == blocks:
-                dk_part = (dk_part.astype(jnp.float32) + handed_back[0].astype(jnp.float32)).astype(jnp.bfloat16)
-                dv_part = (dv_part.astype(jnp.float32) + handed_back[1].astype(jnp.float32)).astype(jnp.bfloat16)
-            arrived = passed_along((dk_part, dv_part), "seq", -distance)
+        if distance == blocks:
+            far_part = (dk_part, dv_part)
+            continue
+        arrived = sent_by((dk_part, dv_part), "seq", [(i, i - distance) for i in range(count) if i % row >= distance])
+        merged.append(
+            sent_by((dk_part, dv_part), "seq", [(i, i + row - distance) for i in range(count) if i % row < distance])
+        )
         key_grad = key_grad + arrived[0].astype(jnp.float32)
         value_grad = value_grad + arrived[1].astype(jnp.float32)
+    dk_far = far_part[0].astype(jnp.float32)
+    dv_far = far_part[1].astype(jnp.float32)
+    for part in merged:
+        dk_far = dk_far + part[0].astype(jnp.float32)
+        dv_far = dv_far + part[1].astype(jnp.float32)
+    arrived = passed_along((dk_far.astype(jnp.bfloat16), dv_far.astype(jnp.bfloat16)), "seq", -blocks)
+    key_grad = key_grad + arrived[0].astype(jnp.float32)
+    value_grad = value_grad + arrived[1].astype(jnp.float32)
     return (dq, key_grad, value_grad)
 
 

time: 330 us -> 415 us (1.26)
  waiting for transfers between devices: 176 us -> 219 us
  starting transfers between devices: 54.3 us -> 82.2 us
  other arithmetic: 19.8 us -> 31.6 us
    ppermute x8 -> x24, waiting for transfers between devices: 41 us -> 182 us  [sent_by(): return lax.ppermute(x, axis, pairs)]
    ppermute x12 -> x4, waiting for transfers between devices: 135 us -> 36.9 us  [passed_along(): return lax.ppermute(x, axis, pairs)]
    ppermute x8 -> x24, starting transfers between devices: 14.2 us -> 71.7 us  [sent_by(): return lax.ppermute(x, axis, pairs)]
    ppermute x12 -> x4, starting transfers between devices: 40.1 us -> 10.5 us  [passed_along(): return lax.ppermute(x, axis, pairs)]
    add x2 -> x6, other arithmetic: 4.12 us -> 16.6 us  [local(): halos[distance] = (direct[0] + relayed[0], direct[1] + relayed[1])]
  transfers between devices with their start and end apart: 20 -> 28, of which waited for: 7 -> 13; matrix products, arithmetic and copies ran while one was open for 7% -> 7% of each run, Pallas kernels for 22% -> 14%
where the time goes in v3:
time: 415 us; the launch traced here: 410 us
  waiting for transfers between devices  219 us (53%)
  starting transfers between devices  82.2 us (20%)
  Pallas kernels  70.7 us (17%)
  other arithmetic  31.6 us (8%)
    ppermute x24, waiting for transfers between devices, sent_by(): return lax.ppermute(x, axis, pairs)  182 us
    ppermute x24, starting transfers between devices, sent_by(): return lax.ppermute(x, axis, pairs)  71.7 us
    pallas_call x5, Pallas kernels, pair_grads(): pl.pallas_call(functools.partial(pair_kernel, group, heads, accumulate),...  70.7 us
    ppermute x4, waiting for transfers between devices, passed_along(): return lax.ppermute(x, axis, pairs)  36.9 us
    add x6, other arithmetic, local(): halos[distance] = (direct[0] + relayed[0], direct[1] + relayed[1])  16.6 us
    ppermute x4, starting transfers between devices, passed_along(): return lax.ppermute(x, axis, pairs)  10.5 us
  transfers between devices with their start and end apart: 28, of which 13 were waited for; matrix products, arithmetic and copies ran while one was open for 7% of the time, Pallas kernels for 14%

profile of v3, /device:TPU:31, one launch (start us, length us, event | category | flops | bytes accessed | tf_op | source)
XLA Modules:
  0.0 409.6 jit_solution(12264294826961247022)
XLA Ops:
  0.6 3.7 collective-permute-start.1
  4.4 2.9 collective-permute-start.4
  7.3 1.3 collective-permute-start.10
  8.6 1.3 collective-permute-start.12
  9.9 1.3 collective-permute-start.6
  11.2 15.7 %collective-permute-done.1.k_ref = bf16[256,2048]{1,0:T(8,128)(2,1)} collective-permute-done((bf16[256,2048]{1,0:T(8,128)(2,1)}, bf16[256,2048]{1,0:T(8,128)(2,1)}, u32[]{:S(2)}, u32[]{:S(2)}) %collective-permute-start.1) | collective-permute-done | bytes 1048608 | tf_op jit(solution)/shard_map/ppermute | solution.py:26
  28.2 21.2 %collective-permute-done.4.v_ref = bf16[256,2048]{1,0:T(8,128)(2,1)} collective-permute-done((bf16[256,2048]{1,0:T(8,128)(2,1)}, bf16[256,2048]{1,0:T(8,128)(2,1)}, u32[]{:S(2)}, u32[]{:S(2)}) %collective-permute-start.4) | collective-permute-done | bytes 1048608 | tf_op jit(solution)/shard_map/ppermute | solution.py:26
  49.4 3.1 collective-permute-start.11
  52.5 2.3 collective-permute-start.13
  55.5 4.0 collective-permute-start.7
  63.9 2.3 collective-permute-start.9
  66.2 29.0 %collective-permute-done.11 = bf16[256,2048]{1,0:T(8,128)(2,1)} collective-permute-done((bf16[256,2048]{1,0:T(8,128)(2,1)}, bf16[256,2048]{1,0:T(8,128)(2,1)}, u32[]{:S(2)}, u32[]{:S(2)}) %collective-permute-start.11) | collective-permute-done | bytes 1048608 | tf_op jit(solution)/shard_map/ppermute | solution.py:110
  95.2 10.9 %collective-permute-start.2 = (bf16[256,2048]{1,0:T(8,128)(2,1)}, bf16[256,2048]{1,0:T(8,128)(2,1)}, u32[]{:S(2)}, u32[]{:S(2)}) collective-permute-start(bf16[256,2048]{1,0:T(8,128)(2,1)} %collective-permute-done.1.k_ref), channel_id=1, source_target_pairs={{20,16},{24,20},{28,24},{36,32},{40,36},{44,40},{52,48},{56,52},{6... | collective-permute-start | bytes 3145736 | tf_op jit(solution)/shard_map/ppermute | solution.py:110
  106.1 2.9 multiply_bitcast_fusion
  109.0 31.1 %collective-permute-done.13 = bf16[256,2048]{1,0:T(8,128)(2,1)} collective-permute-done((bf16[256,2048]{1,0:T(8,128)(2,1)}, bf16[256,2048]{1,0:T(8,128)(2,1)}, u32[]{:S(2)}, u32[]{:S(2)}) %collective-permute-start.13) | collective-permute-done | bytes 1048608 | tf_op jit(solution)/shard_map/ppermute | solution.py:110
  141.5 2.3 collective-permute-start.5
  144.4 2.7 copy.15
  147.1 3.3 reduce_sum.9
  151.8 14.1 %shard_map.94 = (f32[256,4096]{1,0:T(8,128)}, f32[256,2048]{1,0:T(8,128)}, f32[256,2048]{1,0:T(8,128)}) custom-call(s32[3]{0:T(128)} %add_add_fusion.4.sc_ref, bf16[256,4096]{1,0:T(8,128)(2,1)} %q_ref.9, bf16[256,4096]{1,0:T(8,128)(2,1)} %do_ref.9, bf16[256,2048]{1,0:T(8,128)(2,1)} %k_ref.1, bf16[256,2048]{1,0:T(8,128)(2,1)} %v_ref.1, ...), custom_call_target="tpu_custom_call" | custom-call | flops 2684354560 | bytes 18874368 | tf_op jit(solution)/shard_map/pallas_call | solution.py:93
  166.0 14.1 %shard_map.95 = (f32[256,4096]{1,0:T(8,128)}, bf16[256,2048]{1,0:T(8,128)(2,1)}, bf16[256,2048]{1,0:T(8,128)(2,1)}) custom-call(s32[3]{0:T(128)} %add_add_fusion.3.sc_ref, bf16[256,4096]{1,0:T(8,128)(2,1)} %q_ref.9, bf16[256,4096]{1,0:T(8,128)(2,1)} %do_ref.9, bf16[256,2048]{1,0:T(8,128)(2,1)} %collective-permute-done.1.k_ref, ...), custom_call_target="tpu_custom_call", output_to_operand_aliasing={{0}: (7, {})} | custom-call | flops 2684354560 | bytes 18874368 | tf_op jit(solution)/shard_map/pallas_call | solution.py:93
  180.0 2.6 add.68.k_ref
  182.6 2.6 add.69.v_ref
  185.2 2.6 add.66.k_ref
  187.8 2.9 add.67.v_ref
  190.8 2.9 add.64.k_ref
  193.7 14.1 %shard_map.96 = (f32[256,4096]{1,0:T(8,128)}, bf16[256,2048]{1,0:T(8,128)(2,1)}, bf16[256,2048]{1,0:T(8,128)(2,1)}) custom-call(s32[3]{0:T(128)} %add_add_fusion.2.sc_ref, bf16[256,4096]{1,0:T(8,128)(2,1)} %q_ref.9, bf16[256,4096]{1,0:T(8,128)(2,1)} %do_ref.9, bf16[256,2048]{1,0:T(8,128)(2,1)} %add.68.k_ref, ...), custom_call_target="tpu_custom_call", output_to_operand_aliasing={{0}: (7, {})} | custom-call | flops 2684354560 | bytes 18874368 | tf_op jit(solution)/shard_map/pallas_call | solution.py:93
  207.7 14.1 %shard_map.97 = (f32[256,4096]{1,0:T(8,128)}, bf16[256,2048]{1,0:T(8,128)(2,1)}, bf16[256,2048]{1,0:T(8,128)(2,1)}) custom-call(s32[3]{0:T(128)} %add_add_fusion.1.sc_ref, bf16[256,4096]{1,0:T(8,128)(2,1)} %q_ref.9, bf16[256,4096]{1,0:T(8,128)(2,1)} %do_ref.9, bf16[256,2048]{1,0:T(8,128)(2,1)} %add.66.k_ref, ...), custom_call_target="tpu_custom_call", output_to_operand_aliasing={{0}: (7, {})} | custom-call | flops 2684354560 | bytes 18874368 | tf_op jit(solution)/shard_map/pallas_call | solution.py:93
  221.8 2.9 add.65.v_ref
  224.7 14.4 %shard_map.98 = (f32[256,4096]{1,0:T(8,128)}, bf16[256,2048]{1,0:T(8,128)(2,1)}, bf16[256,2048]{1,0:T(8,128)(2,1)}) custom-call(s32[3]{0:T(128)} %add_add_fusion.sc_ref, bf16[256,4096]{1,0:T(8,128)(2,1)} %q_ref.9, bf16[256,4096]{1,0:T(8,128)(2,1)} %do_ref.9, bf16[256,2048]{1,0:T(8,128)(2,1)} %add.64.k_ref, ...), custom_call_target="tpu_custom_call", output_to_operand_aliasing={{0}: (7, {})} | custom-call | flops 2684354560 | bytes 18874368 | tf_op jit(solution)/shard_map/pallas_call | solution.py:93
  240.5 1.3 collective-permute-start.25
  241.8 1.3 collective-permute-start.24
  245.7 17.9 %collective-permute-done.26 = bf16[256,2048]{1,0:T(8,128)(2,1)S(1)} collective-permute-done((bf16[256,2048]{1,0:T(8,128)(2,1)}, bf16[256,2048]{1,0:T(8,128)(2,1)S(1)}, u32[]{:S(2)}, u32[]{:S(2)}) %collective-permute-start.26) | collective-permute-done | bytes 1048608 | tf_op jit(solution)/shard_map/ppermute | solution.py:110
  264.9 3.7 collective-permute-done.25
  268.5 22.5 %collective-permute-start.23 = (bf16[256,2048]{1,0:T(8,128)(2,1)}, bf16[256,2048]{1,0:T(8,128)(2,1)S(1)}, u32[]{:S(2)}, u32[]{:S(2)}) collective-permute-start(bf16[256,2048]{1,0:T(8,128)(2,1)} %get-tuple-element.31), channel_id=1, source_target_pairs={{12,0},{28,16},{44,32},{60,48},{76,64},{92,80},{108,96},{124,112},... | collective-permute-start | bytes 3145736 | tf_op jit(solution)/shard_map/ppermute | solution.py:110
  291.0 25.3 %collective-permute-done.24 = bf16[256,2048]{1,0:T(8,128)(2,1)S(1)} collective-permute-done((bf16[256,2048]{1,0:T(8,128)(2,1)}, bf16[256,2048]{1,0:T(8,128)(2,1)S(1)}, u32[]{:S(2)}, u32[]{:S(2)}) %collective-permute-start.24) | collective-permute-done | bytes 1048608 | tf_op jit(solution)/shard_map/ppermute | solution.py:110
  316.3 1.3 collective-permute-start.22
  317.7 2.5 collective-permute-start.21
  321.0 1.9 collective-permute-start.27
  322.9 15.9 %collective-permute-done.17 = bf16[256,2048]{1,0:T(8,128)(2,1)S(1)} collective-permute-done((bf16[256,2048]{1,0:T(8,128)(2,1)S(1)}, bf16[256,2048]{1,0:T(8,128)(2,1)S(1)}, u32[]{:S(2)}, u32[]{:S(2)}) %collective-permute-start.17) | collective-permute-done | bytes 1048608 | tf_op jit(solution)/shard_map/ppermute | solution.py:110
  338.8 1.3 collective-permute-start.16
  340.9 1.4 collective-permute-start.15
  342.3 2.4 collective-permute-start.14
  344.7 18.0 %collective-permute-done.21 = bf16[256,2048]{1,0:T(8,128)(2,1)S(1)} collective-permute-done((bf16[256,2048]{1,0:T(8,128)(2,1)}, bf16[256,2048]{1,0:T(8,128)(2,1)S(1)}, u32[]{:S(2)}, u32[]{:S(2)}) %collective-permute-start.21) | collective-permute-done | bytes 1048608 | tf_op jit(solution)/shard_map/ppermute | solution.py:110
  362.7 1.9 collective-permute-start.20
  364.6 2.1 convert_add_fusion
  366.7 18.0 %collective-permute-done.16 = bf16[256,2048]{1,0:T(8,128)(2,1)S(1)} collective-permute-done((bf16[256,2048]{1,0:T(8,128)(2,1)S(1)}, bf16[256,2048]{1,0:T(8,128)(2,1)S(1)}, u32[]{:S(2)}, u32[]{:S(2)}) %collective-permute-start.16) | collective-permute-done | bytes 1048608 | tf_op jit(solution)/shard_map/ppermute | solution.py:110
  385.1 22.5 %collective-permute-done.14 = bf16[256,2048]{1,0:T(8,128)(2,1)S(1)} collective-permute-done((bf16[256,2048]{1,0:T(8,128)(2,1)S(1)}, bf16[256,2048]{1,0:T(8,128)(2,1)S(1)}, u32[]{:S(2)}, u32[]{:S(2)}) %collective-permute-start.14) | collective-permute-done | bytes 1048608 | tf_op jit(solution)/shard_map/ppermute | solution.py:110
  407.5 2.1 convert_add_fusion.1
  (50 shorter events, 16.0 us)
Async XLA Ops:
  0.6 26.3 %collective-permute-start.1 = (bf16[256,2048]{1,0:T(8,128)(2,1)}, bf16[256,2048]{1,0:T(8,128)(2,1)}, u32[]{:S(2)}, u32[]{:S(2)}) collective-permute-start(bf16[256,2048]{1,0:T(8,128)(2,1)} %k_ref.1), channel_id=1, source_target_pairs={{0,16},{4,20},{8,24},{12,28},{16,32},{20,36},{24,40},{28,44},{32,4... | collective-permute-start | bytes 3145736 | tf_op jit(solution)/shard_map/ppermute | solution.py:26
  4.4 45.0 %collective-permute-start.4 = (bf16[256,2048]{1,0:T(8,128)(2,1)}, bf16[256,2048]{1,0:T(8,128)(2,1)}, u32[]{:S(2)}, u32[]{:S(2)}) collective-permute-start(bf16[256,2048]{1,0:T(8,128)(2,1)} %v_ref.1), channel_id=1, source_target_pairs={{0,16},{4,20},{8,24},{12,28},{16,32},{20,36},{24,40},{28,44},{32,4... | collective-permute-start | bytes 3145736 | tf_op jit(solution)/shard_map/ppermute | solution.py:26
  7.3 45.2 %collective-permute-start.10 = (bf16[256,2048]{1,0:T(8,128)(2,1)}, bf16[256,2048]{1,0:T(8,128)(2,1)S(1)}, u32[]{:S(2)}, u32[]{:S(2)}) collective-permute-start(bf16[256,2048]{1,0:T(8,128)(2,1)} %k_ref.1), channel_id=1, source_target_pairs={{0,4},{4,8},{8,12},{16,20},{20,24},{24,28},{32,36},{36,40},{40,44}... | collective-permute-start | bytes 3145736 | tf_op jit(solution)/shard_map/ppermute | solution.py:110
  8.6 46.9 %collective-permute-start.12 = (bf16[256,2048]{1,0:T(8,128)(2,1)}, bf16[256,2048]{1,0:T(8,128)(2,1)S(1)}, u32[]{:S(2)}, u32[]{:S(2)}) collective-permute-start(bf16[256,2048]{1,0:T(8,128)(2,1)} %v_ref.1), channel_id=1, source_target_pairs={{0,4},{4,8},{8,12},{16,20},{20,24},{24,28},{32,36},{36,40},{40,44}... | collective-permute-start | bytes 3145736 | tf_op jit(solution)/shard_map/ppermute | solution.py:110
  9.9 52.7 %collective-permute-start.6 = (bf16[256,2048]{1,0:T(8,128)(2,1)}, bf16[256,2048]{1,0:T(8,128)(2,1)S(1)}, u32[]{:S(2)}, u32[]{:S(2)}) collective-permute-start(bf16[256,2048]{1,0:T(8,128)(2,1)} %k_ref.1), channel_id=1, source_target_pairs={{0,8},{4,12},{16,24},{20,28},{32,40},{36,44},{48,56},{52,60},{64,7... | collective-permute-start | bytes 3145736 | tf_op jit(solution)/shard_map/ppermute | solution.py:110
  26.9 37.0 %collective-permute-start.8 = (bf16[256,2048]{1,0:T(8,128)(2,1)}, bf16[256,2048]{1,0:T(8,128)(2,1)}, u32[]{:S(2)}, u32[]{:S(2)}) collective-permute-start(bf16[256,2048]{1,0:T(8,128)(2,1)} %v_ref.1), channel_id=1, source_target_pairs={{0,8},{4,12},{16,24},{20,28},{32,40},{36,44},{48,56},{52,60},{64,7... | collective-permute-start | bytes 3145736 | tf_op jit(solution)/shard_map/ppermute | solution.py:110
  49.4 45.9 %collective-permute-start.11 = (bf16[256,2048]{1,0:T(8,128)(2,1)}, bf16[256,2048]{1,0:T(8,128)(2,1)}, u32[]{:S(2)}, u32[]{:S(2)}) collective-permute-start(bf16[256,2048]{1,0:T(8,128)(2,1)} %collective-permute-done.1.k_ref), channel_id=1, source_target_pairs={{28,16},{44,32},{60,48},{76,64},{92,80},{108,96},{124,112},{29,17}... | collective-permute-start | bytes 3145736 | tf_op jit(solution)/shard_map/ppermute | solution.py:110
  52.5 87.7 %collective-permute-start.13 = (bf16[256,2048]{1,0:T(8,128)(2,1)}, bf16[256,2048]{1,0:T(8,128)(2,1)}, u32[]{:S(2)}, u32[]{:S(2)}) collective-permute-start(bf16[256,2048]{1,0:T(8,128)(2,1)} %collective-permute-done.4.v_ref), channel_id=1, source_target_pairs={{28,16},{44,32},{60,48},{76,64},{92,80},{108,96},{124,112},{29,17}... | collective-permute-start | bytes 3145736 | tf_op jit(solution)/shard_map/ppermute | solution.py:110
  55.5 86.0 %collective-permute-start.7 = (bf16[256,2048]{1,0:T(8,128)(2,1)}, bf16[256,2048]{1,0:T(8,128)(2,1)}, u32[]{:S(2)}, u32[]{:S(2)}) collective-permute-start(bf16[256,2048]{1,0:T(8,128)(2,1)} %collective-permute-done.1.k_ref), channel_id=1, source_target_pairs={{24,16},{28,20},{40,32},{44,36},{56,48},{60,52},{72,64},{76,68},{8... | collective-permute-start | bytes 3145736 | tf_op jit(solution)/shard_map/ppermute | solution.py:110
  62.6 128.1 %collective-permute-start = (bf16[256,2048]{1,0:T(8,128)(2,1)}, bf16[256,2048]{1,0:T(8,128)(2,1)}, u32[]{:S(2)}, u32[]{:S(2)}) collective-permute-start(bf16[256,2048]{1,0:T(8,128)(2,1)} %k_ref.1), channel_id=1, source_target_pairs={{0,12},{16,28},{32,44},{48,60},{64,76},{80,92},{96,108},{112,124},... | collective-permute-start | bytes 3145736 | tf_op jit(solution)/shard_map/ppermute | solution.py:110
  63.9 123.9 %collective-permute-start.9 = (bf16[256,2048]{1,0:T(8,128)(2,1)}, bf16[256,2048]{1,0:T(8,128)(2,1)}, u32[]{:S(2)}, u32[]{:S(2)}) collective-permute-start(bf16[256,2048]{1,0:T(8,128)(2,1)} %collective-permute-done.4.v_ref), channel_id=1, source_target_pairs={{24,16},{28,20},{40,32},{44,36},{56,48},{60,52},{72,64},{76,68},{8... | collective-permute-start | bytes 3145736 | tf_op jit(solution)/shard_map/ppermute | solution.py:110
  95.2 95.5 %collective-permute-start.2 = (bf16[256,2048]{1,0:T(8,128)(2,1)}, bf16[256,2048]{1,0:T(8,128)(2,1)}, u32[]{:S(2)}, u32[]{:S(2)}) collective-permute-start(bf16[256,2048]{1,0:T(8,128)(2,1)} %collective-permute-done.1.k_ref), channel_id=1, source_target_pairs={{20,16},{24,20},{28,24},{36,32},{40,36},{44,40},{52,48},{56,52},{6... | collective-permute-start | bytes 3145736 | tf_op jit(solution)/shard_map/ppermute | solution.py:110
  140.2 81.6 %collective-permute-start.3 = (bf16[256,2048]{1,0:T(8,128)(2,1)}, bf16[256,2048]{1,0:T(8,128)(2,1)}, u32[]{:S(2)}, u32[]{:S(2)}) collective-permute-start(bf16[256,2048]{1,0:T(8,128)(2,1)} %v_ref.1), channel_id=1, source_target_pairs={{0,12},{16,28},{32,44},{48,60},{64,76},{80,92},{96,108},{112,124},... | collective-permute-start | bytes 3145736 | tf_op jit(solution)/shard_map/ppermute | solution.py:110
  141.5 80.3 %collective-permute-start.5 = (bf16[256,2048]{1,0:T(8,128)(2,1)}, bf16[256,2048]{1,0:T(8,128)(2,1)}, u32[]{:S(2)}, u32[]{:S(2)}) collective-permute-start(bf16[256,2048]{1,0:T(8,128)(2,1)} %collective-permute-done.4.v_ref), channel_id=1, source_target_pairs={{20,16},{24,20},{28,24},{36,32},{40,36},{44,40},{52,48},{56,52},{6... | collective-permute-start | bytes 3145736 | tf_op jit(solution)/shard_map/ppermute | solution.py:110
  147.1 4.1 copy-start.4
  224.7 19.6 %copy-start.6 = (bf16[256,2048]{1,0:T(8,128)(2,1)S(1)}, bf16[256,2048]{1,0:T(8,128)(2,1)}, u32[]{:S(2)}) copy-start(bf16[256,2048]{1,0:T(8,128)(2,1)} %get-tuple-element.25) | copy-start | bytes 3145732
  224.7 38.8 %copy-start.5 = (bf16[256,2048]{1,0:T(8,128)(2,1)S(1)}, bf16[256,2048]{1,0:T(8,128)(2,1)}, u32[]{:S(2)}) copy-start(bf16[256,2048]{1,0:T(8,128)(2,1)} %get-tuple-element.24) | copy-start | bytes 3145732
  224.7 95.5 %copy-start.3 = (bf16[256,2048]{1,0:T(8,128)(2,1)S(1)}, bf16[256,2048]{1,0:T(8,128)(2,1)}, u32[]{:S(2)}) copy-start(bf16[256,2048]{1,0:T(8,128)(2,1)} %get-tuple-element.32) | copy-start | bytes 3145732
  239.2 24.4 %collective-permute-start.26 = (bf16[256,2048]{1,0:T(8,128)(2,1)}, bf16[256,2048]{1,0:T(8,128)(2,1)S(1)}, u32[]{:S(2)}, u32[]{:S(2)}) collective-permute-start(bf16[256,2048]{1,0:T(8,128)(2,1)} %get-tuple-element.31), channel_id=1, source_target_pairs={{0,4},{4,8},{8,12},{16,20},{20,24},{24,28},{32,36},{36,40},{40,44}... | collective-permute-start | bytes 3145736 | tf_op jit(solution)/shard_map/ppermute | solution.py:110
  240.5 28.1 %collective-permute-start.25 = (bf16[256,2048]{1,0:T(8,128)(2,1)}, bf16[256,2048]{1,0:T(8,128)(2,1)S(1)}, u32[]{:S(2)}, u32[]{:S(2)}) collective-permute-start(bf16[256,2048]{1,0:T(8,128)(2,1)} %get-tuple-element.30), channel_id=1, source_target_pairs={{0,8},{4,12},{16,24},{20,28},{32,40},{36,44},{48,56},{52,60},{64,7... | collective-permute-start | bytes 3145736 | tf_op jit(solution)/shard_map/ppermute | solution.py:110
  241.8 74.6 %collective-permute-start.24 = (bf16[256,2048]{1,0:T(8,128)(2,1)}, bf16[256,2048]{1,0:T(8,128)(2,1)S(1)}, u32[]{:S(2)}, u32[]{:S(2)}) collective-permute-start(bf16[256,2048]{1,0:T(8,128)(2,1)} %get-tuple-element.29), channel_id=1, source_target_pairs={{0,12},{16,28},{32,44},{48,60},{64,76},{80,92},{96,108},{112,124},... | collective-permute-start | bytes 3145736 | tf_op jit(solution)/shard_map/ppermute | solution.py:110
  243.1 74.7 %collective-permute-start.19 = (bf16[256,2048]{1,0:T(8,128)(2,1)}, bf16[256,2048]{1,0:T(8,128)(2,1)S(1)}, u32[]{:S(2)}, u32[]{:S(2)}) collective-permute-start(bf16[256,2048]{1,0:T(8,128)(2,1)} %get-tuple-element.26), channel_id=1, source_target_pairs={{0,4},{4,8},{8,12},{16,20},{20,24},{24,28},{32,36},{36,40},{40,44}... | collective-permute-start | bytes 3145736 | tf_op jit(solution)/shard_map/ppermute | solution.py:110
  244.4 76.6 %collective-permute-start.18 = (bf16[256,2048]{1,0:T(8,128)(2,1)S(1)}, bf16[256,2048]{1,0:T(8,128)(2,1)S(1)}, u32[]{:S(2)}, u32[]{:S(2)}) collective-permute-start(bf16[256,2048]{1,0:T(8,128)(2,1)S(1)} %copy-done.6), channel_id=1, source_target_pairs={{0,8},{4,12},{16,24},{20,28},{32,40},{36,44},{48,56},{52,60},{64,7... | collective-permute-start | bytes 3145736 | tf_op jit(solution)/shard_map/ppermute | solution.py:110
  263.6 75.2 %collective-permute-start.17 = (bf16[256,2048]{1,0:T(8,128)(2,1)S(1)}, bf16[256,2048]{1,0:T(8,128)(2,1)S(1)}, u32[]{:S(2)}, u32[]{:S(2)}) collective-permute-start(bf16[256,2048]{1,0:T(8,128)(2,1)S(1)} %copy-done.5), channel_id=1, source_target_pairs={{0,12},{16,28},{32,44},{48,60},{64,76},{80,92},{96,108},{112,124},... | collective-permute-start | bytes 3145736 | tf_op jit(solution)/shard_map/ppermute | solution.py:110
  268.5 72.4 %collective-permute-start.23 = (bf16[256,2048]{1,0:T(8,128)(2,1)}, bf16[256,2048]{1,0:T(8,128)(2,1)S(1)}, u32[]{:S(2)}, u32[]{:S(2)}) collective-permute-start(bf16[256,2048]{1,0:T(8,128)(2,1)} %get-tuple-element.31), channel_id=1, source_target_pairs={{12,0},{28,16},{44,32},{60,48},{76,64},{92,80},{108,96},{124,112},... | collective-permute-start | bytes 3145736 | tf_op jit(solution)/shard_map/ppermute | solution.py:110
  316.3 25.9 %collective-permute-start.22 = (bf16[256,2048]{1,0:T(8,128)(2,1)}, bf16[256,2048]{1,0:T(8,128)(2,1)S(1)}, u32[]{:S(2)}, u32[]{:S(2)}) collective-permute-start(bf16[256,2048]{1,0:T(8,128)(2,1)} %get-tuple-element.30), channel_id=1, source_target_pairs={{8,0},{12,4},{24,16},{28,20},{40,32},{44,36},{56,48},{60,52},{72,6... | collective-permute-start | bytes 3145736 | tf_op jit(solution)/shard_map/ppermute | solution.py:110
  317.7 44.9 %collective-permute-start.21 = (bf16[256,2048]{1,0:T(8,128)(2,1)}, bf16[256,2048]{1,0:T(8,128)(2,1)S(1)}, u32[]{:S(2)}, u32[]{:S(2)}) collective-permute-start(bf16[256,2048]{1,0:T(8,128)(2,1)} %get-tuple-element.29), channel_id=1, source_target_pairs={{4,0},{8,4},{12,8},{20,16},{24,20},{28,24},{36,32},{40,36},{44,40}... | collective-permute-start | bytes 3145736 | tf_op jit(solution)/shard_map/ppermute | solution.py:110
  320.3 18.6 %copy-start.7 = (bf16[256,2048]{1,0:T(8,128)(2,1)S(1)}, bf16[256,2048]{1,0:T(8,128)(2,1)}, u32[]{:S(2)}) copy-start(bf16[256,2048]{1,0:T(8,128)(2,1)} %get-tuple-element.26) | copy-start | bytes 3145732
  320.3 19.9 %copy-start.2 = (bf16[256,2048]{1,0:T(8,128)(2,1)S(1)}, bf16[256,2048]{1,0:T(8,128)(2,1)}, u32[]{:S(2)}) copy-start(bf16[256,2048]{1,0:T(8,128)(2,1)} %get-tuple-element.27) | copy-start | bytes 3145732
  321.0 43.6 %collective-permute-start.27 = (bf16[256,2048]{1,0:T(8,128)(2,1)S(1)}, bf16[256,2048]{1,0:T(8,128)(2,1)S(1)}, u32[]{:S(2)}, u32[]{:S(2)}) collective-permute-start(bf16[256,2048]{1,0:T(8,128)(2,1)S(1)} %add_convert_fusion), channel_id=1, source_target_pairs={{16,0},{20,4},{24,8},{28,12},{32,16},{36,20},{40,24},{44,28},{48,3... | collective-permute-start | bytes 3145736 | tf_op jit(solution)/shard_map/ppermute | solution.py:26
  338.8 45.9 %collective-permute-start.16 = (bf16[256,2048]{1,0:T(8,128)(2,1)S(1)}, bf16[256,2048]{1,0:T(8,128)(2,1)S(1)}, u32[]{:S(2)}, u32[]{:S(2)}) collective-permute-start(bf16[256,2048]{1,0:T(8,128)(2,1)S(1)} %copy-done.7), channel_id=1, source_target_pairs={{12,0},{28,16},{44,32},{60,48},{76,64},{92,80},{108,96},{124,112},... | collective-permute-start | bytes 3145736 | tf_op jit(solution)/shard_map/ppermute | solution.py:110
  340.2 24.4 %copy-start.1 = (f32[256,2048]{1,0:T(8,128)S(1)}, f32[256,2048]{1,0:T(8,128)}, u32[]{:S(2)}) copy-start(f32[256,2048]{1,0:T(8,128)} %get-tuple-element.28) | copy-start | bytes 6291460
  340.9 44.1 %collective-permute-start.15 = (bf16[256,2048]{1,0:T(8,128)(2,1)S(1)}, bf16[256,2048]{1,0:T(8,128)(2,1)S(1)}, u32[]{:S(2)}, u32[]{:S(2)}) collective-permute-start(bf16[256,2048]{1,0:T(8,128)(2,1)S(1)} %copy-done.6), channel_id=1, source_target_pairs={{8,0},{12,4},{24,16},{28,20},{40,32},{44,36},{56,48},{60,52},{72,6... | collective-permute-start | bytes 3145736 | tf_op jit(solution)/shard_map/ppermute | solution.py:110
  342.3 65.2 %collective-permute-start.14 = (bf16[256,2048]{1,0:T(8,128)(2,1)S(1)}, bf16[256,2048]{1,0:T(8,128)(2,1)S(1)}, u32[]{:S(2)}, u32[]{:S(2)}) collective-permute-start(bf16[256,2048]{1,0:T(8,128)(2,1)S(1)} %copy-done.5), channel_id=1, source_target_pairs={{4,0},{8,4},{12,8},{20,16},{24,20},{28,24},{36,32},{40,36},{44,40}... | collective-permute-start | bytes 3145736 | tf_op jit(solution)/shard_map/ppermute | solution.py:110
  362.7 44.9 %collective-permute-start.20 = (bf16[256,2048]{1,0:T(8,128)(2,1)S(1)}, bf16[256,2048]{1,0:T(8,128)(2,1)S(1)}, u32[]{:S(2)}, u32[]{:S(2)}) collective-permute-start(bf16[256,2048]{1,0:T(8,128)(2,1)S(1)} %add_convert_fusion.1), channel_id=1, source_target_pairs={{16,0},{20,4},{24,8},{28,12},{32,16},{36,20},{40,24},{44,28},{48,3... | collective-permute-start | bytes 3145736 | tf_op jit(solution)/shard_map/ppermute | solution.py:26
  364.6 42.9 %copy-start = (f32[256,2048]{1,0:T(8,128)S(1)}, f32[256,2048]{1,0:T(8,128)}, u32[]{:S(2)}) copy-start(f32[256,2048]{1,0:T(8,128)} %get-tuple-element.23) | copy-start | bytes 6291460

commit v4 on v3

--- a/solution.py
+++ b/solution.py
@@ -26,7 +26,12 @@
     return lax.ppermute(x, axis, pairs)
 
 
-def pair_kernel(group, heads, accumulate, sc_ref, q_ref, do_ref, k_ref, v_ref, lse_ref, dl_ref, *rest):
+def pair_kernel(group, heads, accumulate, parts, sc_ref, q_ref, do_ref, *refs):
+    k_refs = refs[:parts]
+    v_refs = refs[parts : 2 * parts]
+    lse_ref, dl_ref = refs[2 * parts : 2 * parts + 2]
+    rest = refs[2 * parts + 2 :]
+    k_ref = k_refs[0]
     if accumulate:
         dq_in_ref, dq_ref, dk_ref, dv_ref = rest
     else:
@@ -43,8 +48,11 @@
     tn = (((0,), (0,)), ((), ()))
     for c in range(heads):
         ksl = slice(c * HEAD_SIZE, (c + 1) * HEAD_SIZE)
-        k = k_ref[:, ksl]
-        v = v_ref[:, ksl]
+        k = k_refs[0][:, ksl]
+        v = v_refs[0][:, ksl]
+        for extra in range(1, parts):
+            k = k + k_refs[extra][:, ksl]
+            v = v + v_refs[extra][:, ksl]
         dk = jnp.zeros((cols, HEAD_SIZE), jnp.float32)
         dv = jnp.zeros((cols, HEAD_SIZE), jnp.float32)
         for g in range(group):
@@ -70,16 +78,19 @@
 
 
 def pair_grads(scalars, q, do, k, v, lse3, dl3, dq_in, kv_dtype):
+    k = tuple(k) if isinstance(k, (tuple, list)) else (k,)
+    v = tuple(v) if isinstance(v, (tuple, list)) else (v,)
+    parts = len(k)
     rows = q.shape[0]
-    cols = k.shape[0]
+    cols = k[0].shape[0]
     group = QUERY_HEADS // KEY_VALUE_HEADS
     accumulate = dq_in is not None
     heads = HEADS_PER_STEP
     qspec = pl.BlockSpec((rows, heads * group * HEAD_SIZE), lambda h, sc: (0, h))
     kspec = pl.BlockSpec((cols, heads * HEAD_SIZE), lambda h, sc: (0, h))
     sspec = pl.BlockSpec((heads, group, rows), lambda h, sc: (h, 0, 0))
-    in_specs = [qspec, qspec, kspec, kspec, sspec, sspec]
-    args = [q, do, k, v, lse3, dl3]
+    in_specs = [qspec, qspec] + [kspec] * (2 * parts) + [sspec, sspec]
+    args = [q, do, *k, *v, lse3, dl3]
     if accumulate:
         in_specs.append(qspec)
         args.append(dq_in)
@@ -89,9 +100,9 @@
         jax.ShapeDtypeStruct((cols, KEY_VALUE_HEADS * HEAD_SIZE), kv_dtype),
     )
     flops = 5 * 2 * rows * cols * HEAD_SIZE * QUERY_HEADS
-    nbytes = 2 * (2 * q.size + 2 * k.size) + 4 * q.size * (2 if accumulate else 1) + 2 * 2 * k.size * jnp.dtype(kv_dtype).itemsize
+    nbytes = 2 * (2 * q.size + 2 * parts * k[0].size) + 4 * q.size * (2 if accumulate else 1) + 2 * 2 * k[0].size * jnp.dtype(kv_dtype).itemsize
     return pl.pallas_call(
-        functools.partial(pair_kernel, group, heads, accumulate),
+        functools.partial(pair_kernel, group, heads, accumulate, parts),
         out_shape=out_shape,
         grid_spec=pltpu.PrefetchScalarGridSpec(
             num_scalar_prefetch=1,
@@ -99,7 +110,7 @@
             in_specs=in_specs,
             out_specs=[qspec, kspec, kspec],
         ),
-        input_output_aliases=({7: 0} if accumulate else {}),
+        input_output_aliases=({5 + 2 * parts: 0} if accumulate else {}),
         cost_estimate=pl.CostEstimate(
             flops=flops, transcendentals=rows * cols * QUERY_HEADS, bytes_accessed=int(nbytes)
         ),
@@ -133,8 +144,12 @@
         direct = sent_by(
             kv, "seq", [(i, i + distance) for i in range(count) if i % row + distance < row]
         )
-        relayed = sent_by(far, "seq", [(i, i - row + distance) for i in range(row, count) if i % row >= row - distance])
-        halos[distance] = (direct[0] + relayed[0], direct[1] + relayed[1])
+        relayed = sent_by(
+            far,
+            "seq",
+            [(i, i - row + distance) for i in range(row, count) if i % row >= row - distance],
+        )
+        halos[distance] = ((direct[0], relayed[0]), (direct[1], relayed[1]))
     limit = valid_count[0]
 
     delta = jnp.sum(
@@ -171,9 +186,20 @@
         if distance == blocks:
             far_part = (dk_part, dv_part)
             continue
-        arrived = sent_by((dk_part, dv_part), "seq", [(i, i - distance) for i in range(count) if i % row >= distance])
+        if distance == PAIR_ORDER[-1]:
+            arrived = passed_along((dk_part, dv_part), "seq", -distance)
+            key_grad = key_grad + arrived[0].astype(jnp.float32)
+            value_grad = value_grad + arrived[1].astype(jnp.float32)
+            continue
+        arrived = sent_by(
+            (dk_part, dv_part), "seq", [(i, i - distance) for i in range(count) if i % row >= distance]
+        )
         merged.append(
-            sent_by((dk_part, dv_part), "seq", [(i, i + row - distance) for i in range(count) if i % row < distance])
+            sent_by(
+                (dk_part, dv_part),
+                "seq",
+                [(i, i + row - distance) for i in range(count) if i % row < distance],
+            )
         )
         key_grad = key_grad + arrived[0].astype(jnp.float32)
         value_grad = value_grad + arrived[1].astype(jnp.float32)

time: 415 us -> 349 us (0.84)
  starting transfers between devices: 82.2 us -> 54.4 us
  waiting for transfers between devices: 219 us -> 193 us
  other arithmetic: 31.6 us -> 21.7 us
    ppermute x24 -> x20, waiting for transfers between devices: 182 us -> 95.2 us  [sent_by(): return lax.ppermute(x, axis, pairs)]
    ppermute x4 -> x6, waiting for transfers between devices: 36.9 us -> 97.3 us  [passed_along(): return lax.ppermute(x, axis, pairs)]
    ppermute x24 -> x20, starting transfers between devices: 71.7 us -> 40 us  [sent_by(): return lax.ppermute(x, axis, pairs)]
    add x6 -> x0, other arithmetic: 16.6 us -> none  [local(): halos[distance] = (direct[0] + relayed[0], direct[1] + relayed[1])]
    ppermute x4 -> x6, starting transfers between devices: 10.5 us -> 14.3 us  [passed_along(): return lax.ppermute(x, axis, pairs)]
  transfers between devices with their start and end apart: 28 -> 26, of which waited for: 13 -> 11; matrix products, arithmetic and copies ran while one was open for 7% -> 7% of each run, Pallas kernels for 14% -> 20%
where the time goes in v4:
time: 349 us; the launch traced here: 348 us
  waiting for transfers between devices  193 us (55%)
  Pallas kernels  71.3 us (20%)
  starting transfers between devices  54.4 us (16%)
  other arithmetic  21.7 us (6%)
  local copies, waits for them, and re-layouts  6.29 us (2%)
    ppermute x6, waiting for transfers between devices, passed_along(): return lax.ppermute(x, axis, pairs)  97.3 us
    ppermute x20, waiting for transfers between devices, sent_by(): return lax.ppermute(x, axis, pairs)  95.2 us
    pallas_call x5, Pallas kernels, pair_grads(): pl.pallas_call(functools.partial(pair_kernel, group, heads, accumulate, p...  71.3 us
    ppermute x20, starting transfers between devices, sent_by(): return lax.ppermute(x, axis, pairs)  40 us
    ppermute x6, starting transfers between devices, passed_along(): return lax.ppermute(x, axis, pairs)  14.3 us
  transfers between devices with their start and end apart: 26, of which 11 were waited for; matrix products, arithmetic and copies ran while one was open for 7% of the time, Pallas kernels for 20%

profile of v4, /device:TPU:31, one launch (start us, length us, event | category | flops | bytes accessed | tf_op | source)
XLA Modules:
  0.0 347.8 jit_solution(7239973864018564399)
XLA Ops:
  0.6 3.7 %collective-permute-start.1 = (bf16[256,2048]{1,0:T(8,128)(2,1)}, bf16[256,2048]{1,0:T(8,128)(2,1)}, u32[]{:S(2)}, u32[]{:S(2)}) collective-permute-start(bf16[256,2048]{1,0:T(8,128)(2,1)} %refs_0_.1), channel_id=1, source_target_pairs={{0,16},{4,20},{8,24},{12,28},{16,32},{20,36},{24,40},{28,44},{32,4... | collective-permute-start | bytes 3145736 | tf_op jit(solution)/shard_map/ppermute | solution.py:26
  4.4 2.9 collective-permute-start.4
  7.3 1.3 collective-permute-start.10
  8.6 1.3 collective-permute-start.12
  9.9 1.3 collective-permute-start.6
  11.2 15.7 %collective-permute-done.1.refs_0_ = bf16[256,2048]{1,0:T(8,128)(2,1)} collective-permute-done((bf16[256,2048]{1,0:T(8,128)(2,1)}, bf16[256,2048]{1,0:T(8,128)(2,1)}, u32[]{:S(2)}, u32[]{:S(2)}) %collective-permute-start.1) | collective-permute-done | bytes 1048608 | tf_op jit(solution)/shard_map/ppermute | solution.py:26
  26.9 1.3 collective-permute-start.8
  28.2 21.2 %collective-permute-done.4.refs_1_ = bf16[256,2048]{1,0:T(8,128)(2,1)} collective-permute-done((bf16[256,2048]{1,0:T(8,128)(2,1)}, bf16[256,2048]{1,0:T(8,128)(2,1)}, u32[]{:S(2)}, u32[]{:S(2)}) %collective-permute-start.4) | collective-permute-done | bytes 1048608 | tf_op jit(solution)/shard_map/ppermute | solution.py:26
  49.4 3.2 collective-permute-start.11
  52.5 2.3 collective-permute-start.13
  54.8 5.0 %multiply_bitcast_fusion = f32[32,8,32,128]{3,1,2,0:T(8,128)} fusion(bf16[256,4096]{1,0:T(8,128)(2,1)} %param.10, bf16[256,4096]{1,0:T(8,128)(2,1)} %do_ref.9), kind=kLoop, calls=%fused_computation | loop fusion | flops 3145728 | bytes 8388608
  61.1 2.3 collective-permute-start.7
  63.3 2.3 collective-permute-start.9
  66.8 1.3 collective-permute-start
  68.8 4.9 %copy.15 = f32[32,8,32,128]{3,2,1,0:T(8,128)} copy(f32[32,8,32,128]{3,1,2,0:T(8,128)} %multiply_bitcast_fusion) | data formatting | bytes 8388608
  73.7 3.3 reduce_sum.9
  78.4 14.0 %shard_map.94 = (f32[256,4096]{1,0:T(8,128)}, f32[256,2048]{1,0:T(8,128)}, f32[256,2048]{1,0:T(8,128)}) custom-call(s32[3]{0:T(128)} %add_add_fusion.4.sc_ref, bf16[256,4096]{1,0:T(8,128)(2,1)} %q_ref.9, bf16[256,4096]{1,0:T(8,128)(2,1)} %do_ref.9, bf16[256,2048]{1,0:T(8,128)(2,1)} %refs_0_.1, bf16[256,2048]{1,0:T(8,128)(2,1)} %refs_1_.1, ...), custom_call_target="tpu_custom_call" | custom-call | flops 2684354560 | bytes 18874368 | tf_op jit(solution)/shard_map/pallas_call | solution.py:104
  92.4 14.1 %shard_map.95 = (f32[256,4096]{1,0:T(8,128)}, bf16[256,2048]{1,0:T(8,128)(2,1)}, bf16[256,2048]{1,0:T(8,128)(2,1)}) custom-call(s32[3]{0:T(128)} %add_add_fusion.3.sc_ref, bf16[256,4096]{1,0:T(8,128)(2,1)} %q_ref.9, bf16[256,4096]{1,0:T(8,128)(2,1)} %do_ref.9, bf16[256,2048]{1,0:T(8,128)(2,1)} %collective-permute-done.1.refs_0_, ...), custom_call_target="tpu_custom_call", output_to_operand_aliasing={{0}: (7, {})} | custom-call | flops 2684354560 | bytes 18874368 | tf_op jit(solution)/shard_map/pallas_call | solution.py:104
  106.4 11.2 %collective-permute-done.11.refs_1_ = bf16[256,2048]{1,0:T(8,128)(2,1)} collective-permute-done((bf16[256,2048]{1,0:T(8,128)(2,1)}, bf16[256,2048]{1,0:T(8,128)(2,1)}, u32[]{:S(2)}, u32[]{:S(2)}) %collective-permute-start.11) | collective-permute-done | bytes 1048608 | tf_op jit(solution)/shard_map/ppermute | solution.py:121
  119.0 21.2 %collective-permute-done.13.refs_3_ = bf16[256,2048]{1,0:T(8,128)(2,1)} collective-permute-done((bf16[256,2048]{1,0:T(8,128)(2,1)}, bf16[256,2048]{1,0:T(8,128)(2,1)}, u32[]{:S(2)}, u32[]{:S(2)}) %collective-permute-start.13) | collective-permute-done | bytes 1048608 | tf_op jit(solution)/shard_map/ppermute | solution.py:121
  140.2 2.4 collective-permute-start.2
  142.6 14.4 %shard_map.96 = (f32[256,4096]{1,0:T(8,128)}, bf16[256,2048]{1,0:T(8,128)(2,1)}, bf16[256,2048]{1,0:T(8,128)(2,1)}) custom-call(s32[3]{0:T(128)} %add_add_fusion.2.sc_ref, bf16[256,4096]{1,0:T(8,128)(2,1)} %q_ref.9, bf16[256,4096]{1,0:T(8,128)(2,1)} %do_ref.9, bf16[256,2048]{1,0:T(8,128)(2,1)} %copy-done.4, ...), custom_call_target="tpu_custom_call", output_to_operand_aliasing={{0}: (9, {})} | custom-call | flops 2684354560 | bytes 20971520 | tf_op jit(solution)/shard_map/pallas_call | solution.py:104
  157.0 2.8 collective-permute-start.5
  159.9 14.4 %shard_map.97 = (f32[256,4096]{1,0:T(8,128)}, bf16[256,2048]{1,0:T(8,128)(2,1)}, bf16[256,2048]{1,0:T(8,128)(2,1)}) custom-call(s32[3]{0:T(128)} %add_add_fusion.1.sc_ref, bf16[256,4096]{1,0:T(8,128)(2,1)} %q_ref.9, bf16[256,4096]{1,0:T(8,128)(2,1)} %do_ref.9, bf16[256,2048]{1,0:T(8,128)(2,1)} %copy-done.2, ...), custom_call_target="tpu_custom_call", output_to_operand_aliasing={{0}: (9, {})} | custom-call | flops 2684354560 | bytes 20971520 | tf_op jit(solution)/shard_map/pallas_call | solution.py:104
  174.3 1.3 collective-permute-start.24
  175.6 1.3 collective-permute-start.23
  176.9 1.3 collective-permute-start.18
  178.2 1.3 collective-permute-start.17
  180.1 5.5 %collective-permute-done.5.refs_3_ = bf16[256,2048]{1,0:T(8,128)(2,1)} collective-permute-done((bf16[256,2048]{1,0:T(8,128)(2,1)}, bf16[256,2048]{1,0:T(8,128)(2,1)}, u32[]{:S(2)}, u32[]{:S(2)}) %collective-permute-start.5) | collective-permute-done | bytes 1048608 | tf_op jit(solution)/shard_map/ppermute | solution.py:121
  185.7 6.8 %collective-permute-start.21 = (bf16[256,2048]{1,0:T(8,128)(2,1)}, bf16[256,2048]{1,0:T(8,128)(2,1)}, u32[]{:S(2)}, u32[]{:S(2)}) collective-permute-start(bf16[256,2048]{1,0:T(8,128)(2,1)} %get-tuple-element.30), channel_id=1, source_target_pairs={{8,0},{12,4},{24,16},{28,20},{40,32},{44,36},{56,48},{60,52},{72,6... | collective-permute-start | bytes 3145736 | tf_op jit(solution)/shard_map/ppermute | solution.py:121
  192.5 14.4 %shard_map.98 = (f32[256,4096]{1,0:T(8,128)}, bf16[256,2048]{1,0:T(8,128)(2,1)}, bf16[256,2048]{1,0:T(8,128)(2,1)}) custom-call(s32[3]{0:T(128)} %add_add_fusion.sc_ref, bf16[256,4096]{1,0:T(8,128)(2,1)} %q_ref.9, bf16[256,4096]{1,0:T(8,128)(2,1)} %do_ref.9, bf16[256,2048]{1,0:T(8,128)(2,1)} %copy-done.5, ...), custom_call_target="tpu_custom_call", output_to_operand_aliasing={{0}: (9, {})} | custom-call | flops 2684354560 | bytes 20971520 | tf_op jit(solution)/shard_map/pallas_call | solution.py:104
  206.9 5.9 %collective-permute-done.24 = bf16[256,2048]{1,0:T(8,128)(2,1)} collective-permute-done((bf16[256,2048]{1,0:T(8,128)(2,1)}, bf16[256,2048]{1,0:T(8,128)(2,1)}, u32[]{:S(2)}, u32[]{:S(2)}) %collective-permute-start.24) | collective-permute-done | bytes 1048608 | tf_op jit(solution)/shard_map/ppermute | solution.py:121
  212.8 1.3 collective-permute-start.20
  214.2 35.2 %collective-permute-done.23 = bf16[256,2048]{1,0:T(8,128)(2,1)} collective-permute-done((bf16[256,2048]{1,0:T(8,128)(2,1)}, bf16[256,2048]{1,0:T(8,128)(2,1)}, u32[]{:S(2)}, u32[]{:S(2)}) %collective-permute-start.23) | collective-permute-done | bytes 1048608 | tf_op jit(solution)/shard_map/ppermute | solution.py:121
  249.4 1.9 collective-permute-start.22
  251.3 2.5 add_convert_fusion
  253.9 1.9 collective-permute-start.25
  255.8 16.1 %collective-permute-done.17 = bf16[256,2048]{1,0:T(8,128)(2,1)} collective-permute-done((bf16[256,2048]{1,0:T(8,128)(2,1)}, bf16[256,2048]{1,0:T(8,128)(2,1)}, u32[]{:S(2)}, u32[]{:S(2)}) %collective-permute-start.17) | collective-permute-done | bytes 1048608 | tf_op jit(solution)/shard_map/ppermute | solution.py:121
  271.9 1.3 collective-permute-start.15
  273.3 2.2 add_convert_fusion.1
  275.5 1.9 collective-permute-start.16
  277.5 2.4 collective-permute-start.14
  279.9 1.9 collective-permute-start.19
  281.8 21.8 %collective-permute-done.25 = bf16[256,2048]{1,0:T(8,128)(2,1)S(1)} collective-permute-done((bf16[256,2048]{1,0:T(8,128)(2,1)S(1)}, bf16[256,2048]{1,0:T(8,128)(2,1)S(1)}, u32[]{:S(2)}, u32[]{:S(2)}) %collective-permute-start.25) | collective-permute-done | bytes 1048608 | tf_op jit(solution)/shard_map/ppermute | solution.py:26
  303.7 3.4 convert_add_fusion
  307.1 13.4 %collective-permute-done.16 = bf16[256,2048]{1,0:T(8,128)(2,1)S(1)} collective-permute-done((bf16[256,2048]{1,0:T(8,128)(2,1)S(1)}, bf16[256,2048]{1,0:T(8,128)(2,1)S(1)}, u32[]{:S(2)}, u32[]{:S(2)}) %collective-permute-start.16) | collective-permute-done | bytes 1048608 | tf_op jit(solution)/shard_map/ppermute | solution.py:26
  320.5 25.2 %collective-permute-done.19 = bf16[256,2048]{1,0:T(8,128)(2,1)S(1)} collective-permute-done((bf16[256,2048]{1,0:T(8,128)(2,1)S(1)}, bf16[256,2048]{1,0:T(8,128)(2,1)S(1)}, u32[]{:S(2)}, u32[]{:S(2)}) %collective-permute-start.19) | collective-permute-done | bytes 1048608 | tf_op jit(solution)/shard_map/ppermute | solution.py:26
  345.7 2.1 convert_add_fusion.1
  (50 shorter events, 5.8 us)
Async XLA Ops:
  0.6 26.3 %collective-permute-start.1 = (bf16[256,2048]{1,0:T(8,128)(2,1)}, bf16[256,2048]{1,0:T(8,128)(2,1)}, u32[]{:S(2)}, u32[]{:S(2)}) collective-permute-start(bf16[256,2048]{1,0:T(8,128)(2,1)} %refs_0_.1), channel_id=1, source_target_pairs={{0,16},{4,20},{8,24},{12,28},{16,32},{20,36},{24,40},{28,44},{32,4... | collective-permute-start | bytes 3145736 | tf_op jit(solution)/shard_map/ppermute | solution.py:26
  4.4 45.0 %collective-permute-start.4 = (bf16[256,2048]{1,0:T(8,128)(2,1)}, bf16[256,2048]{1,0:T(8,128)(2,1)}, u32[]{:S(2)}, u32[]{:S(2)}) collective-permute-start(bf16[256,2048]{1,0:T(8,128)(2,1)} %refs_1_.1), channel_id=1, source_target_pairs={{0,16},{4,20},{8,24},{12,28},{16,32},{20,36},{24,40},{28,44},{32,4... | collective-permute-start | bytes 3145736 | tf_op jit(solution)/shard_map/ppermute | solution.py:26
  7.3 45.3 %collective-permute-start.10 = (bf16[256,2048]{1,0:T(8,128)(2,1)}, bf16[256,2048]{1,0:T(8,128)(2,1)S(1)}, u32[]{:S(2)}, u32[]{:S(2)}) collective-permute-start(bf16[256,2048]{1,0:T(8,128)(2,1)} %refs_0_.1), channel_id=1, source_target_pairs={{0,4},{4,8},{8,12},{16,20},{20,24},{24,28},{32,36},{36,40},{40,44}... | collective-permute-start | bytes 3145736 | tf_op jit(solution)/shard_map/ppermute | solution.py:121
  8.6 52.5 %collective-permute-start.12 = (bf16[256,2048]{1,0:T(8,128)(2,1)}, bf16[256,2048]{1,0:T(8,128)(2,1)}, u32[]{:S(2)}, u32[]{:S(2)}) collective-permute-start(bf16[256,2048]{1,0:T(8,128)(2,1)} %refs_1_.1), channel_id=1, source_target_pairs={{0,4},{4,8},{8,12},{16,20},{20,24},{24,28},{32,36},{36,40},{40,44}... | collective-permute-start | bytes 3145736 | tf_op jit(solution)/shard_map/ppermute | solution.py:121
  9.9 53.4 %collective-permute-start.6 = (bf16[256,2048]{1,0:T(8,128)(2,1)}, bf16[256,2048]{1,0:T(8,128)(2,1)S(1)}, u32[]{:S(2)}, u32[]{:S(2)}) collective-permute-start(bf16[256,2048]{1,0:T(8,128)(2,1)} %refs_0_.1), channel_id=1, source_target_pairs={{0,8},{4,12},{16,24},{20,28},{32,40},{36,44},{48,56},{52,60},{64,7... | collective-permute-start | bytes 3145736 | tf_op jit(solution)/shard_map/ppermute | solution.py:121
  26.9 40.0 %collective-permute-start.8 = (bf16[256,2048]{1,0:T(8,128)(2,1)}, bf16[256,2048]{1,0:T(8,128)(2,1)S(1)}, u32[]{:S(2)}, u32[]{:S(2)}) collective-permute-start(bf16[256,2048]{1,0:T(8,128)(2,1)} %refs_1_.1), channel_id=1, source_target_pairs={{0,8},{4,12},{16,24},{20,28},{32,40},{36,44},{48,56},{52,60},{64,7... | collective-permute-start | bytes 3145736 | tf_op jit(solution)/shard_map/ppermute | solution.py:121
  49.4 68.3 %collective-permute-start.11 = (bf16[256,2048]{1,0:T(8,128)(2,1)}, bf16[256,2048]{1,0:T(8,128)(2,1)}, u32[]{:S(2)}, u32[]{:S(2)}) collective-permute-start(bf16[256,2048]{1,0:T(8,128)(2,1)} %collective-permute-done.1.refs_0_), channel_id=1, source_target_pairs={{28,16},{44,32},{60,48},{76,64},{92,80},{108,96},{124,112},{29,17}... | collective-permute-start | bytes 3145736 | tf_op jit(solution)/shard_map/ppermute | solution.py:121
  52.5 7.2 %copy-start.4 = (bf16[256,2048]{1,0:T(8,128)(2,1)}, bf16[256,2048]{1,0:T(8,128)(2,1)S(1)}, u32[]{:S(2)}) copy-start(bf16[256,2048]{1,0:T(8,128)(2,1)S(1)} %collective-permute-done.10.refs_0_) | copy-start | bytes 3145732
  52.5 87.6 %collective-permute-start.13 = (bf16[256,2048]{1,0:T(8,128)(2,1)}, bf16[256,2048]{1,0:T(8,128)(2,1)}, u32[]{:S(2)}, u32[]{:S(2)}) collective-permute-start(bf16[256,2048]{1,0:T(8,128)(2,1)} %collective-permute-done.4.refs_1_), channel_id=1, source_target_pairs={{28,16},{44,32},{60,48},{76,64},{92,80},{108,96},{124,112},{29,17}... | collective-permute-start | bytes 3145736 | tf_op jit(solution)/shard_map/ppermute | solution.py:121
  61.1 95.9 %collective-permute-start.7 = (bf16[256,2048]{1,0:T(8,128)(2,1)}, bf16[256,2048]{1,0:T(8,128)(2,1)}, u32[]{:S(2)}, u32[]{:S(2)}) collective-permute-start(bf16[256,2048]{1,0:T(8,128)(2,1)} %collective-permute-done.1.refs_0_), channel_id=1, source_target_pairs={{24,16},{28,20},{40,32},{44,36},{56,48},{60,52},{72,64},{76,68},{8... | collective-permute-start | bytes 3145736 | tf_op jit(solution)/shard_map/ppermute | solution.py:121
  63.3 10.4 %copy-start.2 = (bf16[256,2048]{1,0:T(8,128)(2,1)}, bf16[256,2048]{1,0:T(8,128)(2,1)S(1)}, u32[]{:S(2)}) copy-start(bf16[256,2048]{1,0:T(8,128)(2,1)S(1)} %collective-permute-done.6.refs_0_) | copy-start | bytes 3145732
  63.3 96.5 %collective-permute-start.9 = (bf16[256,2048]{1,0:T(8,128)(2,1)}, bf16[256,2048]{1,0:T(8,128)(2,1)}, u32[]{:S(2)}, u32[]{:S(2)}) collective-permute-start(bf16[256,2048]{1,0:T(8,128)(2,1)} %collective-permute-done.4.refs_1_), channel_id=1, source_target_pairs={{24,16},{28,20},{40,32},{44,36},{56,48},{60,52},{72,64},{76,68},{8... | collective-permute-start | bytes 3145736 | tf_op jit(solution)/shard_map/ppermute | solution.py:121
  66.8 6.9 %copy-start.3 = (bf16[256,2048]{1,0:T(8,128)(2,1)}, bf16[256,2048]{1,0:T(8,128)(2,1)S(1)}, u32[]{:S(2)}) copy-start(bf16[256,2048]{1,0:T(8,128)(2,1)S(1)} %collective-permute-done.8.refs_2_) | copy-start | bytes 3145732
  66.8 108.7 %collective-permute-start = (bf16[256,2048]{1,0:T(8,128)(2,1)}, bf16[256,2048]{1,0:T(8,128)(2,1)S(1)}, u32[]{:S(2)}, u32[]{:S(2)}) collective-permute-start(bf16[256,2048]{1,0:T(8,128)(2,1)} %refs_0_.1), channel_id=1, source_target_pairs={{0,12},{16,28},{32,44},{48,60},{64,76},{80,92},{96,108},{112,124},... | collective-permute-start | bytes 3145736 | tf_op jit(solution)/shard_map/ppermute | solution.py:121
  73.7 4.1 %copy-start.9 = (f32[32,256]{1,0:T(8,128)S(1)}, f32[32,256]{1,0:T(8,128)}, u32[]{:S(2)}) copy-start(f32[32,256]{1,0:T(8,128)} %param.12) | copy-start | bytes 98308
  117.7 59.2 %collective-permute-start.3 = (bf16[256,2048]{1,0:T(8,128)(2,1)}, bf16[256,2048]{1,0:T(8,128)(2,1)S(1)}, u32[]{:S(2)}, u32[]{:S(2)}) collective-permute-start(bf16[256,2048]{1,0:T(8,128)(2,1)} %refs_1_.1), channel_id=1, source_target_pairs={{0,12},{16,28},{32,44},{48,60},{64,76},{80,92},{96,108},{112,124},... | collective-permute-start | bytes 3145736 | tf_op jit(solution)/shard_map/ppermute | solution.py:121
  140.2 38.1 %collective-permute-start.2 = (bf16[256,2048]{1,0:T(8,128)(2,1)}, bf16[256,2048]{1,0:T(8,128)(2,1)S(1)}, u32[]{:S(2)}, u32[]{:S(2)}) collective-permute-start(bf16[256,2048]{1,0:T(8,128)(2,1)} %collective-permute-done.1.refs_0_), channel_id=1, source_target_pairs={{20,16},{24,20},{28,24},{36,32},{40,36},{44,40},{52,48},{56,52},{6... | collective-permute-start | bytes 3145736 | tf_op jit(solution)/shard_map/ppermute | solution.py:121
  157.0 28.7 %collective-permute-start.5 = (bf16[256,2048]{1,0:T(8,128)(2,1)}, bf16[256,2048]{1,0:T(8,128)(2,1)}, u32[]{:S(2)}, u32[]{:S(2)}) collective-permute-start(bf16[256,2048]{1,0:T(8,128)(2,1)} %collective-permute-done.4.refs_1_), channel_id=1, source_target_pairs={{20,16},{24,20},{28,24},{36,32},{40,36},{44,40},{52,48},{56,52},{6... | collective-permute-start | bytes 3145736 | tf_op jit(solution)/shard_map/ppermute | solution.py:121
  174.3 38.5 %collective-permute-start.24 = (bf16[256,2048]{1,0:T(8,128)(2,1)}, bf16[256,2048]{1,0:T(8,128)(2,1)}, u32[]{:S(2)}, u32[]{:S(2)}) collective-permute-start(bf16[256,2048]{1,0:T(8,128)(2,1)} %get-tuple-element.30), channel_id=1, source_target_pairs={{0,8},{4,12},{16,24},{20,28},{32,40},{36,44},{48,56},{52,60},{64,7... | collective-permute-start | bytes 3145736 | tf_op jit(solution)/shard_map/ppermute | solution.py:121
  175.6 16.9 %copy-start.5 = (bf16[256,2048]{1,0:T(8,128)(2,1)}, bf16[256,2048]{1,0:T(8,128)(2,1)S(1)}, u32[]{:S(2)}) copy-start(bf16[256,2048]{1,0:T(8,128)(2,1)S(1)} %collective-permute-done.refs_0_) | copy-start | bytes 3145732
  175.6 73.8 %collective-permute-start.23 = (bf16[256,2048]{1,0:T(8,128)(2,1)}, bf16[256,2048]{1,0:T(8,128)(2,1)}, u32[]{:S(2)}, u32[]{:S(2)}) collective-permute-start(bf16[256,2048]{1,0:T(8,128)(2,1)} %get-tuple-element.29), channel_id=1, source_target_pairs={{0,12},{16,28},{32,44},{48,60},{64,76},{80,92},{96,108},{112,124},... | collective-permute-start | bytes 3145736 | tf_op jit(solution)/shard_map/ppermute | solution.py:121
  176.9 15.6 %copy-start.6 = (bf16[256,2048]{1,0:T(8,128)(2,1)}, bf16[256,2048]{1,0:T(8,128)(2,1)S(1)}, u32[]{:S(2)}) copy-start(bf16[256,2048]{1,0:T(8,128)(2,1)S(1)} %collective-permute-done.3.refs_2_) | copy-start | bytes 3145732
  176.9 77.0 %collective-permute-start.18 = (bf16[256,2048]{1,0:T(8,128)(2,1)}, bf16[256,2048]{1,0:T(8,128)(2,1)}, u32[]{:S(2)}, u32[]{:S(2)}) collective-permute-start(bf16[256,2048]{1,0:T(8,128)(2,1)} %get-tuple-element.25), channel_id=1, source_target_pairs={{0,8},{4,12},{16,24},{20,28},{32,40},{36,44},{48,56},{52,60},{64,7... | collective-permute-start | bytes 3145736 | tf_op jit(solution)/shard_map/ppermute | solution.py:121
  178.2 14.3 %copy-start.7 = (bf16[256,2048]{1,0:T(8,128)(2,1)}, bf16[256,2048]{1,0:T(8,128)(2,1)S(1)}, u32[]{:S(2)}) copy-start(bf16[256,2048]{1,0:T(8,128)(2,1)S(1)} %collective-permute-done.2.refs_1_) | copy-start | bytes 3145732
  178.2 93.6 %collective-permute-start.17 = (bf16[256,2048]{1,0:T(8,128)(2,1)}, bf16[256,2048]{1,0:T(8,128)(2,1)}, u32[]{:S(2)}, u32[]{:S(2)}) collective-permute-start(bf16[256,2048]{1,0:T(8,128)(2,1)} %get-tuple-element.24), channel_id=1, source_target_pairs={{0,12},{16,28},{32,44},{48,60},{64,76},{80,92},{96,108},{112,124},... | collective-permute-start | bytes 3145736 | tf_op jit(solution)/shard_map/ppermute | solution.py:121
  185.7 91.8 %collective-permute-start.21 = (bf16[256,2048]{1,0:T(8,128)(2,1)}, bf16[256,2048]{1,0:T(8,128)(2,1)}, u32[]{:S(2)}, u32[]{:S(2)}) collective-permute-start(bf16[256,2048]{1,0:T(8,128)(2,1)} %get-tuple-element.30), channel_id=1, source_target_pairs={{8,0},{12,4},{24,16},{28,20},{40,32},{44,36},{56,48},{60,52},{72,6... | collective-permute-start | bytes 3145736 | tf_op jit(solution)/shard_map/ppermute | solution.py:121
  212.8 67.1 %collective-permute-start.20 = (bf16[256,2048]{1,0:T(8,128)(2,1)}, bf16[256,2048]{1,0:T(8,128)(2,1)S(1)}, u32[]{:S(2)}, u32[]{:S(2)}) collective-permute-start(bf16[256,2048]{1,0:T(8,128)(2,1)} %get-tuple-element.29), channel_id=1, source_target_pairs={{4,0},{8,4},{12,8},{20,16},{24,20},{28,24},{36,32},{40,36},{44,40}... | collective-permute-start | bytes 3145736 | tf_op jit(solution)/shard_map/ppermute | solution.py:121
  249.4 26.1 %collective-permute-start.22 = (bf16[256,2048]{1,0:T(8,128)(2,1)}, bf16[256,2048]{1,0:T(8,128)(2,1)S(1)}, u32[]{:S(2)}, u32[]{:S(2)}) collective-permute-start(bf16[256,2048]{1,0:T(8,128)(2,1)} %get-tuple-element.31), channel_id=1, source_target_pairs={{12,0},{16,4},{20,8},{24,12},{28,16},{32,20},{36,24},{40,28},{44,3... | collective-permute-start | bytes 3145736 | tf_op jit(solution)/shard_map/ppermute | solution.py:26
  251.3 20.6 %copy-start.11 = (bf16[256,2048]{1,0:T(8,128)(2,1)S(1)}, bf16[256,2048]{1,0:T(8,128)(2,1)}, u32[]{:S(2)}) copy-start(bf16[256,2048]{1,0:T(8,128)(2,1)} %get-tuple-element.25) | copy-start | bytes 3145732
  251.3 21.9 %copy-start.8 = (bf16[256,2048]{1,0:T(8,128)(2,1)S(1)}, bf16[256,2048]{1,0:T(8,128)(2,1)}, u32[]{:S(2)}) copy-start(bf16[256,2048]{1,0:T(8,128)(2,1)} %get-tuple-element.27) | copy-start | bytes 3145732
  253.9 49.8 %collective-permute-start.25 = (bf16[256,2048]{1,0:T(8,128)(2,1)S(1)}, bf16[256,2048]{1,0:T(8,128)(2,1)S(1)}, u32[]{:S(2)}, u32[]{:S(2)}) collective-permute-start(bf16[256,2048]{1,0:T(8,128)(2,1)S(1)} %add_convert_fusion), channel_id=1, source_target_pairs={{16,0},{20,4},{24,8},{28,12},{32,16},{36,20},{40,24},{44,28},{48,3... | collective-permute-start | bytes 3145736 | tf_op jit(solution)/shard_map/ppermute | solution.py:26
  271.9 48.6 %collective-permute-start.15 = (bf16[256,2048]{1,0:T(8,128)(2,1)S(1)}, bf16[256,2048]{1,0:T(8,128)(2,1)S(1)}, u32[]{:S(2)}, u32[]{:S(2)}) collective-permute-start(bf16[256,2048]{1,0:T(8,128)(2,1)S(1)} %copy-done.11), channel_id=1, source_target_pairs={{8,0},{12,4},{24,16},{28,20},{40,32},{44,36},{56,48},{60,52},{72,6... | collective-permute-start | bytes 3145736 | tf_op jit(solution)/shard_map/ppermute | solution.py:121
  273.2 2.3 copy-start.12
  273.2 4.2 %copy-start.10 = (bf16[256,2048]{1,0:T(8,128)(2,1)S(1)}, bf16[256,2048]{1,0:T(8,128)(2,1)}, u32[]{:S(2)}) copy-start(bf16[256,2048]{1,0:T(8,128)(2,1)} %get-tuple-element.24) | copy-start | bytes 3145732
  273.3 30.4 %copy-start.1 = (f32[256,2048]{1,0:T(8,128)S(1)}, f32[256,2048]{1,0:T(8,128)}, u32[]{:S(2)}) copy-start(f32[256,2048]{1,0:T(8,128)} %get-tuple-element.28) | copy-start | bytes 6291460
  275.5 45.0 %collective-permute-start.16 = (bf16[256,2048]{1,0:T(8,128)(2,1)S(1)}, bf16[256,2048]{1,0:T(8,128)(2,1)S(1)}, u32[]{:S(2)}, u32[]{:S(2)}) collective-permute-start(bf16[256,2048]{1,0:T(8,128)(2,1)S(1)} %copy-done.12), channel_id=1, source_target_pairs={{12,0},{16,4},{20,8},{24,12},{28,16},{32,20},{36,24},{40,28},{44,3... | collective-permute-start | bytes 3145736 | tf_op jit(solution)/shard_map/ppermute | solution.py:26
  277.5 43.1 %collective-permute-start.14 = (bf16[256,2048]{1,0:T(8,128)(2,1)S(1)}, bf16[256,2048]{1,0:T(8,128)(2,1)S(1)}, u32[]{:S(2)}, u32[]{:S(2)}) collective-permute-start(bf16[256,2048]{1,0:T(8,128)(2,1)S(1)} %copy-done.10), channel_id=1, source_target_pairs={{4,0},{8,4},{12,8},{20,16},{24,20},{28,24},{36,32},{40,36},{44,40}... | collective-permute-start | bytes 3145736 | tf_op jit(solution)/shard_map/ppermute | solution.py:121
  279.9 65.8 %collective-permute-start.19 = (bf16[256,2048]{1,0:T(8,128)(2,1)S(1)}, bf16[256,2048]{1,0:T(8,128)(2,1)S(1)}, u32[]{:S(2)}, u32[]{:S(2)}) collective-permute-start(bf16[256,2048]{1,0:T(8,128)(2,1)S(1)} %add_convert_fusion.1), channel_id=1, source_target_pairs={{16,0},{20,4},{24,8},{28,12},{32,16},{36,20},{40,24},{44,28},{48,3... | collective-permute-start | bytes 3145736 | tf_op jit(solution)/shard_map/ppermute | solution.py:26
  303.7 42.0 %copy-start = (f32[256,2048]{1,0:T(8,128)S(1)}, f32[256,2048]{1,0:T(8,128)}, u32[]{:S(2)}) copy-start(f32[256,2048]{1,0:T(8,128)} %get-tuple-element.23) | copy-start | bytes 6291460

commit v5 on v4

--- a/solution.py
+++ b/solution.py
@@ -14,7 +14,7 @@
 WINDOW = 1024
 HEADS_PER_STEP = 4
 ROW_DEVICES = 4
-PAIR_ORDER = (4, 1, 2, 3)
+PAIR_ORDER = (1, 3, 2, 4)
 
 
 score_scale = 168.0 ** (-0.5)
@@ -139,17 +139,18 @@
     kv = (stored_keys, stored_values)
     assert blocks == row
     far = passed_along(kv, "seq", blocks)
-    halos = {blocks: far}
-    for distance in range(1, blocks):
-        direct = sent_by(
-            kv, "seq", [(i, i + distance) for i in range(count) if i % row + distance < row]
-        )
-        relayed = sent_by(
-            far,
-            "seq",
-            [(i, i - row + distance) for i in range(row, count) if i % row >= row - distance],
-        )
-        halos[distance] = ((direct[0], relayed[0]), (direct[1], relayed[1]))
+    near1 = sent_by(kv, "seq", [(i, i + 1) for i in range(count) if i % row < row - 1])
+    relay1 = sent_by(far, "seq", [(i, i - row + 1) for i in range(row, count) if i % row == row - 1])
+    near3 = sent_by(kv, "seq", [(i, i + row - 1) for i in range(count) if i % row == 0])
+    relay3 = sent_by(far, "seq", [(i, i - 1) for i in range(row, count) if i % row >= 1])
+    fwd2a = sent_by(near1, "seq", [(i, i + 1) for i in range(count) if 1 <= i % row <= row - 2])
+    fwd2b = sent_by(relay3, "seq", [(i, i - 1) for i in range(row, count) if 1 <= i % row <= row - 2])
+    halos = {
+        blocks: far,
+        1: ((near1[0], relay1[0]), (near1[1], relay1[1])),
+        2: ((fwd2a[0], fwd2b[0]), (fwd2a[1], fwd2b[1])),
+        3: ((near3[0], relay3[0]), (near3[1], relay3[1])),
+    }
     limit = valid_count[0]
 
     delta = jnp.sum(
@@ -186,20 +187,9 @@
         if distance == blocks:
             far_part = (dk_part, dv_part)
             continue
-        if distance == PAIR_ORDER[-1]:
-            arrived = passed_along((dk_part, dv_part), "seq", -distance)
-            key_grad = key_grad + arrived[0].astype(jnp.float32)
-            value_grad = value_grad + arrived[1].astype(jnp.float32)
-            continue
-        arrived = sent_by(
-            (dk_part, dv_part), "seq", [(i, i - distance) for i in range(count) if i % row >= distance]
-        )
+        arrived = sent_by((dk_part, dv_part), "seq", [(i, i - distance) for i in range(count) if i % row >= distance])
         merged.append(
-            sent_by(
-                (dk_part, dv_part),
-                "seq",
-                [(i, i + row - distance) for i in range(count) if i % row < distance],
-            )
+            sent_by((dk_part, dv_part), "seq", [(i, i + row - distance) for i in range(count) if i % row < distance])
         )
         key_grad = key_grad + arrived[0].astype(jnp.float32)
         value_grad = value_grad + arrived[1].astype(jnp.float32)

time: 349 us -> 326 us (0.934)
  the two profiles are of different devices: /device:TPU:31 before, /device:TPU:50 now
where the time goes in v5:
time: 326 us; the launch traced here: 325 us
  waiting for transfers between devices  165 us (51%)
  Pallas kernels  71.3 us (22%)
  starting transfers between devices  64.7 us (20%)
  other arithmetic  18.4 us (6%)
  local copies, waits for them, and re-layouts  4.13 us (1%)
    ppermute x24, waiting for transfers between devices, sent_by(): return lax.ppermute(x, axis, pairs)  131 us
    pallas_call x5, Pallas kernels, pair_grads(): pl.pallas_call(functools.partial(pair_kernel, group, heads, accumulate, p...  71.3 us
    ppermute x24, starting transfers between devices, sent_by(): return lax.ppermute(x, axis, pairs)  53.6 us
    ppermute x4, waiting for transfers between devices, passed_along(): return lax.ppermute(x, axis, pairs)  33.4 us
    ppermute x4, starting transfers between devices, passed_along(): return lax.ppermute(x, axis, pairs)  11 us
  transfers between devices with their start and end apart: 28, of which 11 were waited for; matrix products, arithmetic and copies ran while one was open for 6% of the time, Pallas kernels for 22%

profile of v5, /device:TPU:50, one launch (start us, length us, event | category | flops | bytes accessed | tf_op | source)
XLA Modules:
  0.0 324.9 jit_solution(13888623585124607032)
XLA Ops:
  0.6 3.2 collective-permute-start
  3.8 4.0 %collective-permute-start.1 = (bf16[256,2048]{1,0:T(8,128)(2,1)}, bf16[256,2048]{1,0:T(8,128)(2,1)}, u32[]{:S(2)}, u32[]{:S(2)}) collective-permute-start(bf16[256,2048]{1,0:T(8,128)(2,1)} %refs_1_.1), channel_id=1, source_target_pairs={{0,16},{4,20},{8,24},{12,28},{16,32},{20,36},{24,40},{28,44},{32,4... | collective-permute-start | bytes 3145736 | tf_op jit(solution)/shard_map/ppermute | solution.py:26
  7.8 3.4 %collective-permute-start.2 = (bf16[256,2048]{1,0:T(8,128)(2,1)}, bf16[256,2048]{1,0:T(8,128)(2,1)S(1)}, u32[]{:S(2)}, u32[]{:S(2)}) collective-permute-start(bf16[256,2048]{1,0:T(8,128)(2,1)} %refs_0_.1), channel_id=1, source_target_pairs={{0,4},{4,8},{8,12},{16,20},{20,24},{24,28},{32,36},{36,40},{40,44}... | collective-permute-start | bytes 3145736 | tf_op jit(solution)/shard_map/ppermute | solution.py:121
  11.3 3.1 collective-permute-start.6
  14.4 1.7 collective-permute-start.10
  16.1 13.7 %collective-permute-done.refs_0_ = bf16[256,2048]{1,0:T(8,128)(2,1)} collective-permute-done((bf16[256,2048]{1,0:T(8,128)(2,1)}, bf16[256,2048]{1,0:T(8,128)(2,1)}, u32[]{:S(2)}, u32[]{:S(2)}) %collective-permute-start) | collective-permute-done | bytes 1048608 | tf_op jit(solution)/shard_map/ppermute | solution.py:26
  29.8 1.7 collective-permute-start.12
  31.4 19.7 %collective-permute-done.1.refs_1_ = bf16[256,2048]{1,0:T(8,128)(2,1)} collective-permute-done((bf16[256,2048]{1,0:T(8,128)(2,1)}, bf16[256,2048]{1,0:T(8,128)(2,1)}, u32[]{:S(2)}, u32[]{:S(2)}) %collective-permute-start.1) | collective-permute-done | bytes 1048608 | tf_op jit(solution)/shard_map/ppermute | solution.py:26
  51.1 1.6 collective-permute-start.13
  52.8 2.1 collective-permute-start.4
  54.9 1.9 collective-permute-done.6.refs_2_
  56.8 1.9 collective-permute-start.8
  59.9 1.6 collective-permute-start.11
  61.6 2.9 multiply_bitcast_fusion
  64.5 5.0 %collective-permute-start.3 = (bf16[256,2048]{1,0:T(8,128)(2,1)S(1)}, bf16[256,2048]{1,0:T(8,128)(2,1)}, u32[]{:S(2)}, u32[]{:S(2)}) collective-permute-start(bf16[256,2048]{1,0:T(8,128)(2,1)S(1)} %collective-permute-done.2.refs_0_), channel_id=1, source_target_pairs={{4,8},{8,12},{20,24},{24,28},{36,40},{40,44},{52,56},{56,60},{68,7... | collective-permute-start | bytes 3145736 | tf_op jit(solution)/shard_map/ppermute | solution.py:121
  69.5 4.0 %collective-permute-start.7 = (bf16[256,2048]{1,0:T(8,128)(2,1)S(1)}, bf16[256,2048]{1,0:T(8,128)(2,1)}, u32[]{:S(2)}, u32[]{:S(2)}) collective-permute-start(bf16[256,2048]{1,0:T(8,128)(2,1)S(1)} %collective-permute-done.6.refs_2_), channel_id=1, source_target_pairs={{4,8},{8,12},{20,24},{24,28},{36,40},{40,44},{52,56},{56,60},{68,7... | collective-permute-start | bytes 3145736 | tf_op jit(solution)/shard_map/ppermute | solution.py:121
  73.5 7.4 %collective-permute-done.4.refs_1_ = bf16[256,2048]{1,0:T(8,128)(2,1)S(1)} collective-permute-done((bf16[256,2048]{1,0:T(8,128)(2,1)}, bf16[256,2048]{1,0:T(8,128)(2,1)S(1)}, u32[]{:S(2)}, u32[]{:S(2)}) %collective-permute-start.4) | collective-permute-done | bytes 1048608 | tf_op jit(solution)/shard_map/ppermute | solution.py:121
  80.9 2.1 collective-permute-start.5
  83.0 20.5 %collective-permute-done.8.refs_3_ = bf16[256,2048]{1,0:T(8,128)(2,1)} collective-permute-done((bf16[256,2048]{1,0:T(8,128)(2,1)}, bf16[256,2048]{1,0:T(8,128)(2,1)}, u32[]{:S(2)}, u32[]{:S(2)}) %collective-permute-start.8) | collective-permute-done | bytes 1048608 | tf_op jit(solution)/shard_map/ppermute | solution.py:121
  103.5 2.1 collective-permute-start.9
  106.2 2.7 copy.15
  109.0 3.3 %reduce_sum.9 = f32[256,32]{1,0:T(8,128)S(1)} reduce(f32[256,32,128]{2,1,0:T(8,128)} %bitcast.9, f32[]{:T(128)} %constant.17.clone.1), dimensions={2}, to_apply=%region_0.0 | reduce | flops 1040384 | bytes 4227076 | tf_op jit(solution)/shard_map/reduce_sum | solution.py:156
  114.2 14.0 %shard_map.94 = (f32[256,4096]{1,0:T(8,128)}, f32[256,2048]{1,0:T(8,128)}, f32[256,2048]{1,0:T(8,128)}) custom-call(s32[3]{0:T(128)} %add_add_fusion.4.sc_ref, bf16[256,4096]{1,0:T(8,128)(2,1)} %q_ref.9, bf16[256,4096]{1,0:T(8,128)(2,1)} %do_ref.9, bf16[256,2048]{1,0:T(8,128)(2,1)} %refs_0_.1, bf16[256,2048]{1,0:T(8,128)(2,1)} %refs_1_.1, ...), custom_call_target="tpu_custom_call" | custom-call | flops 2684354560 | bytes 18874368 | tf_op jit(solution)/shard_map/pallas_call | solution.py:104
  128.2 14.4 %shard_map.95 = (f32[256,4096]{1,0:T(8,128)}, bf16[256,2048]{1,0:T(8,128)(2,1)}, bf16[256,2048]{1,0:T(8,128)(2,1)}) custom-call(s32[3]{0:T(128)} %add_add_fusion.3.sc_ref, bf16[256,4096]{1,0:T(8,128)(2,1)} %q_ref.9, bf16[256,4096]{1,0:T(8,128)(2,1)} %do_ref.9, bf16[256,2048]{1,0:T(8,128)(2,1)} %copy-done.3, ...), custom_call_target="tpu_custom_call", output_to_operand_aliasing={{0}: (9, {})} | custom-call | flops 2684354560 | bytes 20971520 | tf_op jit(solution)/shard_map/pallas_call | solution.py:104
  142.6 14.4 %shard_map.96 = (f32[256,4096]{1,0:T(8,128)}, bf16[256,2048]{1,0:T(8,128)(2,1)}, bf16[256,2048]{1,0:T(8,128)(2,1)}) custom-call(s32[3]{0:T(128)} %add_add_fusion.2.sc_ref, bf16[256,4096]{1,0:T(8,128)(2,1)} %q_ref.9, bf16[256,4096]{1,0:T(8,128)(2,1)} %do_ref.9, bf16[256,2048]{1,0:T(8,128)(2,1)} %collective-permute-done.10.refs_0_, ...), custom_call_target="tpu_custom_call", output_to_operand_aliasing={{0}: (9, {})} | custom-call | flops 2684354560 | bytes 20971520 | tf_op jit(solution)/shard_map/pallas_call | solution.py:104
  157.1 4.7 %collective-permute-start.25 = (bf16[256,2048]{1,0:T(8,128)(2,1)}, bf16[256,2048]{1,0:T(8,128)(2,1)}, u32[]{:S(2)}, u32[]{:S(2)}) collective-permute-start(bf16[256,2048]{1,0:T(8,128)(2,1)} %get-tuple-element.30), channel_id=1, source_target_pairs={{0,4},{4,8},{8,12},{16,20},{20,24},{24,28},{32,36},{36,40},{40,44}... | collective-permute-start | bytes 3145736 | tf_op jit(solution)/shard_map/ppermute | solution.py:121
  163.2 2.1 collective-permute-start.18
  165.3 14.4 %shard_map.97 = (f32[256,4096]{1,0:T(8,128)}, bf16[256,2048]{1,0:T(8,128)(2,1)}, bf16[256,2048]{1,0:T(8,128)(2,1)}) custom-call(s32[3]{0:T(128)} %add_add_fusion.1.sc_ref, bf16[256,4096]{1,0:T(8,128)(2,1)} %q_ref.9, bf16[256,4096]{1,0:T(8,128)(2,1)} %do_ref.9, bf16[256,2048]{1,0:T(8,128)(2,1)} %collective-permute-done.3.refs_0_, ...), custom_call_target="tpu_custom_call", output_to_operand_aliasing={{0}: (9, {})} | custom-call | flops 2684354560 | bytes 20971520 | tf_op jit(solution)/shard_map/pallas_call | solution.py:104
  179.7 2.3 collective-permute-start.26
  182.7 2.9 collective-permute-done.25
  185.6 4.9 %collective-permute-start.19 = (bf16[256,2048]{1,0:T(8,128)(2,1)}, bf16[256,2048]{1,0:T(8,128)(2,1)}, u32[]{:S(2)}, u32[]{:S(2)}) collective-permute-start(bf16[256,2048]{1,0:T(8,128)(2,1)} %get-tuple-element.26), channel_id=1, source_target_pairs={{0,8},{4,12},{16,24},{20,28},{32,40},{36,44},{48,56},{52,60},{64,7... | collective-permute-start | bytes 3145736 | tf_op jit(solution)/shard_map/ppermute | solution.py:121
  191.2 14.1 %shard_map.98 = (f32[256,4096]{1,0:T(8,128)}, bf16[256,2048]{1,0:T(8,128)(2,1)}, bf16[256,2048]{1,0:T(8,128)(2,1)}) custom-call(s32[3]{0:T(128)} %add_add_fusion.sc_ref, bf16[256,4096]{1,0:T(8,128)(2,1)} %q_ref.9, bf16[256,4096]{1,0:T(8,128)(2,1)} %do_ref.9, bf16[256,2048]{1,0:T(8,128)(2,1)} %collective-permute-done.refs_0_, ...), custom_call_target="tpu_custom_call", output_to_operand_aliasing={{0}: (7, {})} | custom-call | flops 2684354560 | bytes 18874368 | tf_op jit(solution)/shard_map/pallas_call | solution.py:104
  205.2 0.7 collective-permute-start.22
  206.0 41.9 %collective-permute-done.18 = bf16[256,2048]{1,0:T(8,128)(2,1)S(1)} collective-permute-done((bf16[256,2048]{1,0:T(8,128)(2,1)}, bf16[256,2048]{1,0:T(8,128)(2,1)S(1)}, u32[]{:S(2)}, u32[]{:S(2)}) %collective-permute-start.18) | collective-permute-done | bytes 1048608 | tf_op jit(solution)/shard_map/ppermute | solution.py:121
  247.9 1.9 collective-permute-start.21
  249.8 1.3 collective-permute-start.23
  251.2 2.7 add_convert_fusion
  253.9 1.9 collective-permute-start.27
  256.6 2.1 add_convert_fusion.1
  258.7 1.9 collective-permute-start.14
  260.6 11.9 %collective-permute-done.21 = bf16[256,2048]{1,0:T(8,128)(2,1)S(1)} collective-permute-done((bf16[256,2048]{1,0:T(8,128)(2,1)}, bf16[256,2048]{1,0:T(8,128)(2,1)S(1)}, u32[]{:S(2)}, u32[]{:S(2)}) %collective-permute-start.21) | collective-permute-done | bytes 1048608 | tf_op jit(solution)/shard_map/ppermute | solution.py:121
  272.5 1.3 collective-permute-start.16
  273.8 25.6 %collective-permute-done.23 = bf16[256,2048]{1,0:T(8,128)(2,1)S(1)} collective-permute-done((bf16[256,2048]{1,0:T(8,128)(2,1)}, bf16[256,2048]{1,0:T(8,128)(2,1)S(1)}, u32[]{:S(2)}, u32[]{:S(2)}) %collective-permute-start.23) | collective-permute-done | bytes 1048608 | tf_op jit(solution)/shard_map/ppermute | solution.py:121
  299.4 1.9 collective-permute-start.20
  301.4 2.1 convert_add_fusion
  303.5 2.8 collective-permute-done.14
  306.2 16.6 %collective-permute-done.16 = bf16[256,2048]{1,0:T(8,128)(2,1)S(1)} collective-permute-done((bf16[256,2048]{1,0:T(8,128)(2,1)S(1)}, bf16[256,2048]{1,0:T(8,128)(2,1)S(1)}, u32[]{:S(2)}, u32[]{:S(2)}) %collective-permute-start.16) | collective-permute-done | bytes 1048608 | tf_op jit(solution)/shard_map/ppermute | solution.py:121
  322.8 2.1 convert_add_fusion.1
  (48 shorter events, 6.7 us)
Async XLA Ops:
  0.6 29.1 %collective-permute-start = (bf16[256,2048]{1,0:T(8,128)(2,1)}, bf16[256,2048]{1,0:T(8,128)(2,1)}, u32[]{:S(2)}, u32[]{:S(2)}) collective-permute-start(bf16[256,2048]{1,0:T(8,128)(2,1)} %refs_0_.1), channel_id=1, source_target_pairs={{0,16},{4,20},{8,24},{12,28},{16,32},{20,36},{24,40},{28,44},{32,4... | collective-permute-start | bytes 3145736 | tf_op jit(solution)/shard_map/ppermute | solution.py:26
  3.8 47.3 %collective-permute-start.1 = (bf16[256,2048]{1,0:T(8,128)(2,1)}, bf16[256,2048]{1,0:T(8,128)(2,1)}, u32[]{:S(2)}, u32[]{:S(2)}) collective-permute-start(bf16[256,2048]{1,0:T(8,128)(2,1)} %refs_1_.1), channel_id=1, source_target_pairs={{0,16},{4,20},{8,24},{12,28},{16,32},{20,36},{24,40},{28,44},{32,4... | collective-permute-start | bytes 3145736 | tf_op jit(solution)/shard_map/ppermute | solution.py:26
  7.8 44.9 %collective-permute-start.2 = (bf16[256,2048]{1,0:T(8,128)(2,1)}, bf16[256,2048]{1,0:T(8,128)(2,1)S(1)}, u32[]{:S(2)}, u32[]{:S(2)}) collective-permute-start(bf16[256,2048]{1,0:T(8,128)(2,1)} %refs_0_.1), channel_id=1, source_target_pairs={{0,4},{4,8},{8,12},{16,20},{20,24},{24,28},{32,36},{36,40},{40,44}... | collective-permute-start | bytes 3145736 | tf_op jit(solution)/shard_map/ppermute | solution.py:121
  11.3 45.5 %collective-permute-start.6 = (bf16[256,2048]{1,0:T(8,128)(2,1)}, bf16[256,2048]{1,0:T(8,128)(2,1)S(1)}, u32[]{:S(2)}, u32[]{:S(2)}) collective-permute-start(bf16[256,2048]{1,0:T(8,128)(2,1)} %refs_1_.1), channel_id=1, source_target_pairs={{0,4},{4,8},{8,12},{16,20},{20,24},{24,28},{32,36},{36,40},{40,44}... | collective-permute-start | bytes 3145736 | tf_op jit(solution)/shard_map/ppermute | solution.py:121
  14.4 45.6 %collective-permute-start.10 = (bf16[256,2048]{1,0:T(8,128)(2,1)}, bf16[256,2048]{1,0:T(8,128)(2,1)}, u32[]{:S(2)}, u32[]{:S(2)}) collective-permute-start(bf16[256,2048]{1,0:T(8,128)(2,1)} %refs_0_.1), channel_id=1, source_target_pairs={{0,12},{16,28},{32,44},{48,60},{64,76},{80,92},{96,108},{112,124},... | collective-permute-start | bytes 3145736 | tf_op jit(solution)/shard_map/ppermute | solution.py:121
  29.8 34.7 %collective-permute-start.12 = (bf16[256,2048]{1,0:T(8,128)(2,1)}, bf16[256,2048]{1,0:T(8,128)(2,1)}, u32[]{:S(2)}, u32[]{:S(2)}) collective-permute-start(bf16[256,2048]{1,0:T(8,128)(2,1)} %collective-permute-done.refs_0_), channel_id=1, source_target_pairs={{28,16},{44,32},{60,48},{76,64},{92,80},{108,96},{124,112},{29,17}... | collective-permute-start | bytes 3145736 | tf_op jit(solution)/shard_map/ppermute | solution.py:121
  51.1 18.4 %collective-permute-start.13 = (bf16[256,2048]{1,0:T(8,128)(2,1)}, bf16[256,2048]{1,0:T(8,128)(2,1)}, u32[]{:S(2)}, u32[]{:S(2)}) collective-permute-start(bf16[256,2048]{1,0:T(8,128)(2,1)} %collective-permute-done.1.refs_1_), channel_id=1, source_target_pairs={{28,16},{44,32},{60,48},{76,64},{92,80},{108,96},{124,112},{29,17}... | collective-permute-start | bytes 3145736 | tf_op jit(solution)/shard_map/ppermute | solution.py:121
  52.8 11.8 %copy-start.3 = (bf16[256,2048]{1,0:T(8,128)(2,1)}, bf16[256,2048]{1,0:T(8,128)(2,1)S(1)}, u32[]{:S(2)}) copy-start(bf16[256,2048]{1,0:T(8,128)(2,1)S(1)} %collective-permute-done.2.refs_0_) | copy-start | bytes 3145732
  52.8 28.1 %collective-permute-start.4 = (bf16[256,2048]{1,0:T(8,128)(2,1)}, bf16[256,2048]{1,0:T(8,128)(2,1)S(1)}, u32[]{:S(2)}, u32[]{:S(2)}) collective-permute-start(bf16[256,2048]{1,0:T(8,128)(2,1)} %collective-permute-done.refs_0_), channel_id=1, source_target_pairs={{20,16},{24,20},{28,24},{36,32},{40,36},{44,40},{52,48},{56,52},{6... | collective-permute-start | bytes 3145736 | tf_op jit(solution)/shard_map/ppermute | solution.py:121
  56.8 12.8 %copy-start.2 = (bf16[256,2048]{1,0:T(8,128)(2,1)}, bf16[256,2048]{1,0:T(8,128)(2,1)S(1)}, u32[]{:S(2)}) copy-start(bf16[256,2048]{1,0:T(8,128)(2,1)S(1)} %collective-permute-done.6.refs_2_) | copy-start | bytes 3145732
  56.8 46.7 %collective-permute-start.8 = (bf16[256,2048]{1,0:T(8,128)(2,1)}, bf16[256,2048]{1,0:T(8,128)(2,1)}, u32[]{:S(2)}, u32[]{:S(2)}) collective-permute-start(bf16[256,2048]{1,0:T(8,128)(2,1)} %collective-permute-done.1.refs_1_), channel_id=1, source_target_pairs={{20,16},{24,20},{28,24},{36,32},{40,36},{44,40},{52,48},{56,52},{6... | collective-permute-start | bytes 3145736 | tf_op jit(solution)/shard_map/ppermute | solution.py:121
  59.9 82.7 %collective-permute-start.11 = (bf16[256,2048]{1,0:T(8,128)(2,1)}, bf16[256,2048]{1,0:T(8,128)(2,1)}, u32[]{:S(2)}, u32[]{:S(2)}) collective-permute-start(bf16[256,2048]{1,0:T(8,128)(2,1)} %refs_1_.1), channel_id=1, source_target_pairs={{0,12},{16,28},{32,44},{48,60},{64,76},{80,92},{96,108},{112,124},... | collective-permute-start | bytes 3145736 | tf_op jit(solution)/shard_map/ppermute | solution.py:121
  64.5 97.9 %collective-permute-start.3 = (bf16[256,2048]{1,0:T(8,128)(2,1)S(1)}, bf16[256,2048]{1,0:T(8,128)(2,1)}, u32[]{:S(2)}, u32[]{:S(2)}) collective-permute-start(bf16[256,2048]{1,0:T(8,128)(2,1)S(1)} %collective-permute-done.2.refs_0_), channel_id=1, source_target_pairs={{4,8},{8,12},{20,24},{24,28},{36,40},{40,44},{52,56},{56,60},{68,7... | collective-permute-start | bytes 3145736 | tf_op jit(solution)/shard_map/ppermute | solution.py:121
  69.5 93.6 %collective-permute-start.7 = (bf16[256,2048]{1,0:T(8,128)(2,1)S(1)}, bf16[256,2048]{1,0:T(8,128)(2,1)}, u32[]{:S(2)}, u32[]{:S(2)}) collective-permute-start(bf16[256,2048]{1,0:T(8,128)(2,1)S(1)} %collective-permute-done.6.refs_2_), channel_id=1, source_target_pairs={{4,8},{8,12},{20,24},{24,28},{36,40},{40,44},{52,56},{56,60},{68,7... | collective-permute-start | bytes 3145736 | tf_op jit(solution)/shard_map/ppermute | solution.py:121
  80.9 28.1 %copy-start.4 = (bf16[256,2048]{1,0:T(8,128)(2,1)}, bf16[256,2048]{1,0:T(8,128)(2,1)S(1)}, u32[]{:S(2)}) copy-start(bf16[256,2048]{1,0:T(8,128)(2,1)S(1)} %collective-permute-done.4.refs_1_) | copy-start | bytes 3145732
  80.9 84.4 %collective-permute-start.5 = (bf16[256,2048]{1,0:T(8,128)(2,1)S(1)}, bf16[256,2048]{1,0:T(8,128)(2,1)}, u32[]{:S(2)}, u32[]{:S(2)}) collective-permute-start(bf16[256,2048]{1,0:T(8,128)(2,1)S(1)} %collective-permute-done.4.refs_1_), channel_id=1, source_target_pairs={{20,16},{24,20},{36,32},{40,36},{52,48},{56,52},{68,64},{72,68},{8... | collective-permute-start | bytes 3145736 | tf_op jit(solution)/shard_map/ppermute | solution.py:121
  103.5 61.8 %collective-permute-start.9 = (bf16[256,2048]{1,0:T(8,128)(2,1)}, bf16[256,2048]{1,0:T(8,128)(2,1)}, u32[]{:S(2)}, u32[]{:S(2)}) collective-permute-start(bf16[256,2048]{1,0:T(8,128)(2,1)} %collective-permute-done.8.refs_3_), channel_id=1, source_target_pairs={{20,16},{24,20},{36,32},{40,36},{52,48},{56,52},{68,64},{72,68},{8... | collective-permute-start | bytes 3145736 | tf_op jit(solution)/shard_map/ppermute | solution.py:121
  109.0 4.1 %copy-start.6 = (f32[32,256]{1,0:T(8,128)S(1)}, f32[32,256]{1,0:T(8,128)}, u32[]{:S(2)}) copy-start(f32[32,256]{1,0:T(8,128)} %param.12) | copy-start | bytes 98308
  157.1 28.5 %collective-permute-start.25 = (bf16[256,2048]{1,0:T(8,128)(2,1)}, bf16[256,2048]{1,0:T(8,128)(2,1)}, u32[]{:S(2)}, u32[]{:S(2)}) collective-permute-start(bf16[256,2048]{1,0:T(8,128)(2,1)} %get-tuple-element.30), channel_id=1, source_target_pairs={{0,4},{4,8},{8,12},{16,20},{20,24},{24,28},{32,36},{36,40},{40,44}... | collective-permute-start | bytes 3145736 | tf_op jit(solution)/shard_map/ppermute | solution.py:121
  162.4 42.8 %collective-permute-start.24 = (bf16[256,2048]{1,0:T(8,128)(2,1)}, bf16[256,2048]{1,0:T(8,128)(2,1)S(1)}, u32[]{:S(2)}, u32[]{:S(2)}) collective-permute-start(bf16[256,2048]{1,0:T(8,128)(2,1)} %get-tuple-element.29), channel_id=1, source_target_pairs={{0,12},{16,28},{32,44},{48,60},{64,76},{80,92},{96,108},{112,124},... | collective-permute-start | bytes 3145736 | tf_op jit(solution)/shard_map/ppermute | solution.py:121
  163.2 84.8 %collective-permute-start.18 = (bf16[256,2048]{1,0:T(8,128)(2,1)}, bf16[256,2048]{1,0:T(8,128)(2,1)S(1)}, u32[]{:S(2)}, u32[]{:S(2)}) collective-permute-start(bf16[256,2048]{1,0:T(8,128)(2,1)} %get-tuple-element.25), channel_id=1, source_target_pairs={{0,4},{4,8},{8,12},{16,20},{20,24},{24,28},{32,36},{36,40},{40,44}... | collective-permute-start | bytes 3145736 | tf_op jit(solution)/shard_map/ppermute | solution.py:121
  179.7 70.1 %collective-permute-start.26 = (bf16[256,2048]{1,0:T(8,128)(2,1)}, bf16[256,2048]{1,0:T(8,128)(2,1)}, u32[]{:S(2)}, u32[]{:S(2)}) collective-permute-start(bf16[256,2048]{1,0:T(8,128)(2,1)} %get-tuple-element.31), channel_id=1, source_target_pairs={{0,8},{4,12},{16,24},{20,28},{32,40},{36,44},{48,56},{52,60},{64,7... | collective-permute-start | bytes 3145736 | tf_op jit(solution)/shard_map/ppermute | solution.py:121
  182.0 71.9 %collective-permute-start.17 = (bf16[256,2048]{1,0:T(8,128)(2,1)}, bf16[256,2048]{1,0:T(8,128)(2,1)S(1)}, u32[]{:S(2)}, u32[]{:S(2)}) collective-permute-start(bf16[256,2048]{1,0:T(8,128)(2,1)} %get-tuple-element.24), channel_id=1, source_target_pairs={{0,12},{16,28},{32,44},{48,60},{64,76},{80,92},{96,108},{112,124},... | collective-permute-start | bytes 3145736 | tf_op jit(solution)/shard_map/ppermute | solution.py:121
  185.6 70.2 %collective-permute-start.19 = (bf16[256,2048]{1,0:T(8,128)(2,1)}, bf16[256,2048]{1,0:T(8,128)(2,1)}, u32[]{:S(2)}, u32[]{:S(2)}) collective-permute-start(bf16[256,2048]{1,0:T(8,128)(2,1)} %get-tuple-element.26), channel_id=1, source_target_pairs={{0,8},{4,12},{16,24},{20,28},{32,40},{36,44},{48,56},{52,60},{64,7... | collective-permute-start | bytes 3145736 | tf_op jit(solution)/shard_map/ppermute | solution.py:121
  205.2 53.5 %collective-permute-start.22 = (bf16[256,2048]{1,0:T(8,128)(2,1)}, bf16[256,2048]{1,0:T(8,128)(2,1)S(1)}, u32[]{:S(2)}, u32[]{:S(2)}) collective-permute-start(bf16[256,2048]{1,0:T(8,128)(2,1)} %get-tuple-element.30), channel_id=1, source_target_pairs={{12,0},{28,16},{44,32},{60,48},{76,64},{92,80},{108,96},{124,112},... | collective-permute-start | bytes 3145736 | tf_op jit(solution)/shard_map/ppermute | solution.py:121
  247.9 24.6 %collective-permute-start.21 = (bf16[256,2048]{1,0:T(8,128)(2,1)}, bf16[256,2048]{1,0:T(8,128)(2,1)S(1)}, u32[]{:S(2)}, u32[]{:S(2)}) collective-permute-start(bf16[256,2048]{1,0:T(8,128)(2,1)} %get-tuple-element.29), channel_id=1, source_target_pairs={{4,0},{8,4},{12,8},{20,16},{24,20},{28,24},{36,32},{40,36},{44,40}... | collective-permute-start | bytes 3145736 | tf_op jit(solution)/shard_map/ppermute | solution.py:121
  249.8 49.6 %collective-permute-start.23 = (bf16[256,2048]{1,0:T(8,128)(2,1)}, bf16[256,2048]{1,0:T(8,128)(2,1)S(1)}, u32[]{:S(2)}, u32[]{:S(2)}) collective-permute-start(bf16[256,2048]{1,0:T(8,128)(2,1)} %get-tuple-element.31), channel_id=1, source_target_pairs={{8,0},{12,4},{24,16},{28,20},{40,32},{44,36},{56,48},{60,52},{72,6... | collective-permute-start | bytes 3145736 | tf_op jit(solution)/shard_map/ppermute | solution.py:121
  251.1 4.7 %copy-start.8 = (bf16[256,2048]{1,0:T(8,128)(2,1)S(1)}, bf16[256,2048]{1,0:T(8,128)(2,1)}, u32[]{:S(2)}) copy-start(bf16[256,2048]{1,0:T(8,128)(2,1)} %get-tuple-element.25) | copy-start | bytes 3145732
  251.1 5.4 %copy-start.5 = (bf16[256,2048]{1,0:T(8,128)(2,1)S(1)}, bf16[256,2048]{1,0:T(8,128)(2,1)}, u32[]{:S(2)}) copy-start(bf16[256,2048]{1,0:T(8,128)(2,1)} %get-tuple-element.27) | copy-start | bytes 3145732
  253.9 47.5 %collective-permute-start.27 = (bf16[256,2048]{1,0:T(8,128)(2,1)S(1)}, bf16[256,2048]{1,0:T(8,128)(2,1)S(1)}, u32[]{:S(2)}, u32[]{:S(2)}) collective-permute-start(bf16[256,2048]{1,0:T(8,128)(2,1)S(1)} %add_convert_fusion), channel_id=1, source_target_pairs={{16,0},{20,4},{24,8},{28,12},{32,16},{36,20},{40,24},{44,28},{48,3... | collective-permute-start | bytes 3145736 | tf_op jit(solution)/shard_map/ppermute | solution.py:26
  255.8 47.7 %collective-permute-start.15 = (bf16[256,2048]{1,0:T(8,128)(2,1)S(1)}, bf16[256,2048]{1,0:T(8,128)(2,1)S(1)}, u32[]{:S(2)}, u32[]{:S(2)}) collective-permute-start(bf16[256,2048]{1,0:T(8,128)(2,1)S(1)} %copy-done.8), channel_id=1, source_target_pairs={{12,0},{28,16},{44,32},{60,48},{76,64},{92,80},{108,96},{124,112},... | collective-permute-start | bytes 3145736 | tf_op jit(solution)/shard_map/ppermute | solution.py:121
  256.6 2.1 copy-start.7
  256.6 16.0 %copy-start.9 = (bf16[256,2048]{1,0:T(8,128)(2,1)S(1)}, bf16[256,2048]{1,0:T(8,128)(2,1)}, u32[]{:S(2)}) copy-start(bf16[256,2048]{1,0:T(8,128)(2,1)} %get-tuple-element.26) | copy-start | bytes 3145732
  256.6 44.8 %copy-start.1 = (f32[256,2048]{1,0:T(8,128)S(1)}, f32[256,2048]{1,0:T(8,128)}, u32[]{:S(2)}) copy-start(f32[256,2048]{1,0:T(8,128)} %get-tuple-element.28) | copy-start | bytes 6291460
  258.7 47.5 %collective-permute-start.14 = (bf16[256,2048]{1,0:T(8,128)(2,1)S(1)}, bf16[256,2048]{1,0:T(8,128)(2,1)S(1)}, u32[]{:S(2)}, u32[]{:S(2)}) collective-permute-start(bf16[256,2048]{1,0:T(8,128)(2,1)S(1)} %copy-done.7), channel_id=1, source_target_pairs={{4,0},{8,4},{12,8},{20,16},{24,20},{28,24},{36,32},{40,36},{44,40}... | collective-permute-start | bytes 3145736 | tf_op jit(solution)/shard_map/ppermute | solution.py:121
  272.5 50.3 %collective-permute-start.16 = (bf16[256,2048]{1,0:T(8,128)(2,1)S(1)}, bf16[256,2048]{1,0:T(8,128)(2,1)S(1)}, u32[]{:S(2)}, u32[]{:S(2)}) collective-permute-start(bf16[256,2048]{1,0:T(8,128)(2,1)S(1)} %copy-done.9), channel_id=1, source_target_pairs={{8,0},{12,4},{24,16},{28,20},{40,32},{44,36},{56,48},{60,52},{72,6... | collective-permute-start | bytes 3145736 | tf_op jit(solution)/shard_map/ppermute | solution.py:121
  299.4 23.4 %collective-permute-start.20 = (bf16[256,2048]{1,0:T(8,128)(2,1)S(1)}, bf16[256,2048]{1,0:T(8,128)(2,1)S(1)}, u32[]{:S(2)}, u32[]{:S(2)}) collective-permute-start(bf16[256,2048]{1,0:T(8,128)(2,1)S(1)} %add_convert_fusion.1), channel_id=1, source_target_pairs={{16,0},{20,4},{24,8},{28,12},{32,16},{36,20},{40,24},{44,28},{48,3... | collective-permute-start | bytes 3145736 | tf_op jit(solution)/shard_map/ppermute | solution.py:26
  301.4 21.5 %copy-start = (f32[256,2048]{1,0:T(8,128)S(1)}, f32[256,2048]{1,0:T(8,128)}, u32[]{:S(2)}) copy-start(f32[256,2048]{1,0:T(8,128)} %get-tuple-element.23) | copy-start | bytes 6291460

commit v6 on v5

--- a/solution.py
+++ b/solution.py
@@ -187,12 +187,17 @@
         if distance == blocks:
             far_part = (dk_part, dv_part)
             continue
-        arrived = sent_by((dk_part, dv_part), "seq", [(i, i - distance) for i in range(count) if i % row >= distance])
-        merged.append(
-            sent_by((dk_part, dv_part), "seq", [(i, i + row - distance) for i in range(count) if i % row < distance])
+        got = sent_by(
+            (dk_part, dv_part),
+            "seq",
+            [(i, i - distance) if i % row >= distance else (i, i + row - distance) for i in range(count)
+             if (i - distance >= 0 if i % row >= distance else i + row - distance < count)],
         )
-        key_grad = key_grad + arrived[0].astype(jnp.float32)
-        value_grad = value_grad + arrived[1].astype(jnp.float32)
+        direct = shard % row + distance < row
+        zero = jnp.zeros((), jnp.bfloat16)
+        merged.append((jnp.where(direct, zero, got[0]), jnp.where(direct, zero, got[1])))
+        key_grad = key_grad + jnp.where(direct, got[0], zero).astype(jnp.float32)
+        value_grad = value_grad + jnp.where(direct, got[1], zero).astype(jnp.float32)
     dk_far = far_part[0].astype(jnp.float32)
     dv_far = far_part[1].astype(jnp.float32)
     for part in merged:

time: 326 us -> 276 us (0.85)
  the two profiles are of different devices: /device:TPU:50 before, /device:TPU:28 now
where the time goes in v6:
time: 276 us
  waiting for transfers between devices  128 us (46%)
  Pallas kernels  71.3 us (26%)
  starting transfers between devices  51.6 us (19%)
  other arithmetic  19.4 us (7%)
  local copies, waits for them, and re-layouts  4.1 us (1%)
    ppermute x18, waiting for transfers between devices, sent_by(): return lax.ppermute(x, axis, pairs)  72.8 us
    pallas_call x5, Pallas kernels, pair_grads(): pl.pallas_call(functools.partial(pair_kernel, group, heads, accumulate, p...  71.3 us
    ppermute x4, waiting for transfers between devices, passed_along(): return lax.ppermute(x, axis, pairs)  54.9 us
    ppermute x18, starting transfers between devices, sent_by(): return lax.ppermute(x, axis, pairs)  40.6 us
    ppermute x4, starting transfers between devices, passed_along(): return lax.ppermute(x, axis, pairs)  11 us
  transfers between devices with their start and end apart: 22, of which 8 were waited for; matrix products, arithmetic and copies ran while one was open for 7% of the time, Pallas kernels for 26%

profile of v6, /device:TPU:28, one launch (start us, length us, event | category | flops | bytes accessed | tf_op | source)
XLA Modules:
  0.0 275.7 jit_solution(2212069593631111663)
XLA Ops:
  0.6 4.0 %collective-permute-start = (bf16[256,2048]{1,0:T(8,128)(2,1)}, bf16[256,2048]{1,0:T(8,128)(2,1)}, u32[]{:S(2)}, u32[]{:S(2)}) collective-permute-start(bf16[256,2048]{1,0:T(8,128)(2,1)} %refs_0_.1), channel_id=1, source_target_pairs={{0,16},{4,20},{8,24},{12,28},{16,32},{20,36},{24,40},{28,44},{32,4... | collective-permute-start | bytes 3145736 | tf_op jit(solution)/shard_map/ppermute | solution.py:26
  4.6 3.2 %collective-permute-start.1 = (bf16[256,2048]{1,0:T(8,128)(2,1)}, bf16[256,2048]{1,0:T(8,128)(2,1)}, u32[]{:S(2)}, u32[]{:S(2)}) collective-permute-start(bf16[256,2048]{1,0:T(8,128)(2,1)} %refs_1_.1), channel_id=1, source_target_pairs={{0,16},{4,20},{8,24},{12,28},{16,32},{20,36},{24,40},{28,44},{32,4... | collective-permute-start | bytes 3145736 | tf_op jit(solution)/shard_map/ppermute | solution.py:26
  7.8 3.1 %collective-permute-start.2 = (bf16[256,2048]{1,0:T(8,128)(2,1)}, bf16[256,2048]{1,0:T(8,128)(2,1)S(1)}, u32[]{:S(2)}, u32[]{:S(2)}) collective-permute-start(bf16[256,2048]{1,0:T(8,128)(2,1)} %refs_0_.1), channel_id=1, source_target_pairs={{0,4},{4,8},{8,12},{16,20},{20,24},{24,28},{32,36},{36,40},{40,44}... | collective-permute-start | bytes 3145736 | tf_op jit(solution)/shard_map/ppermute | solution.py:121
  11.0 1.9 collective-permute-start.6
  12.9 0.7 collective-permute-start.10
  13.6 15.2 %collective-permute-done.refs_0_ = bf16[256,2048]{1,0:T(8,128)(2,1)} collective-permute-done((bf16[256,2048]{1,0:T(8,128)(2,1)}, bf16[256,2048]{1,0:T(8,128)(2,1)}, u32[]{:S(2)}, u32[]{:S(2)}) %collective-permute-start) | collective-permute-done | bytes 1048608 | tf_op jit(solution)/shard_map/ppermute | solution.py:26
  28.9 1.7 collective-permute-start.12
  30.5 19.7 %collective-permute-done.1.refs_1_ = bf16[256,2048]{1,0:T(8,128)(2,1)} collective-permute-done((bf16[256,2048]{1,0:T(8,128)(2,1)}, bf16[256,2048]{1,0:T(8,128)(2,1)}, u32[]{:S(2)}, u32[]{:S(2)}) %collective-permute-start.1) | collective-permute-done | bytes 1048608 | tf_op jit(solution)/shard_map/ppermute | solution.py:26
  50.2 1.7 collective-permute-start.13
  51.9 2.4 collective-permute-start.4
  54.3 2.5 collective-permute-done.6.refs_2_
  56.8 2.4 collective-permute-start.8
  59.9 0.6 add_add_fusion.4.sc_ref
  60.5 1.7 collective-permute-start.11
  62.1 2.9 %multiply_bitcast_fusion = f32[32,8,32,128]{3,1,2,0:T(8,128)S(1)} fusion(bf16[256,4096]{1,0:T(8,128)(2,1)} %param.10, bf16[256,4096]{1,0:T(8,128)(2,1)} %do_ref.9), kind=kLoop, calls=%fused_computation | loop fusion | flops 3145728 | bytes 8388608
  65.1 4.0 %collective-permute-start.3 = (bf16[256,2048]{1,0:T(8,128)(2,1)S(1)}, bf16[256,2048]{1,0:T(8,128)(2,1)}, u32[]{:S(2)}, u32[]{:S(2)}) collective-permute-start(bf16[256,2048]{1,0:T(8,128)(2,1)S(1)} %collective-permute-done.2.refs_0_), channel_id=1, source_target_pairs={{4,8},{8,12},{20,24},{24,28},{36,40},{40,44},{52,56},{56,60},{68,7... | collective-permute-start | bytes 3145736 | tf_op jit(solution)/shard_map/ppermute | solution.py:121
  69.1 8.4 %collective-permute-start.7 = (bf16[256,2048]{1,0:T(8,128)(2,1)S(1)}, bf16[256,2048]{1,0:T(8,128)(2,1)}, u32[]{:S(2)}, u32[]{:S(2)}) collective-permute-start(bf16[256,2048]{1,0:T(8,128)(2,1)S(1)} %collective-permute-done.6.refs_2_), channel_id=1, source_target_pairs={{4,8},{8,12},{20,24},{24,28},{36,40},{40,44},{52,56},{56,60},{68,7... | collective-permute-start | bytes 3145736 | tf_op jit(solution)/shard_map/ppermute | solution.py:121
  77.6 2.8 %collective-permute-done.4.refs_1_ = bf16[256,2048]{1,0:T(8,128)(2,1)} collective-permute-done((bf16[256,2048]{1,0:T(8,128)(2,1)}, bf16[256,2048]{1,0:T(8,128)(2,1)}, u32[]{:S(2)}, u32[]{:S(2)}) %collective-permute-start.4) | collective-permute-done | bytes 1048608 | tf_op jit(solution)/shard_map/ppermute | solution.py:121
  80.4 3.2 %collective-permute-start.5 = (bf16[256,2048]{1,0:T(8,128)(2,1)}, bf16[256,2048]{1,0:T(8,128)(2,1)}, u32[]{:S(2)}, u32[]{:S(2)}) collective-permute-start(bf16[256,2048]{1,0:T(8,128)(2,1)} %collective-permute-done.4.refs_1_), channel_id=1, source_target_pairs={{20,16},{24,20},{36,32},{40,36},{52,48},{56,52},{68,64},{72,68},{8... | collective-permute-start | bytes 3145736 | tf_op jit(solution)/shard_map/ppermute | solution.py:121
  83.6 17.3 %collective-permute-done.8.refs_3_ = bf16[256,2048]{1,0:T(8,128)(2,1)} collective-permute-done((bf16[256,2048]{1,0:T(8,128)(2,1)}, bf16[256,2048]{1,0:T(8,128)(2,1)}, u32[]{:S(2)}, u32[]{:S(2)}) %collective-permute-start.8) | collective-permute-done | bytes 1048608 | tf_op jit(solution)/shard_map/ppermute | solution.py:121
  100.9 5.1 %collective-permute-start.9 = (bf16[256,2048]{1,0:T(8,128)(2,1)}, bf16[256,2048]{1,0:T(8,128)(2,1)}, u32[]{:S(2)}, u32[]{:S(2)}) collective-permute-start(bf16[256,2048]{1,0:T(8,128)(2,1)} %collective-permute-done.8.refs_3_), channel_id=1, source_target_pairs={{20,16},{24,20},{36,32},{40,36},{52,48},{56,52},{68,64},{72,68},{8... | collective-permute-start | bytes 3145736 | tf_op jit(solution)/shard_map/ppermute | solution.py:121
  106.0 0.6 add_add_fusion.3.sc_ref
  106.6 2.7 copy.15
  109.3 3.3 %reduce_sum.9 = f32[256,32]{1,0:T(8,128)S(1)} reduce(f32[256,32,128]{2,1,0:T(8,128)} %bitcast.9, f32[]{:T(128)} %constant.35.clone.1), dimensions={2}, to_apply=%region_0.0 | reduce | flops 1040384 | bytes 4227076 | tf_op jit(solution)/shard_map/reduce_sum | solution.py:156
  112.7 0.1 copy.14
  112.7 0.6 reshape.17.refs_3_.refs_5_
  113.4 0.6 reshape.15.refs_2_.refs_4_
  114.0 0.6 add_add_fusion.2.sc_ref
  114.5 14.0 %shard_map.94 = (f32[256,4096]{1,0:T(8,128)}, f32[256,2048]{1,0:T(8,128)}, f32[256,2048]{1,0:T(8,128)}) custom-call(s32[3]{0:T(128)} %add_add_fusion.4.sc_ref, bf16[256,4096]{1,0:T(8,128)(2,1)} %q_ref.9, bf16[256,4096]{1,0:T(8,128)(2,1)} %do_ref.9, bf16[256,2048]{1,0:T(8,128)(2,1)} %refs_0_.1, bf16[256,2048]{1,0:T(8,128)(2,1)} %refs_1_.1, ...), custom_call_target="tpu_custom_call" | custom-call | flops 2684354560 | bytes 18874368 | tf_op jit(solution)/shard_map/pallas_call | solution.py:104
  128.5 14.4 %shard_map.95 = (f32[256,4096]{1,0:T(8,128)}, bf16[256,2048]{1,0:T(8,128)(2,1)}, bf16[256,2048]{1,0:T(8,128)(2,1)}) custom-call(s32[3]{0:T(128)} %add_add_fusion.3.sc_ref, bf16[256,4096]{1,0:T(8,128)(2,1)} %q_ref.9, bf16[256,4096]{1,0:T(8,128)(2,1)} %do_ref.9, bf16[256,2048]{1,0:T(8,128)(2,1)} %copy-done.3, ...), custom_call_target="tpu_custom_call", output_to_operand_aliasing={{0}: (9, {})} | custom-call | flops 2684354560 | bytes 20971520 | tf_op jit(solution)/shard_map/pallas_call | solution.py:104
  142.9 14.4 %shard_map.96 = (f32[256,4096]{1,0:T(8,128)}, bf16[256,2048]{1,0:T(8,128)(2,1)}, bf16[256,2048]{1,0:T(8,128)(2,1)}) custom-call(s32[3]{0:T(128)} %add_add_fusion.2.sc_ref, bf16[256,4096]{1,0:T(8,128)(2,1)} %q_ref.9, bf16[256,4096]{1,0:T(8,128)(2,1)} %do_ref.9, bf16[256,2048]{1,0:T(8,128)(2,1)} %copy-done.4, ...), custom_call_target="tpu_custom_call", output_to_operand_aliasing={{0}: (9, {})} | custom-call | flops 2684354560 | bytes 20971520 | tf_op jit(solution)/shard_map/pallas_call | solution.py:104
  157.4 0.1 collective-permute-start.19
  157.5 0.6 add_add_fusion.1.sc_ref
  158.1 2.0 collective-permute-start.18
  160.1 14.4 %shard_map.97 = (f32[256,4096]{1,0:T(8,128)}, bf16[256,2048]{1,0:T(8,128)(2,1)}, bf16[256,2048]{1,0:T(8,128)(2,1)}) custom-call(s32[3]{0:T(128)} %add_add_fusion.1.sc_ref, bf16[256,4096]{1,0:T(8,128)(2,1)} %q_ref.9, bf16[256,4096]{1,0:T(8,128)(2,1)} %do_ref.9, bf16[256,2048]{1,0:T(8,128)(2,1)} %collective-permute-done.3.refs_0_, ...), custom_call_target="tpu_custom_call", output_to_operand_aliasing={{0}: (9, {})} | custom-call | flops 2684354560 | bytes 20971520 | tf_op jit(solution)/shard_map/pallas_call | solution.py:104
  174.5 0.1 collective-permute-start.20
  174.6 2.1 collective-permute-start.15
  176.7 29.4 %collective-permute-done.19 = bf16[256,2048]{1,0:T(8,128)(2,1)S(1)} collective-permute-done((bf16[256,2048]{1,0:T(8,128)(2,1)}, bf16[256,2048]{1,0:T(8,128)(2,1)S(1)}, u32[]{:S(2)}, u32[]{:S(2)}) %collective-permute-start.19) | collective-permute-done | bytes 1048608 | tf_op jit(solution)/shard_map/ppermute | solution.py:121
  206.2 0.6 add_add_fusion.sc_ref
  206.8 14.1 %shard_map.98 = (f32[256,4096]{1,0:T(8,128)}, bf16[256,2048]{1,0:T(8,128)(2,1)}, bf16[256,2048]{1,0:T(8,128)(2,1)}) custom-call(s32[3]{0:T(128)} %add_add_fusion.sc_ref, bf16[256,4096]{1,0:T(8,128)(2,1)} %q_ref.9, bf16[256,4096]{1,0:T(8,128)(2,1)} %do_ref.9, bf16[256,2048]{1,0:T(8,128)(2,1)} %collective-permute-done.refs_0_, ...), custom_call_target="tpu_custom_call", output_to_operand_aliasing={{0}: (7, {})} | custom-call | flops 2684354560 | bytes 18874368 | tf_op jit(solution)/shard_map/pallas_call | solution.py:104
  220.9 2.4 add_convert_fusion
  223.3 1.9 collective-permute-start.21
  225.2 20.8 %collective-permute-done.15 = bf16[256,2048]{1,0:T(8,128)(2,1)S(1)} collective-permute-done((bf16[256,2048]{1,0:T(8,128)(2,1)}, bf16[256,2048]{1,0:T(8,128)(2,1)S(1)}, u32[]{:S(2)}, u32[]{:S(2)}) %collective-permute-start.15) | collective-permute-done | bytes 1048608 | tf_op jit(solution)/shard_map/ppermute | solution.py:121
  246.0 2.2 add_convert_fusion.1
  248.2 1.9 collective-permute-start.17
  250.2 2.2 convert_add_fusion
  252.3 20.0 %collective-permute-done.17 = bf16[256,2048]{1,0:T(8,128)(2,1)S(1)} collective-permute-done((bf16[256,2048]{1,0:T(8,128)(2,1)S(1)}, bf16[256,2048]{1,0:T(8,128)(2,1)S(1)}, u32[]{:S(2)}, u32[]{:S(2)}) %collective-permute-start.17) | collective-permute-done | bytes 1048608 | tf_op jit(solution)/shard_map/ppermute | solution.py:26
  272.3 3.4 %convert_add_fusion.1 = f32[256,2048]{1,0:T(8,128)} fusion(bf16[256,2048]{1,0:T(8,128)(2,1)S(1)} %collective-permute-done.17, f32[256,2048]{1,0:T(8,128)S(1)} %copy-done, bf16[256,2048]{1,0:T(8,128)(2,1)} %collective-permute-done.16, bf16[256,2048]{1,0:T(8,128)(2,1)S(1)} %collective-permute-done.15, bf16[256,2048]{1,0:T(8,128)(2,1)} %collective-permute-done.14, ...), kind=kLoop, calls=%fused_computation.3 | loop fusion | flops 5767168 | bytes 8388611 | tf_op jit(solution)/shard_map/add | solution.py:207
  (30 shorter events, 0.1 us)
Async XLA Ops:
  0.6 28.2 %collective-permute-start = (bf16[256,2048]{1,0:T(8,128)(2,1)}, bf16[256,2048]{1,0:T(8,128)(2,1)}, u32[]{:S(2)}, u32[]{:S(2)}) collective-permute-start(bf16[256,2048]{1,0:T(8,128)(2,1)} %refs_0_.1), channel_id=1, source_target_pairs={{0,16},{4,20},{8,24},{12,28},{16,32},{20,36},{24,40},{28,44},{32,4... | collective-permute-start | bytes 3145736 | tf_op jit(solution)/shard_map/ppermute | solution.py:26
  4.6 45.6 %collective-permute-start.1 = (bf16[256,2048]{1,0:T(8,128)(2,1)}, bf16[256,2048]{1,0:T(8,128)(2,1)}, u32[]{:S(2)}, u32[]{:S(2)}) collective-permute-start(bf16[256,2048]{1,0:T(8,128)(2,1)} %refs_1_.1), channel_id=1, source_target_pairs={{0,16},{4,20},{8,24},{12,28},{16,32},{20,36},{24,40},{28,44},{32,4... | collective-permute-start | bytes 3145736 | tf_op jit(solution)/shard_map/ppermute | solution.py:26
  7.8 44.0 %collective-permute-start.2 = (bf16[256,2048]{1,0:T(8,128)(2,1)}, bf16[256,2048]{1,0:T(8,128)(2,1)S(1)}, u32[]{:S(2)}, u32[]{:S(2)}) collective-permute-start(bf16[256,2048]{1,0:T(8,128)(2,1)} %refs_0_.1), channel_id=1, source_target_pairs={{0,4},{4,8},{8,12},{16,20},{20,24},{24,28},{32,36},{36,40},{40,44}... | collective-permute-start | bytes 3145736 | tf_op jit(solution)/shard_map/ppermute | solution.py:121
  11.0 45.8 %collective-permute-start.6 = (bf16[256,2048]{1,0:T(8,128)(2,1)}, bf16[256,2048]{1,0:T(8,128)(2,1)S(1)}, u32[]{:S(2)}, u32[]{:S(2)}) collective-permute-start(bf16[256,2048]{1,0:T(8,128)(2,1)} %refs_1_.1), channel_id=1, source_target_pairs={{0,4},{4,8},{8,12},{16,20},{20,24},{24,28},{32,36},{36,40},{40,44}... | collective-permute-start | bytes 3145736 | tf_op jit(solution)/shard_map/ppermute | solution.py:121
  12.9 47.6 %collective-permute-start.10 = (bf16[256,2048]{1,0:T(8,128)(2,1)}, bf16[256,2048]{1,0:T(8,128)(2,1)S(1)}, u32[]{:S(2)}, u32[]{:S(2)}) collective-permute-start(bf16[256,2048]{1,0:T(8,128)(2,1)} %refs_0_.1), channel_id=1, source_target_pairs={{0,12},{16,28},{32,44},{48,60},{64,76},{80,92},{96,108},{112,124},... | collective-permute-start | bytes 3145736 | tf_op jit(solution)/shard_map/ppermute | solution.py:121
  28.9 36.2 %collective-permute-start.12 = (bf16[256,2048]{1,0:T(8,128)(2,1)}, bf16[256,2048]{1,0:T(8,128)(2,1)}, u32[]{:S(2)}, u32[]{:S(2)}) collective-permute-start(bf16[256,2048]{1,0:T(8,128)(2,1)} %collective-permute-done.refs_0_), channel_id=1, source_target_pairs={{28,16},{44,32},{60,48},{76,64},{92,80},{108,96},{124,112},{29,17}... | collective-permute-start | bytes 3145736 | tf_op jit(solution)/shard_map/ppermute | solution.py:121
  50.2 18.9 %collective-permute-start.13 = (bf16[256,2048]{1,0:T(8,128)(2,1)}, bf16[256,2048]{1,0:T(8,128)(2,1)}, u32[]{:S(2)}, u32[]{:S(2)}) collective-permute-start(bf16[256,2048]{1,0:T(8,128)(2,1)} %collective-permute-done.1.refs_1_), channel_id=1, source_target_pairs={{28,16},{44,32},{60,48},{76,64},{92,80},{108,96},{124,112},{29,17}... | collective-permute-start | bytes 3145736 | tf_op jit(solution)/shard_map/ppermute | solution.py:121
  51.9 13.2 %copy-start.3 = (bf16[256,2048]{1,0:T(8,128)(2,1)}, bf16[256,2048]{1,0:T(8,128)(2,1)S(1)}, u32[]{:S(2)}) copy-start(bf16[256,2048]{1,0:T(8,128)(2,1)S(1)} %collective-permute-done.2.refs_0_) | copy-start | bytes 3145732
  51.9 28.5 %collective-permute-start.4 = (bf16[256,2048]{1,0:T(8,128)(2,1)}, bf16[256,2048]{1,0:T(8,128)(2,1)}, u32[]{:S(2)}, u32[]{:S(2)}) collective-permute-start(bf16[256,2048]{1,0:T(8,128)(2,1)} %collective-permute-done.refs_0_), channel_id=1, source_target_pairs={{20,16},{24,20},{28,24},{36,32},{40,36},{44,40},{52,48},{56,52},{6... | collective-permute-start | bytes 3145736 | tf_op jit(solution)/shard_map/ppermute | solution.py:121
  56.8 12.4 %copy-start.2 = (bf16[256,2048]{1,0:T(8,128)(2,1)}, bf16[256,2048]{1,0:T(8,128)(2,1)S(1)}, u32[]{:S(2)}) copy-start(bf16[256,2048]{1,0:T(8,128)(2,1)S(1)} %collective-permute-done.6.refs_2_) | copy-start | bytes 3145732
  56.8 44.1 %collective-permute-start.8 = (bf16[256,2048]{1,0:T(8,128)(2,1)}, bf16[256,2048]{1,0:T(8,128)(2,1)}, u32[]{:S(2)}, u32[]{:S(2)}) collective-permute-start(bf16[256,2048]{1,0:T(8,128)(2,1)} %collective-permute-done.1.refs_1_), channel_id=1, source_target_pairs={{20,16},{24,20},{28,24},{36,32},{40,36},{44,40},{52,48},{56,52},{6... | collective-permute-start | bytes 3145736 | tf_op jit(solution)/shard_map/ppermute | solution.py:121
  60.5 4.6 %copy-start.4 = (bf16[256,2048]{1,0:T(8,128)(2,1)}, bf16[256,2048]{1,0:T(8,128)(2,1)S(1)}, u32[]{:S(2)}) copy-start(bf16[256,2048]{1,0:T(8,128)(2,1)S(1)} %collective-permute-done.10.refs_0_) | copy-start | bytes 3145732
  60.5 82.5 %collective-permute-start.11 = (bf16[256,2048]{1,0:T(8,128)(2,1)}, bf16[256,2048]{1,0:T(8,128)(2,1)}, u32[]{:S(2)}, u32[]{:S(2)}) collective-permute-start(bf16[256,2048]{1,0:T(8,128)(2,1)} %refs_1_.1), channel_id=1, source_target_pairs={{0,12},{16,28},{32,44},{48,60},{64,76},{80,92},{96,108},{112,124},... | collective-permute-start | bytes 3145736 | tf_op jit(solution)/shard_map/ppermute | solution.py:121
  65.1 93.0 %collective-permute-start.3 = (bf16[256,2048]{1,0:T(8,128)(2,1)S(1)}, bf16[256,2048]{1,0:T(8,128)(2,1)}, u32[]{:S(2)}, u32[]{:S(2)}) collective-permute-start(bf16[256,2048]{1,0:T(8,128)(2,1)S(1)} %collective-permute-done.2.refs_0_), channel_id=1, source_target_pairs={{4,8},{8,12},{20,24},{24,28},{36,40},{40,44},{52,56},{56,60},{68,7... | collective-permute-start | bytes 3145736 | tf_op jit(solution)/shard_map/ppermute | solution.py:121
  69.1 91.0 %collective-permute-start.7 = (bf16[256,2048]{1,0:T(8,128)(2,1)S(1)}, bf16[256,2048]{1,0:T(8,128)(2,1)}, u32[]{:S(2)}, u32[]{:S(2)}) collective-permute-start(bf16[256,2048]{1,0:T(8,128)(2,1)S(1)} %collective-permute-done.6.refs_2_), channel_id=1, source_target_pairs={{4,8},{8,12},{20,24},{24,28},{36,40},{40,44},{52,56},{56,60},{68,7... | collective-permute-start | bytes 3145736 | tf_op jit(solution)/shard_map/ppermute | solution.py:121
  80.4 79.7 %collective-permute-start.5 = (bf16[256,2048]{1,0:T(8,128)(2,1)}, bf16[256,2048]{1,0:T(8,128)(2,1)}, u32[]{:S(2)}, u32[]{:S(2)}) collective-permute-start(bf16[256,2048]{1,0:T(8,128)(2,1)} %collective-permute-done.4.refs_1_), channel_id=1, source_target_pairs={{20,16},{24,20},{36,32},{40,36},{52,48},{56,52},{68,64},{72,68},{8... | collective-permute-start | bytes 3145736 | tf_op jit(solution)/shard_map/ppermute | solution.py:121
  100.9 59.2 %collective-permute-start.9 = (bf16[256,2048]{1,0:T(8,128)(2,1)}, bf16[256,2048]{1,0:T(8,128)(2,1)}, u32[]{:S(2)}, u32[]{:S(2)}) collective-permute-start(bf16[256,2048]{1,0:T(8,128)(2,1)} %collective-permute-done.8.refs_3_), channel_id=1, source_target_pairs={{20,16},{24,20},{36,32},{40,36},{52,48},{56,52},{68,64},{72,68},{8... | collective-permute-start | bytes 3145736 | tf_op jit(solution)/shard_map/ppermute | solution.py:121
  109.3 4.1 %copy-start.6 = (f32[32,256]{1,0:T(8,128)S(1)}, f32[32,256]{1,0:T(8,128)}, u32[]{:S(2)}) copy-start(f32[32,256]{1,0:T(8,128)} %param.12) | copy-start | bytes 98308
  157.4 48.8 %collective-permute-start.19 = (bf16[256,2048]{1,0:T(8,128)(2,1)}, bf16[256,2048]{1,0:T(8,128)(2,1)S(1)}, u32[]{:S(2)}, u32[]{:S(2)}) collective-permute-start(bf16[256,2048]{1,0:T(8,128)(2,1)} %get-tuple-element.30), channel_id=1, source_target_pairs={{0,4},{4,8},{8,12},{12,0},{16,20},{20,24},{24,28},{28,16},{32,36},... | collective-permute-start | bytes 3145736 | tf_op jit(solution)/shard_map/ppermute | solution.py:121
  158.1 62.8 %collective-permute-start.18 = (bf16[256,2048]{1,0:T(8,128)(2,1)}, bf16[256,2048]{1,0:T(8,128)(2,1)S(1)}, u32[]{:S(2)}, u32[]{:S(2)}) collective-permute-start(bf16[256,2048]{1,0:T(8,128)(2,1)} %get-tuple-element.29), channel_id=1, source_target_pairs={{0,12},{4,0},{8,4},{12,8},{16,28},{20,16},{24,20},{28,24},{32,44},... | collective-permute-start | bytes 3145736 | tf_op jit(solution)/shard_map/ppermute | solution.py:121
  174.5 46.3 %collective-permute-start.20 = (bf16[256,2048]{1,0:T(8,128)(2,1)}, bf16[256,2048]{1,0:T(8,128)(2,1)}, u32[]{:S(2)}, u32[]{:S(2)}) collective-permute-start(bf16[256,2048]{1,0:T(8,128)(2,1)} %get-tuple-element.31), channel_id=1, source_target_pairs={{0,8},{4,12},{8,0},{12,4},{16,24},{20,28},{24,16},{28,20},{32,40},... | collective-permute-start | bytes 3145736 | tf_op jit(solution)/shard_map/ppermute | solution.py:121
  174.6 71.4 %collective-permute-start.15 = (bf16[256,2048]{1,0:T(8,128)(2,1)}, bf16[256,2048]{1,0:T(8,128)(2,1)S(1)}, u32[]{:S(2)}, u32[]{:S(2)}) collective-permute-start(bf16[256,2048]{1,0:T(8,128)(2,1)} %get-tuple-element.25), channel_id=1, source_target_pairs={{0,4},{4,8},{8,12},{12,0},{16,20},{20,24},{24,28},{28,16},{32,36},... | collective-permute-start | bytes 3145736 | tf_op jit(solution)/shard_map/ppermute | solution.py:121
  176.7 69.3 %collective-permute-start.14 = (bf16[256,2048]{1,0:T(8,128)(2,1)}, bf16[256,2048]{1,0:T(8,128)(2,1)}, u32[]{:S(2)}, u32[]{:S(2)}) collective-permute-start(bf16[256,2048]{1,0:T(8,128)(2,1)} %get-tuple-element.24), channel_id=1, source_target_pairs={{0,12},{4,0},{8,4},{12,8},{16,28},{20,16},{24,20},{28,24},{32,44},... | collective-permute-start | bytes 3145736 | tf_op jit(solution)/shard_map/ppermute | solution.py:121
  206.2 39.8 %collective-permute-start.16 = (bf16[256,2048]{1,0:T(8,128)(2,1)}, bf16[256,2048]{1,0:T(8,128)(2,1)}, u32[]{:S(2)}, u32[]{:S(2)}) collective-permute-start(bf16[256,2048]{1,0:T(8,128)(2,1)} %get-tuple-element.26), channel_id=1, source_target_pairs={{0,8},{4,12},{8,0},{12,4},{16,24},{20,28},{24,16},{28,20},{32,40},... | collective-permute-start | bytes 3145736 | tf_op jit(solution)/shard_map/ppermute | solution.py:121
  220.9 25.1 %copy-start.5 = (bf16[256,2048]{1,0:T(8,128)(2,1)S(1)}, bf16[256,2048]{1,0:T(8,128)(2,1)}, u32[]{:S(2)}) copy-start(bf16[256,2048]{1,0:T(8,128)(2,1)} %get-tuple-element.27) | copy-start | bytes 3145732
  223.3 26.8 %collective-permute-start.21 = (bf16[256,2048]{1,0:T(8,128)(2,1)S(1)}, bf16[256,2048]{1,0:T(8,128)(2,1)S(1)}, u32[]{:S(2)}, u32[]{:S(2)}) collective-permute-start(bf16[256,2048]{1,0:T(8,128)(2,1)S(1)} %add_convert_fusion), channel_id=1, source_target_pairs={{16,0},{20,4},{24,8},{28,12},{32,16},{36,20},{40,24},{44,28},{48,3... | collective-permute-start | bytes 3145736 | tf_op jit(solution)/shard_map/ppermute | solution.py:26
  246.0 4.1 %copy-start.1 = (f32[256,2048]{1,0:T(8,128)S(1)}, f32[256,2048]{1,0:T(8,128)}, u32[]{:S(2)}) copy-start(f32[256,2048]{1,0:T(8,128)} %get-tuple-element.28) | copy-start | bytes 6291460
  248.2 24.1 %collective-permute-start.17 = (bf16[256,2048]{1,0:T(8,128)(2,1)S(1)}, bf16[256,2048]{1,0:T(8,128)(2,1)S(1)}, u32[]{:S(2)}, u32[]{:S(2)}) collective-permute-start(bf16[256,2048]{1,0:T(8,128)(2,1)S(1)} %add_convert_fusion.1), channel_id=1, source_target_pairs={{16,0},{20,4},{24,8},{28,12},{32,16},{36,20},{40,24},{44,28},{48,3... | collective-permute-start | bytes 3145736 | tf_op jit(solution)/shard_map/ppermute | solution.py:26
  250.1 22.2 %copy-start = (f32[256,2048]{1,0:T(8,128)S(1)}, f32[256,2048]{1,0:T(8,128)}, u32[]{:S(2)}) copy-start(f32[256,2048]{1,0:T(8,128)} %get-tuple-element.23) | copy-start | bytes 6291460

commit v7 on v6

--- a/solution.py
+++ b/solution.py
@@ -12,9 +12,9 @@
 KEY_VALUE_HEADS = 16
 HEAD_SIZE = 128
 WINDOW = 1024
-HEADS_PER_STEP = 4
+HEADS_PER_STEP = 2
 ROW_DEVICES = 4
-PAIR_ORDER = (1, 3, 2, 4)
+PAIR_ORDER = (1, 3, 4, 2)
 
 
 score_scale = 168.0 ** (-0.5)
@@ -187,6 +187,11 @@
         if distance == blocks:
             far_part = (dk_part, dv_part)
             continue
+        if distance == PAIR_ORDER[-1]:
+            got = passed_along((dk_part, dv_part), "seq", -distance)
+            key_grad = key_grad + got[0].astype(jnp.float32)
+            value_grad = value_grad + got[1].astype(jnp.float32)
+            continue
         got = sent_by(
             (dk_part, dv_part),
             "seq",

time: 276 us -> 298 us (1.080)
  the two profiles are of different devices: /device:TPU:28 before, /device:TPU:60 now
where the time goes in v7:
time: 298 us; the launch traced here: 297 us
  waiting for transfers between devices  132 us (44%)
  Pallas kernels  73.5 us (25%)
  starting transfers between devices  58.9 us (20%)
  other arithmetic  22.9 us (8%)
  local copies, waits for them, and re-layouts  7.84 us (3%)
    ppermute x6, waiting for transfers between devices, passed_along(): return lax.ppermute(x, axis, pairs)  74 us
    pallas_call x5, Pallas kernels, pair_grads(): pl.pallas_call(functools.partial(pair_kernel, group, heads, accumulate, p...  73.5 us
    ppermute x16, waiting for transfers between devices, sent_by(): return lax.ppermute(x, axis, pairs)  57.7 us
    ppermute x16, starting transfers between devices, sent_by(): return lax.ppermute(x, axis, pairs)  36.7 us
    ppermute x6, starting transfers between devices, passed_along(): return lax.ppermute(x, axis, pairs)  22.2 us
    unnamed x15, local copies, waits for them, and re-layouts  6.52 us
  transfers between devices with their start and end apart: 22, of which 8 were waited for; matrix products, arithmetic and copies ran while one was open for 9% of the time, Pallas kernels for 25%

profile of v7, /device:TPU:60, one launch (start us, length us, event | category | flops | bytes accessed | tf_op | source)
XLA Modules:
  0.0 296.5 jit_solution(9192496751092669577)
XLA Ops:
  0.6 4.0 %collective-permute-start.2 = (bf16[256,2048]{1,0:T(8,128)(2,1)}, bf16[256,2048]{1,0:T(8,128)(2,1)}, u32[]{:S(2)}, u32[]{:S(2)}) collective-permute-start(bf16[256,2048]{1,0:T(8,128)(2,1)} %refs_0_.1), channel_id=1, source_target_pairs={{0,16},{4,20},{8,24},{12,28},{16,32},{20,36},{24,40},{28,44},{32,4... | collective-permute-start | bytes 3145736 | tf_op jit(solution)/shard_map/ppermute | solution.py:26
  4.6 3.2 %collective-permute-start.7 = (bf16[256,2048]{1,0:T(8,128)(2,1)}, bf16[256,2048]{1,0:T(8,128)(2,1)}, u32[]{:S(2)}, u32[]{:S(2)}) collective-permute-start(bf16[256,2048]{1,0:T(8,128)(2,1)} %refs_1_.1), channel_id=1, source_target_pairs={{0,16},{4,20},{8,24},{12,28},{16,32},{20,36},{24,40},{28,44},{32,4... | collective-permute-start | bytes 3145736 | tf_op jit(solution)/shard_map/ppermute | solution.py:26
  7.8 3.1 %collective-permute-start = (bf16[256,2048]{1,0:T(8,128)(2,1)}, bf16[256,2048]{1,0:T(8,128)(2,1)}, u32[]{:S(2)}, u32[]{:S(2)}) collective-permute-start(bf16[256,2048]{1,0:T(8,128)(2,1)} %refs_0_.1), channel_id=1, source_target_pairs={{0,4},{4,8},{8,12},{16,20},{20,24},{24,28},{32,36},{36,40},{40,44}... | collective-permute-start | bytes 3145736 | tf_op jit(solution)/shard_map/ppermute | solution.py:121
  11.0 1.9 collective-permute-start.5
  12.9 16.0 %collective-permute-done.2.refs_0_ = bf16[256,2048]{1,0:T(8,128)(2,1)} collective-permute-done((bf16[256,2048]{1,0:T(8,128)(2,1)}, bf16[256,2048]{1,0:T(8,128)(2,1)}, u32[]{:S(2)}, u32[]{:S(2)}) %collective-permute-start.2) | collective-permute-done | bytes 1048608 | tf_op jit(solution)/shard_map/ppermute | solution.py:26
  28.9 1.7 collective-permute-start.12
  30.5 19.7 %collective-permute-done.7.refs_1_ = bf16[256,2048]{1,0:T(8,128)(2,1)} collective-permute-done((bf16[256,2048]{1,0:T(8,128)(2,1)}, bf16[256,2048]{1,0:T(8,128)(2,1)}, u32[]{:S(2)}, u32[]{:S(2)}) %collective-permute-start.7) | collective-permute-done | bytes 1048608 | tf_op jit(solution)/shard_map/ppermute | solution.py:26
  50.2 1.6 collective-permute-start.13
  51.8 0.7 collective-permute-start.10
  52.6 1.7 collective-permute-start.11
  54.3 2.6 collective-permute-done.5.refs_2_
  56.9 2.4 collective-permute-start.3
  59.3 6.2 %collective-permute-start.8 = (bf16[256,2048]{1,0:T(8,128)(2,1)}, bf16[256,2048]{1,0:T(8,128)(2,1)S(1)}, u32[]{:S(2)}, u32[]{:S(2)}) collective-permute-start(bf16[256,2048]{1,0:T(8,128)(2,1)} %collective-permute-done.7.refs_1_), channel_id=1, source_target_pairs={{20,16},{24,20},{28,24},{36,32},{40,36},{44,40},{52,48},{56,52},{6... | collective-permute-start | bytes 3145736 | tf_op jit(solution)/shard_map/ppermute | solution.py:121
  65.5 5.0 %multiply_bitcast_fusion = f32[32,8,32,128]{3,1,2,0:T(8,128)} fusion(bf16[256,4096]{1,0:T(8,128)(2,1)} %param.10, bf16[256,4096]{1,0:T(8,128)(2,1)} %do_ref.9), kind=kLoop, calls=%fused_computation | loop fusion | flops 3145728 | bytes 8388608
  71.2 4.9 %copy.15 = f32[32,8,32,128]{3,2,1,0:T(8,128)} copy(f32[32,8,32,128]{3,1,2,0:T(8,128)} %multiply_bitcast_fusion) | data formatting | bytes 8388608
  76.1 3.3 %reduce_sum.9 = f32[256,32]{1,0:T(8,128)S(1)} reduce(f32[256,32,128]{2,1,0:T(8,128)} %bitcast.9, f32[]{:T(128)} %constant.32.clone.1), dimensions={2}, to_apply=%region_0.0 | reduce | flops 1040384 | bytes 4227076 | tf_op jit(solution)/shard_map/reduce_sum | solution.py:156
  79.5 0.6 reshape.17.refs_3_.refs_5_
  80.1 0.6 reshape.15.refs_2_.refs_4_
  80.8 0.6 add_add_fusion.4.sc_ref
  81.4 0.6 add_add_fusion.3.sc_ref
  82.0 0.6 add_add_fusion.2.sc_ref
  82.6 14.3 %shard_map.94 = (f32[256,4096]{1,0:T(8,128)}, f32[256,2048]{1,0:T(8,128)}, f32[256,2048]{1,0:T(8,128)}) custom-call(s32[3]{0:T(128)} %add_add_fusion.4.sc_ref, bf16[256,4096]{1,0:T(8,128)(2,1)} %q_ref.9, bf16[256,4096]{1,0:T(8,128)(2,1)} %do_ref.9, bf16[256,2048]{1,0:T(8,128)(2,1)} %refs_0_.1, bf16[256,2048]{1,0:T(8,128)(2,1)} %refs_1_.1, ...), custom_call_target="tpu_custom_call" | custom-call | flops 2684354560 | bytes 18874368 | tf_op jit(solution)/shard_map/pallas_call | solution.py:104
  96.9 1.9 collective-permute-start.1
  98.8 14.9 %shard_map.95 = (f32[256,4096]{1,0:T(8,128)}, bf16[256,2048]{1,0:T(8,128)(2,1)}, bf16[256,2048]{1,0:T(8,128)(2,1)}) custom-call(s32[3]{0:T(128)} %add_add_fusion.3.sc_ref, bf16[256,4096]{1,0:T(8,128)(2,1)} %q_ref.9, bf16[256,4096]{1,0:T(8,128)(2,1)} %do_ref.9, bf16[256,2048]{1,0:T(8,128)(2,1)} %collective-permute-done.refs_0_, ...), custom_call_target="tpu_custom_call", output_to_operand_aliasing={{0}: (9, {})} | custom-call | flops 2684354560 | bytes 20971520 | tf_op jit(solution)/shard_map/pallas_call | solution.py:104
  113.9 0.9 copy-done.4
  115.4 14.9 %shard_map.96 = (f32[256,4096]{1,0:T(8,128)}, bf16[256,2048]{1,0:T(8,128)(2,1)}, bf16[256,2048]{1,0:T(8,128)(2,1)}) custom-call(s32[3]{0:T(128)} %add_add_fusion.2.sc_ref, bf16[256,4096]{1,0:T(8,128)(2,1)} %q_ref.9, bf16[256,4096]{1,0:T(8,128)(2,1)} %do_ref.9, bf16[256,2048]{1,0:T(8,128)(2,1)} %copy-done.4, ...), custom_call_target="tpu_custom_call", output_to_operand_aliasing={{0}: (9, {})} | custom-call | flops 2684354560 | bytes 20971520 | tf_op jit(solution)/shard_map/pallas_call | solution.py:104
  130.5 3.0 %collective-permute-start.18 = (bf16[256,2048]{1,0:T(8,128)(2,1)}, bf16[256,2048]{1,0:T(8,128)(2,1)S(1)}, u32[]{:S(2)}, u32[]{:S(2)}) collective-permute-start(bf16[256,2048]{1,0:T(8,128)(2,1)} %get-tuple-element.29), channel_id=1, source_target_pairs={{0,12},{4,0},{8,4},{12,8},{16,28},{20,16},{24,20},{28,24},{32,44},... | collective-permute-start | bytes 3145736 | tf_op jit(solution)/shard_map/ppermute | solution.py:121
  133.5 1.9 collective-permute-start.6
  135.4 6.0 %collective-permute-start.4 = (bf16[256,2048]{1,0:T(8,128)(2,1)}, bf16[256,2048]{1,0:T(8,128)(2,1)}, u32[]{:S(2)}, u32[]{:S(2)}) collective-permute-start(bf16[256,2048]{1,0:T(8,128)(2,1)} %copy-done.2), channel_id=1, source_target_pairs={{20,16},{24,20},{36,32},{40,36},{52,48},{56,52},{68,64},{72,68},{8... | collective-permute-start | bytes 3145736 | tf_op jit(solution)/shard_map/ppermute | solution.py:121
  141.4 2.4 collective-permute-start.9
  143.7 0.6 add_add_fusion.1.sc_ref
  144.4 0.6 add_add_fusion.sc_ref
  145.0 12.6 %collective-permute-done.19 = bf16[256,2048]{1,0:T(8,128)(2,1)S(1)} collective-permute-done((bf16[256,2048]{1,0:T(8,128)(2,1)}, bf16[256,2048]{1,0:T(8,128)(2,1)S(1)}, u32[]{:S(2)}, u32[]{:S(2)}) %collective-permute-start.19) | collective-permute-done | bytes 1048608 | tf_op jit(solution)/shard_map/ppermute | solution.py:121
  157.6 2.1 collective-permute-start.14
  159.7 14.4 %shard_map.97 = (f32[256,4096]{1,0:T(8,128)}, bf16[256,2048]{1,0:T(8,128)(2,1)}, bf16[256,2048]{1,0:T(8,128)(2,1)}) custom-call(s32[3]{0:T(128)} %add_add_fusion.1.sc_ref, bf16[256,4096]{1,0:T(8,128)(2,1)} %q_ref.9, bf16[256,4096]{1,0:T(8,128)(2,1)} %do_ref.9, bf16[256,2048]{1,0:T(8,128)(2,1)} %collective-permute-done.2.refs_0_, ...), custom_call_target="tpu_custom_call", output_to_operand_aliasing={{0}: (7, {})} | custom-call | flops 2684354560 | bytes 18874368 | tf_op jit(solution)/shard_map/pallas_call | solution.py:104
  174.1 2.7 add_convert_fusion
  176.9 3.3 %collective-permute-done.6.refs_2_ = bf16[256,2048]{1,0:T(8,128)(2,1)} collective-permute-done((bf16[256,2048]{1,0:T(8,128)(2,1)}, bf16[256,2048]{1,0:T(8,128)(2,1)}, u32[]{:S(2)}, u32[]{:S(2)}) %collective-permute-start.6) | collective-permute-done | bytes 1048608 | tf_op jit(solution)/shard_map/ppermute | solution.py:121
  180.2 3.7 %collective-permute-start.21 = (bf16[256,2048]{1,0:T(8,128)(2,1)}, bf16[256,2048]{1,0:T(8,128)(2,1)}, u32[]{:S(2)}, u32[]{:S(2)}) collective-permute-start(bf16[256,2048]{1,0:T(8,128)(2,1)} %add_convert_fusion), channel_id=1, source_target_pairs={{16,0},{20,4},{24,8},{28,12},{32,16},{36,20},{40,24},{44,28},{48,3... | collective-permute-start | bytes 3145736 | tf_op jit(solution)/shard_map/ppermute | solution.py:26
  183.9 18.4 %collective-permute-done.9.refs_3_ = bf16[256,2048]{1,0:T(8,128)(2,1)} collective-permute-done((bf16[256,2048]{1,0:T(8,128)(2,1)}, bf16[256,2048]{1,0:T(8,128)(2,1)}, u32[]{:S(2)}, u32[]{:S(2)}) %collective-permute-start.9) | collective-permute-done | bytes 1048608 | tf_op jit(solution)/shard_map/ppermute | solution.py:121
  202.3 14.9 %shard_map.98 = (f32[256,4096]{1,0:T(8,128)}, bf16[256,2048]{1,0:T(8,128)(2,1)}, bf16[256,2048]{1,0:T(8,128)(2,1)}) custom-call(s32[3]{0:T(128)} %add_add_fusion.sc_ref, bf16[256,4096]{1,0:T(8,128)(2,1)} %q_ref.9, bf16[256,4096]{1,0:T(8,128)(2,1)} %do_ref.9, bf16[256,2048]{1,0:T(8,128)(2,1)} %collective-permute-done.1.refs_0_, ...), custom_call_target="tpu_custom_call", output_to_operand_aliasing={{0}: (9, {})} | custom-call | flops 2684354560 | bytes 20971520 | tf_op jit(solution)/shard_map/pallas_call | solution.py:104
  217.2 5.8 %collective-permute-start.20 = (bf16[256,2048]{1,0:T(8,128)(2,1)}, bf16[256,2048]{1,0:T(8,128)(2,1)S(1)}, u32[]{:S(2)}, u32[]{:S(2)}) collective-permute-start(bf16[256,2048]{1,0:T(8,128)(2,1)} %get-tuple-element.31), channel_id=1, source_target_pairs={{8,0},{12,4},{16,8},{20,12},{24,16},{28,20},{32,24},{36,28},{40,32... | collective-permute-start | bytes 3145736 | tf_op jit(solution)/shard_map/ppermute | solution.py:26
  223.0 20.8 %collective-permute-done.14 = bf16[256,2048]{1,0:T(8,128)(2,1)} collective-permute-done((bf16[256,2048]{1,0:T(8,128)(2,1)}, bf16[256,2048]{1,0:T(8,128)(2,1)}, u32[]{:S(2)}, u32[]{:S(2)}) %collective-permute-start.14) | collective-permute-done | bytes 1048608 | tf_op jit(solution)/shard_map/ppermute | solution.py:121
  243.9 1.9 add_convert_fusion.1
  245.8 3.6 %collective-permute-start.17 = (bf16[256,2048]{1,0:T(8,128)(2,1)S(1)}, bf16[256,2048]{1,0:T(8,128)(2,1)S(1)}, u32[]{:S(2)}, u32[]{:S(2)}) collective-permute-start(bf16[256,2048]{1,0:T(8,128)(2,1)S(1)} %add_convert_fusion.1), channel_id=1, source_target_pairs={{16,0},{20,4},{24,8},{28,12},{32,16},{36,20},{40,24},{44,28},{48,3... | collective-permute-start | bytes 3145736 | tf_op jit(solution)/shard_map/ppermute | solution.py:26
  249.3 1.9 collective-permute-start.16
  251.3 3.5 %convert_add_fusion = f32[256,2048]{1,0:T(8,128)} fusion(bf16[256,2048]{1,0:T(8,128)(2,1)} %collective-permute-done.21, bf16[256,2048]{1,0:T(8,128)(2,1)S(1)} %collective-permute-done.20, f32[256,2048]{1,0:T(8,128)S(1)} %copy-done.1, bf16[256,2048]{1,0:T(8,128)(2,1)S(1)} %collective-permute-done.19, bf16[256,2048]{1,0:T(8,128)(2,1)S(1)} %collective-permute-done.18, ...), kind=kLoop, calls=%fused_computation.1 | loop fusion | flops 5242880 | bytes 8388610 | tf_op jit(solution)/shard_map/add | solution.py:213
  254.8 38.4 %collective-permute-done.17 = bf16[256,2048]{1,0:T(8,128)(2,1)S(1)} collective-permute-done((bf16[256,2048]{1,0:T(8,128)(2,1)S(1)}, bf16[256,2048]{1,0:T(8,128)(2,1)S(1)}, u32[]{:S(2)}, u32[]{:S(2)}) %collective-permute-start.17) | collective-permute-done | bytes 1048608 | tf_op jit(solution)/shard_map/ppermute | solution.py:26
  293.2 3.3 %convert_add_fusion.1 = f32[256,2048]{1,0:T(8,128)} fusion(bf16[256,2048]{1,0:T(8,128)(2,1)S(1)} %collective-permute-done.17, bf16[256,2048]{1,0:T(8,128)(2,1)S(1)} %collective-permute-done.16, f32[256,2048]{1,0:T(8,128)S(1)} %copy-done, bf16[256,2048]{1,0:T(8,128)(2,1)S(1)} %collective-permute-done.15, bf16[256,2048]{1,0:T(8,128)(2,1)} %collective-permute-done.14, ...), kind=kLoop, calls=%fused_computation.3 | loop fusion | flops 5242880 | bytes 8388610 | tf_op jit(solution)/shard_map/add | solution.py:212
  (30 shorter events, 0.8 us)
Async XLA Ops:
  0.6 28.2 %collective-permute-start.2 = (bf16[256,2048]{1,0:T(8,128)(2,1)}, bf16[256,2048]{1,0:T(8,128)(2,1)}, u32[]{:S(2)}, u32[]{:S(2)}) collective-permute-start(bf16[256,2048]{1,0:T(8,128)(2,1)} %refs_0_.1), channel_id=1, source_target_pairs={{0,16},{4,20},{8,24},{12,28},{16,32},{20,36},{24,40},{28,44},{32,4... | collective-permute-start | bytes 3145736 | tf_op jit(solution)/shard_map/ppermute | solution.py:26
  4.6 45.6 %collective-permute-start.7 = (bf16[256,2048]{1,0:T(8,128)(2,1)}, bf16[256,2048]{1,0:T(8,128)(2,1)}, u32[]{:S(2)}, u32[]{:S(2)}) collective-permute-start(bf16[256,2048]{1,0:T(8,128)(2,1)} %refs_1_.1), channel_id=1, source_target_pairs={{0,16},{4,20},{8,24},{12,28},{16,32},{20,36},{24,40},{28,44},{32,4... | collective-permute-start | bytes 3145736 | tf_op jit(solution)/shard_map/ppermute | solution.py:26
  7.8 44.7 %collective-permute-start = (bf16[256,2048]{1,0:T(8,128)(2,1)}, bf16[256,2048]{1,0:T(8,128)(2,1)}, u32[]{:S(2)}, u32[]{:S(2)}) collective-permute-start(bf16[256,2048]{1,0:T(8,128)(2,1)} %refs_0_.1), channel_id=1, source_target_pairs={{0,4},{4,8},{8,12},{16,20},{20,24},{24,28},{32,36},{36,40},{40,44}... | collective-permute-start | bytes 3145736 | tf_op jit(solution)/shard_map/ppermute | solution.py:121
  11.0 45.9 %collective-permute-start.5 = (bf16[256,2048]{1,0:T(8,128)(2,1)}, bf16[256,2048]{1,0:T(8,128)(2,1)}, u32[]{:S(2)}, u32[]{:S(2)}) collective-permute-start(bf16[256,2048]{1,0:T(8,128)(2,1)} %refs_1_.1), channel_id=1, source_target_pairs={{0,4},{4,8},{8,12},{16,20},{20,24},{24,28},{32,36},{36,40},{40,44}... | collective-permute-start | bytes 3145736 | tf_op jit(solution)/shard_map/ppermute | solution.py:121
  28.9 30.4 %collective-permute-start.12 = (bf16[256,2048]{1,0:T(8,128)(2,1)}, bf16[256,2048]{1,0:T(8,128)(2,1)}, u32[]{:S(2)}, u32[]{:S(2)}) collective-permute-start(bf16[256,2048]{1,0:T(8,128)(2,1)} %collective-permute-done.2.refs_0_), channel_id=1, source_target_pairs={{28,16},{44,32},{60,48},{76,64},{92,80},{108,96},{124,112},{29,17}... | collective-permute-start | bytes 3145736 | tf_op jit(solution)/shard_map/ppermute | solution.py:121
  50.2 46.7 %collective-permute-start.13 = (bf16[256,2048]{1,0:T(8,128)(2,1)}, bf16[256,2048]{1,0:T(8,128)(2,1)}, u32[]{:S(2)}, u32[]{:S(2)}) collective-permute-start(bf16[256,2048]{1,0:T(8,128)(2,1)} %collective-permute-done.7.refs_1_), channel_id=1, source_target_pairs={{28,16},{44,32},{60,48},{76,64},{92,80},{108,96},{124,112},{29,17}... | collective-permute-start | bytes 3145736 | tf_op jit(solution)/shard_map/ppermute | solution.py:121
  51.8 61.9 %collective-permute-start.10 = (bf16[256,2048]{1,0:T(8,128)(2,1)}, bf16[256,2048]{1,0:T(8,128)(2,1)S(1)}, u32[]{:S(2)}, u32[]{:S(2)}) collective-permute-start(bf16[256,2048]{1,0:T(8,128)(2,1)} %refs_0_.1), channel_id=1, source_target_pairs={{0,12},{16,28},{32,44},{48,60},{64,76},{80,92},{96,108},{112,124},... | collective-permute-start | bytes 3145736 | tf_op jit(solution)/shard_map/ppermute | solution.py:121
  52.6 61.2 %collective-permute-start.11 = (bf16[256,2048]{1,0:T(8,128)(2,1)}, bf16[256,2048]{1,0:T(8,128)(2,1)}, u32[]{:S(2)}, u32[]{:S(2)}) collective-permute-start(bf16[256,2048]{1,0:T(8,128)(2,1)} %refs_1_.1), channel_id=1, source_target_pairs={{0,12},{16,28},{32,44},{48,60},{64,76},{80,92},{96,108},{112,124},... | collective-permute-start | bytes 3145736 | tf_op jit(solution)/shard_map/ppermute | solution.py:121
  56.9 57.0 %collective-permute-start.3 = (bf16[256,2048]{1,0:T(8,128)(2,1)}, bf16[256,2048]{1,0:T(8,128)(2,1)S(1)}, u32[]{:S(2)}, u32[]{:S(2)}) collective-permute-start(bf16[256,2048]{1,0:T(8,128)(2,1)} %collective-permute-done.2.refs_0_), channel_id=1, source_target_pairs={{20,16},{24,20},{28,24},{36,32},{40,36},{44,40},{52,48},{56,52},{6... | collective-permute-start | bytes 3145736 | tf_op jit(solution)/shard_map/ppermute | solution.py:121
  59.3 54.5 %collective-permute-start.8 = (bf16[256,2048]{1,0:T(8,128)(2,1)}, bf16[256,2048]{1,0:T(8,128)(2,1)S(1)}, u32[]{:S(2)}, u32[]{:S(2)}) collective-permute-start(bf16[256,2048]{1,0:T(8,128)(2,1)} %collective-permute-done.7.refs_1_), channel_id=1, source_target_pairs={{20,16},{24,20},{28,24},{36,32},{40,36},{44,40},{52,48},{56,52},{6... | collective-permute-start | bytes 3145736 | tf_op jit(solution)/shard_map/ppermute | solution.py:121
  76.1 4.1 %copy-start.5 = (f32[32,256]{1,0:T(8,128)S(1)}, f32[32,256]{1,0:T(8,128)}, u32[]{:S(2)}) copy-start(f32[32,256]{1,0:T(8,128)} %param.12) | copy-start | bytes 98308
  96.9 44.5 %collective-permute-start.1 = (bf16[256,2048]{1,0:T(8,128)(2,1)}, bf16[256,2048]{1,0:T(8,128)(2,1)}, u32[]{:S(2)}, u32[]{:S(2)}) collective-permute-start(bf16[256,2048]{1,0:T(8,128)(2,1)} %collective-permute-done.refs_0_), channel_id=1, source_target_pairs={{4,8},{8,12},{20,24},{24,28},{36,40},{40,44},{52,56},{56,60},{68,7... | collective-permute-start | bytes 3145736 | tf_op jit(solution)/shard_map/ppermute | solution.py:121
  113.8 1.0 copy-start.4
  113.8 1.3 copy-start.2
  113.8 1.6 copy-start.3
  130.4 27.2 %collective-permute-start.19 = (bf16[256,2048]{1,0:T(8,128)(2,1)}, bf16[256,2048]{1,0:T(8,128)(2,1)S(1)}, u32[]{:S(2)}, u32[]{:S(2)}) collective-permute-start(bf16[256,2048]{1,0:T(8,128)(2,1)} %get-tuple-element.30), channel_id=1, source_target_pairs={{0,4},{4,8},{8,12},{12,0},{16,20},{20,24},{24,28},{28,16},{32,36},... | collective-permute-start | bytes 3145736 | tf_op jit(solution)/shard_map/ppermute | solution.py:121
  130.5 27.2 %collective-permute-start.18 = (bf16[256,2048]{1,0:T(8,128)(2,1)}, bf16[256,2048]{1,0:T(8,128)(2,1)S(1)}, u32[]{:S(2)}, u32[]{:S(2)}) collective-permute-start(bf16[256,2048]{1,0:T(8,128)(2,1)} %get-tuple-element.29), channel_id=1, source_target_pairs={{0,12},{4,0},{8,4},{12,8},{16,28},{20,16},{24,20},{28,24},{32,44},... | collective-permute-start | bytes 3145736 | tf_op jit(solution)/shard_map/ppermute | solution.py:121
  133.5 46.7 %collective-permute-start.6 = (bf16[256,2048]{1,0:T(8,128)(2,1)}, bf16[256,2048]{1,0:T(8,128)(2,1)}, u32[]{:S(2)}, u32[]{:S(2)}) collective-permute-start(bf16[256,2048]{1,0:T(8,128)(2,1)} %collective-permute-done.5.refs_2_), channel_id=1, source_target_pairs={{4,8},{8,12},{20,24},{24,28},{36,40},{40,44},{52,56},{56,60},{68,7... | collective-permute-start | bytes 3145736 | tf_op jit(solution)/shard_map/ppermute | solution.py:121
  135.4 48.5 %collective-permute-start.4 = (bf16[256,2048]{1,0:T(8,128)(2,1)}, bf16[256,2048]{1,0:T(8,128)(2,1)}, u32[]{:S(2)}, u32[]{:S(2)}) collective-permute-start(bf16[256,2048]{1,0:T(8,128)(2,1)} %copy-done.2), channel_id=1, source_target_pairs={{20,16},{24,20},{36,32},{40,36},{52,48},{56,52},{68,64},{72,68},{8... | collective-permute-start | bytes 3145736 | tf_op jit(solution)/shard_map/ppermute | solution.py:121
  141.4 60.9 %collective-permute-start.9 = (bf16[256,2048]{1,0:T(8,128)(2,1)}, bf16[256,2048]{1,0:T(8,128)(2,1)}, u32[]{:S(2)}, u32[]{:S(2)}) collective-permute-start(bf16[256,2048]{1,0:T(8,128)(2,1)} %copy-done.3), channel_id=1, source_target_pairs={{20,16},{24,20},{36,32},{40,36},{52,48},{56,52},{68,64},{72,68},{8... | collective-permute-start | bytes 3145736 | tf_op jit(solution)/shard_map/ppermute | solution.py:121
  157.6 65.4 %collective-permute-start.15 = (bf16[256,2048]{1,0:T(8,128)(2,1)}, bf16[256,2048]{1,0:T(8,128)(2,1)S(1)}, u32[]{:S(2)}, u32[]{:S(2)}) collective-permute-start(bf16[256,2048]{1,0:T(8,128)(2,1)} %get-tuple-element.25), channel_id=1, source_target_pairs={{0,4},{4,8},{8,12},{12,0},{16,20},{20,24},{24,28},{28,16},{32,36},... | collective-permute-start | bytes 3145736 | tf_op jit(solution)/shard_map/ppermute | solution.py:121
  157.6 86.2 %collective-permute-start.14 = (bf16[256,2048]{1,0:T(8,128)(2,1)}, bf16[256,2048]{1,0:T(8,128)(2,1)}, u32[]{:S(2)}, u32[]{:S(2)}) collective-permute-start(bf16[256,2048]{1,0:T(8,128)(2,1)} %get-tuple-element.24), channel_id=1, source_target_pairs={{0,12},{4,0},{8,4},{12,8},{16,28},{20,16},{24,20},{28,24},{32,44},... | collective-permute-start | bytes 3145736 | tf_op jit(solution)/shard_map/ppermute | solution.py:121
  180.2 71.1 %collective-permute-start.21 = (bf16[256,2048]{1,0:T(8,128)(2,1)}, bf16[256,2048]{1,0:T(8,128)(2,1)}, u32[]{:S(2)}, u32[]{:S(2)}) collective-permute-start(bf16[256,2048]{1,0:T(8,128)(2,1)} %add_convert_fusion), channel_id=1, source_target_pairs={{16,0},{20,4},{24,8},{28,12},{32,16},{36,20},{40,24},{44,28},{48,3... | collective-permute-start | bytes 3145736 | tf_op jit(solution)/shard_map/ppermute | solution.py:26
  217.2 34.1 %collective-permute-start.20 = (bf16[256,2048]{1,0:T(8,128)(2,1)}, bf16[256,2048]{1,0:T(8,128)(2,1)S(1)}, u32[]{:S(2)}, u32[]{:S(2)}) collective-permute-start(bf16[256,2048]{1,0:T(8,128)(2,1)} %get-tuple-element.31), channel_id=1, source_target_pairs={{8,0},{12,4},{16,8},{20,12},{24,16},{28,20},{32,24},{36,28},{40,32... | collective-permute-start | bytes 3145736 | tf_op jit(solution)/shard_map/ppermute | solution.py:26
  243.9 5.5 %copy-start.6 = (bf16[256,2048]{1,0:T(8,128)(2,1)S(1)}, bf16[256,2048]{1,0:T(8,128)(2,1)}, u32[]{:S(2)}) copy-start(bf16[256,2048]{1,0:T(8,128)(2,1)} %get-tuple-element.26) | copy-start | bytes 3145732
  243.9 7.4 %copy-start.1 = (f32[256,2048]{1,0:T(8,128)S(1)}, f32[256,2048]{1,0:T(8,128)}, u32[]{:S(2)}) copy-start(f32[256,2048]{1,0:T(8,128)} %get-tuple-element.28) | copy-start | bytes 6291460
  245.8 47.4 %collective-permute-start.17 = (bf16[256,2048]{1,0:T(8,128)(2,1)S(1)}, bf16[256,2048]{1,0:T(8,128)(2,1)S(1)}, u32[]{:S(2)}, u32[]{:S(2)}) collective-permute-start(bf16[256,2048]{1,0:T(8,128)(2,1)S(1)} %add_convert_fusion.1), channel_id=1, source_target_pairs={{16,0},{20,4},{24,8},{28,12},{32,16},{36,20},{40,24},{44,28},{48,3... | collective-permute-start | bytes 3145736 | tf_op jit(solution)/shard_map/ppermute | solution.py:26
  249.3 43.9 %collective-permute-start.16 = (bf16[256,2048]{1,0:T(8,128)(2,1)S(1)}, bf16[256,2048]{1,0:T(8,128)(2,1)S(1)}, u32[]{:S(2)}, u32[]{:S(2)}) collective-permute-start(bf16[256,2048]{1,0:T(8,128)(2,1)S(1)} %copy-done.6), channel_id=1, source_target_pairs={{8,0},{12,4},{16,8},{20,12},{24,16},{28,20},{32,24},{36,28},{40,32... | collective-permute-start | bytes 3145736 | tf_op jit(solution)/shard_map/ppermute | solution.py:26
  251.3 41.9 %copy-start = (f32[256,2048]{1,0:T(8,128)S(1)}, f32[256,2048]{1,0:T(8,128)}, u32[]{:S(2)}) copy-start(f32[256,2048]{1,0:T(8,128)} %get-tuple-element.23) | copy-start | bytes 6291460
